TPU v7x, 512 devices: a whole 4x8x8 slice. The times are simulated.
512 devices in a mesh: mode: 16 (over z_hi, x), mer: 32 (over y, z_lo, core).
Axes of the slice: x: 4, y: 8, z: 8 (z_hi: 4, z_lo: 2; z = z_hi * 2 + z_lo), core: 2. Of those that a mesh axis runs over, the one named last changes fastest.
Arguments:
- field: float32 [128, 6, 16384], P('mode', None, 'mer'), may hold values from -6 to 6
- velocity: bfloat16 [3, 256, 16384], P(None, None, ('mer', 'mode')), may hold values from -4 to 4
- stiffness: float32 [64, 64], replicated, may hold values from -0.75 to 0.75
- curl_matrix: float32 [64, 64], replicated, may hold values from -0.75 to 0.75
- mass: float32 [16384], P('mer'), may hold values from 0.5 to 2
- connect: int32 [512, 64], P('mer'), may hold values from 0 to 767
- wall_index: int32 [2048], P('mer'), may hold values from 0 to 511, as said below
- dtn: bfloat16 [128, 2048, 2048], P('mode', 'mer'), as said below
Outputs:
- advanced: float32 [128, 6, 16384], P('mode', None, 'mer')
- wall_flux: float32 [2, 128, 2, 2048], P(None, 'mode', None, 'mer')
Inputs may be any that keep to these rules, and one draw needn't show every extreme that they name: `wall_index`: within each block of 64 consecutive entries the numbers are distinct. `dtn`: each mode's matrix is symmetric.
All inputs are finite; a program needn't handle non-finite values.
Results may differ from a plain program's by a relative error of at most 0.005.
Values may be sent and summed in bfloat16 or wider, within the bound.
No kernel may reach another device: no remote copies, remote signals or barrier semaphores. Data moves between devices by JAX's collectives and lax.ppermute only.
A program may use at most 64 MiB of HBM per device.

v0:
```python
import jax
import jax.numpy as jnp
from jax import lax
from jax.sharding import PartitionSpec as P

GHOST = 256


HI = lax.Precision.HIGHEST


def from_behind(block, axis, distance):
    devices = range(lax.axis_size(axis))
    route = [(i - distance, i) for i in devices if i - distance in devices]
    return lax.ppermute(block, axis, route)


def tables(modes, nphi):
    m = jnp.arange(modes, dtype=jnp.float32)
    k = jnp.arange(nphi, dtype=jnp.float32)
    angle = 2.0 * jnp.pi * m[:, None] * k[None, :] / nphi
    forward = jnp.stack([jnp.cos(angle), -jnp.sin(angle)], 1)
    return (forward, forward / nphi)


def induced(moved, velocity):
    modes = moved.shape[0]
    nphi = velocity.shape[1]
    forward, inverse = tables(modes, nphi)
    phys = jnp.einsum("mpcn,mpk->ckn", moved.reshape(modes, 2, 3, -1), forward, precision=HI)
    vel = velocity.astype(jnp.float32)
    cross = jnp.stack(
        [
            vel[1] * phys[2] - vel[2] * phys[1],
            vel[2] * phys[0] - vel[0] * phys[2],
            vel[0] * phys[1] - vel[1] * phys[0],
        ]
    )
    back = jnp.einsum("ckn,mpk->mpcn", cross, inverse, precision=HI)
    return back.reshape(modes, 6, -1)


def split_pair(values):
    upper = values.astype(jnp.bfloat16)
    lower = (values - upper.astype(jnp.float32)).astype(jnp.bfloat16)
    return (upper, lower)


def element_sweep(extended, stiffness, curl_matrix, connect):
    mode_dev = extended.shape[0]
    ext_len = extended.shape[2]
    elem_dev = connect.shape[0]
    npe = connect.shape[1]
    per_block = min(elem_dev, max(1, 512 // npe))
    blocks = elem_dev // per_block
    rows = extended.reshape(mode_dev * 12, ext_len)
    rows_hi, rows_lo = split_pair(rows)
    indices = connect.reshape(blocks, per_block * npe)
    columns = jnp.arange(ext_len, dtype=jnp.int32)

    def step(summed, idx):
        onehot = (idx[:, None] == columns[None, :]).astype(jnp.bfloat16)
        picked = lax.dot_general(
            rows_hi, onehot, (((1,), (1,)), ((), ())), preferred_element_type=jnp.float32
        )
        picked = picked + lax.dot_general(
            rows_lo, onehot, (((1,), (1,)), ((), ())), preferred_element_type=jnp.float32
        )
        picked = picked.reshape(mode_dev, 12, per_block, npe)
        fvals = picked[:, :6]
        evals = picked[:, 6:].reshape(mode_dev, 2, 3, per_block, npe)
        evals = jnp.roll(evals, 1, axis=2).reshape(mode_dev, 6, per_block, npe)
        local = -1.0 * jnp.einsum("pq,maeq->maep", stiffness, fvals, precision=HI)
        local = local + jnp.einsum("pq,maeq->maep", curl_matrix, evals, precision=HI)
        flat = local.reshape(mode_dev * 6, per_block * npe)
        loc_hi, loc_lo = split_pair(flat)
        summed = summed + jnp.dot(loc_hi, onehot, preferred_element_type=jnp.float32)
        summed = summed + jnp.dot(loc_lo, onehot, preferred_element_type=jnp.float32)
        return (summed, None)

    start = jnp.zeros((mode_dev * 6, ext_len), jnp.float32)
    summed, unused = lax.scan(step, start, indices)
    return summed.reshape(mode_dev, 6, ext_len)


def rate(field, velocity, stiffness, curl_matrix, mass, connect, wall_index, dtn):
    mode_dev = field.shape[0]
    nodes_dev = field.shape[2]
    extra = GHOST
    field_far = from_behind(field[:, :, :extra], "mer", -1)
    moved = lax.all_to_all(field, "mode", split_axis=2, concat_axis=0, tiled=True)
    back = induced(moved, velocity)
    emf = lax.all_to_all(back, "mode", split_axis=0, concat_axis=2, tiled=True)
    emf_far = from_behind(emf[:, :, :extra], "mer", -1)
    far = jnp.concatenate([field_far, emf_far], 1)
    extended = jnp.concatenate([jnp.concatenate([field, emf], 1), far], 2)
    summed = element_sweep(extended, stiffness, curl_matrix, connect)
    incoming = from_behind(summed[:, :, nodes_dev:], "mer", 1)
    assembled = summed[:, :, :nodes_dev].at[:, :, :extra].add(incoming)
    trace = field[:, jnp.array([2, 5])][:, :, wall_index].astype(jnp.bfloat16)
    whole = lax.all_gather(trace, "mer", axis=2, tiled=True)
    flux = jnp.einsum("mwv,mpv->mpw", dtn, whole, preferred_element_type=jnp.float32)
    mode_num = lax.axis_index("mode") * mode_dev + jnp.arange(mode_dev, dtype=jnp.int32)
    coef = (mode_num.astype(jnp.float32) / all_modes(velocity)) ** 2
    total = assembled - 4.0 * coef[:, None, None] * mass[None, None, :] * field
    total = total.at[:, 2, wall_index].add(-0.5 * flux[:, 0])
    total = total.at[:, 5, wall_index].add(-0.5 * flux[:, 1])
    return (total / mass[None, None, :], flux)


def all_modes(velocity):
    return velocity.shape[1] // 2


def body(field, velocity, stiffness, curl_matrix, mass, connect, wall_index, dtn):
    args = (velocity, stiffness, curl_matrix, mass, connect, wall_index, dtn)
    first, flux_one = rate(field, *args)
    section = field + 0.2 * first
    second, flux_two = rate(section, *args)
    return (0.5 * (field + section + 0.2 * second), jnp.stack([flux_one, flux_two]))


def solution(mesh):
    placed = (
        P("mode", None, "mer"),
        P(None, None, ("mer", "mode")),
        P(),
        P(),
        P("mer"),
        P("mer", None),
        P("mer"),
        P("mode", "mer", None),
    )
    return jax.shard_map(
        body,
        mesh=mesh,
        in_specs=placed,
        out_specs=(P("mode", None, "mer"), P(None, "mode", None, "mer")),
        check_vma=False,
    )
```

profile of v0, /device:TPU:1, one launch (start us, length us, event | category | flops | bytes accessed | tf_op | source)
XLA Modules:
  0.0 251.2 jit_solution(7026488388729421583)
XLA Ops:
  0.6 3.0 %copy.153 = f32[8,6,512]{0,1,2:T(8,128)} copy(f32[8,6,512]{2,0,1:T(8,128)} %param.18) | data formatting | bytes 196608 | tf_op args[0]
  3.6 2.9 %reshape.321 = f32[16,1,1536]{2,1,0:T(1,128)} reshape(f32[512,6,8]{2,1,0:T(8,128)} %bitcast.196) | data formatting | bytes 196608
  6.6 13.5 %all-to-all-start = ((f32[16,1,1536]{2,1,0:T(1,128)}), f32[16,1,1536]{2,1,0:T(1,128)}, u32[]{:S(2)}, u32[]{:S(2)}) async-start(f32[16,1,1536]{2,1,0:T(1,128)} %reshape.321), calls=%async_computation | async-start | bytes 196608 | tf_op jit(solution)/shard_map/all_to_all | solution.py:91
  20.7 2.9 %collective-permute-start = (f32[8,6,256]{2,0,1:T(8,128)}, f32[8,6,256]{2,0,1:T(8,128)}, u32[]{:S(2)}, u32[]{:S(2)}) collective-permute-start(f32[8,6,256]{2,0,1:T(8,128)} %slice.160), channel_id=1, source_target_pairs={{1,0},{2,1},{3,2},{4,3},{5,4},{6,5},{7,6},{8,7},{9,8},{10,9},{11,1... | collective-permute-start | bytes 147464 | tf_op jit(solution)/shard_map/ppermute | solution.py:15
  26.2 37.7 %all_gather.6 = bf16[8,2,2048]{0,1,2:T(2,128)(2,1)S(1)} all-gather(bf16[8,2,64]{0,1,2:T(2,128)(2,1)S(1)} %bitcast.215), channel_id=1, replica_groups=mesh['mode'=16,'mer'=32] {'mer'}, dimensions={2}, use_global_device_ids=true | all-gather | bytes 67584 | tf_op jit(solution)/shard_map/all_gather | solution.py:101
  68.1 2.2 reshape.322
  70.3 2.0 copy.154
  74.7 9.4 %all-to-all-start.1 = ((f32[16,1,1536]{2,1,0:T(1,128)}), f32[16,1,1536]{2,1,0:T(1,128)S(1)}, u32[]{:S(2)}, u32[]{:S(2)}) async-start(f32[16,1,1536]{2,1,0:T(1,128)} %reshape.323), calls=%async_computation.1 | async-start | bytes 196608 | tf_op jit(solution)/shard_map/all_to_all | solution.py:93
  84.2 9.0 %all-to-all-done.1 = f32[16,1,1536]{2,1,0:T(1,128)S(1)} async-done(((f32[16,1,1536]{2,1,0:T(1,128)}), f32[16,1,1536]{2,1,0:T(1,128)S(1)}, u32[]{:S(2)}, u32[]{:S(2)}) %all-to-all-start.1) | async-done | bytes 98336 | tf_op jit(solution)/shard_map/all_to_all | solution.py:93
  96.3 3.6 %collective-permute-start.1 = (f32[8,6,256]{2,0,1:T(8,128)S(1)}, f32[8,6,256]{2,0,1:T(8,128)S(1)}, u32[]{:S(2)}, u32[]{:S(2)}) collective-permute-start(f32[8,6,256]{2,0,1:T(8,128)S(1)} %slice.213), channel_id=1, source_target_pairs={{1,0},{2,1},{3,2},{4,3},{5,4},{6,5},{7,6},{8,7},{9,8},{10,9},{11,1... | collective-permute-start | bytes 147464 | tf_op jit(solution)/shard_map/ppermute | solution.py:15
  103.5 10.9 %while.24 = (s32[]{:T(128)}, f32[48,768]{1,0:T(8,128)}, s32[2,512]{1,0:T(2,128)S(1)}, bf16[96,768]{1,0:T(8,128)(2,1)}, bf16[96,768]{1,0:T(8,128)(2,1)}, /*index=...) while((s32[]{:T(128)}, f32[48,768]{1,0:T(8,128)}, s32[2,512]{1,0:T(2,128)S(1)}, ...), condition=%wide.region_1.2_spmd.clone, body=%wide.region_0.1_spmd.clone.sunk | while | flops 266170368 | bytes 4665507 | solution.py:82
  115.3 2.1 collective-permute-start.2
  120.1 7.0 %scatter_fusion = f32[8,6,512]{0,2,1:T(8,128)} fusion(f32[8,6,512]{0,2,1:T(8,128)} %copy.165, s32[64]{0:T(128)S(1)} %select_bitcast_fusion.1, f32[64,8]{1,0:T(8,128)S(1)} %copy.166), kind=kCustom, calls=%fused_computation.4 | custom fusion | flops 512 | bytes 6656 | tf_op jit(solution)/shard_map/scatter-add | solution.py:106
  127.1 7.0 %scatter_fusion.1 = f32[8,6,512]{0,2,1:T(8,128)} fusion(f32[8,6,512]{0,2,1:T(8,128)} %scatter_fusion, s32[64]{0:T(128)S(1)} %get-tuple-element.204, f32[64,8]{1,0:T(8,128)S(1)} %copy.167), kind=kCustom, calls=%fused_computation.5 | custom fusion | flops 512 | bytes 6656 | tf_op jit(solution)/shard_map/scatter-add | solution.py:107
  134.2 1.8 copy.168
  136.0 1.9 copy.169
  138.0 2.9 %reshape.325 = f32[16,1,1536]{2,1,0:T(1,128)} reshape(f32[512,6,8]{2,1,0:T(8,128)} %bitcast.197) | data formatting | bytes 196608
  140.9 4.2 %all-to-all-start.2 = ((f32[16,1,1536]{2,1,0:T(1,128)}), f32[16,1,1536]{2,1,0:T(1,128)}, u32[]{:S(2)}, u32[]{:S(2)}) async-start(f32[16,1,1536]{2,1,0:T(1,128)} %reshape.325), calls=%async_computation.2 | async-start | bytes 196608 | tf_op jit(solution)/shard_map/all_to_all | solution.py:91
  146.3 2.1 collective-permute-start.3
  149.9 35.8 %all_gather.7 = bf16[8,2,2048]{0,1,2:T(2,128)(2,1)S(1)} all-gather(bf16[8,2,64]{0,1,2:T(2,128)(2,1)} %bitcast.214), channel_id=1, replica_groups=mesh['mode'=16,'mer'=32] {'mer'}, dimensions={2}, use_global_device_ids=true | all-gather | bytes 67584 | tf_op jit(solution)/shard_map/all_gather | solution.py:101
  187.5 1.8 reduce.6
  189.2 2.2 reshape.326
  191.4 2.1 copy.170
  195.8 9.2 %all-to-all-start.3 = ((f32[16,1,1536]{2,1,0:T(1,128)}), f32[16,1,1536]{2,1,0:T(1,128)S(1)}, u32[]{:S(2)}, u32[]{:S(2)}) async-start(f32[16,1,1536]{2,1,0:T(1,128)} %reshape.327), calls=%async_computation.3 | async-start | bytes 196608 | tf_op jit(solution)/shard_map/all_to_all | solution.py:93
  205.7 8.4 %all-to-all-done.3 = f32[16,1,1536]{2,1,0:T(1,128)S(1)} async-done(((f32[16,1,1536]{2,1,0:T(1,128)}), f32[16,1,1536]{2,1,0:T(1,128)S(1)}, u32[]{:S(2)}, u32[]{:S(2)}) %all-to-all-start.3) | async-done | bytes 98336 | tf_op jit(solution)/shard_map/all_to_all | solution.py:93
  215.6 3.7 %collective-permute-start.4 = (f32[8,6,256]{2,0,1:T(8,128)S(1)}, f32[8,6,256]{2,0,1:T(8,128)S(1)}, u32[]{:S(2)}, u32[]{:S(2)}) collective-permute-start(f32[8,6,256]{2,0,1:T(8,128)S(1)} %slice.223), channel_id=1, source_target_pairs={{1,0},{2,1},{3,2},{4,3},{5,4},{6,5},{7,6},{8,7},{9,8},{10,9},{11,1... | collective-permute-start | bytes 147464 | tf_op jit(solution)/shard_map/ppermute | solution.py:15
  219.3 1.8 collective-permute-done.4
  222.0 7.7 %while.25 = (s32[]{:T(128)}, f32[48,768]{1,0:T(8,128)S(1)}, s32[2,512]{1,0:T(2,128)S(1)}, bf16[96,768]{1,0:T(8,128)(2,1)}, bf16[96,768]{1,0:T(8,128)(2,1)S(1)}, ...) while((s32[]{:T(128)}, f32[48,768]{1,0:T(8,128)S(1)}, ...), condition=%wide.region_5.6_spmd.clone, body=%wide.region_4.5_spmd.clone.sunk | while | flops 266170368 | bytes 3485803 | solution.py:82
  229.8 1.9 collective-permute-start.5
  234.7 7.0 %scatter_fusion.2 = f32[8,6,512]{0,2,1:T(8,128)} fusion(f32[8,6,512]{0,2,1:T(8,128)} %copy.181, s32[64]{0:T(128)S(1)} %select_bitcast_fusion.1, f32[64,8]{1,0:T(8,128)S(1)} %copy.182), kind=kCustom, calls=%fused_computation.6 | custom fusion | flops 512 | bytes 6656 | tf_op jit(solution)/shard_map/scatter-add | solution.py:106
  241.7 7.0 %scatter_fusion.3 = f32[8,6,512]{0,2,1:T(8,128)} fusion(f32[8,6,512]{0,2,1:T(8,128)} %scatter_fusion.2, s32[64]{0:T(128)S(1)} %get-tuple-element.204, f32[64,8]{1,0:T(8,128)S(1)} %copy.183), kind=kCustom, calls=%fused_computation.7 | custom fusion | flops 512 | bytes 6656 | tf_op jit(solution)/shard_map/scatter-add | solution.py:107
  248.7 1.8 copy.184
  (192 shorter events, 51.5 us)
Async XLA Ops:
  0.6 63.9 %copy-start = (bf16[8,64,2048]{2,1,0:T(8,128)(2,1)S(1)}, bf16[8,64,2048]{2,1,0:T(8,128)(2,1)}, u32[]{:S(2)}) copy-start(bf16[8,64,2048]{2,1,0:T(8,128)(2,1)} %param.25) | copy-start | bytes 6291460
  3.6 16.4 %copy-start.3 = (f32[8,6,512]{2,0,1:T(8,128)S(1)}, f32[8,6,512]{2,0,1:T(8,128)}, u32[]{:S(2)}) copy-start(f32[8,6,512]{2,0,1:T(8,128)} %param.18) | copy-start | bytes 294916
  3.6 19.9 %copy-start.14 = (bf16[3,256,32]{1,2,0:T(8,128)(2,1)S(1)}, bf16[3,256,32]{1,2,0:T(8,128)(2,1)}, u32[]{:S(2)}) copy-start(bf16[3,256,32]{1,2,0:T(8,128)(2,1)} %param.19) | copy-start | bytes 147460
  3.6 20.6 %copy-start.24 = (s32[64]{0:T(128)S(1)}, s32[64]{0:T(128)}, u32[]{:S(2)}) copy-start(s32[64]{0:T(128)} %param.24) | copy-start | bytes 772
  3.6 21.1 %copy-start.23 = (s32[2]{0:T(128)S(1)}, s32[2]{0:T(128)}, u32[]{:S(2)}) copy-start(s32[2]{0:T(128)} %constant.185) | copy-start | bytes 28
  6.6 59.2 %all-to-all-start = ((f32[16,1,1536]{2,1,0:T(1,128)}), f32[16,1,1536]{2,1,0:T(1,128)}, u32[]{:S(2)}, u32[]{:S(2)}) async-start(f32[16,1,1536]{2,1,0:T(1,128)} %reshape.321), calls=%async_computation | async-start | bytes 196608 | tf_op jit(solution)/shard_map/all_to_all | solution.py:91
  20.7 79.3 %collective-permute-start = (f32[8,6,256]{2,0,1:T(8,128)}, f32[8,6,256]{2,0,1:T(8,128)}, u32[]{:S(2)}, u32[]{:S(2)}) collective-permute-start(f32[8,6,256]{2,0,1:T(8,128)} %slice.160), channel_id=1, source_target_pairs={{1,0},{2,1},{3,2},{4,3},{5,4},{6,5},{7,6},{8,7},{9,8},{10,9},{11,1... | collective-permute-start | bytes 147464 | tf_op jit(solution)/shard_map/ppermute | solution.py:15
  23.6 49.5 %copy-start.8 = (f32[3,256,32]{1,2,0:T(8,128)}, f32[3,256,32]{1,2,0:T(8,128)S(1)}, u32[]{:S(2)}) copy-start(f32[3,256,32]{1,2,0:T(8,128)S(1)} %convert_element_type.56) | copy-start | bytes 294916
  24.8 1.4 copy-start.19
  65.2 34.7 %copy-start.15 = (f32[8,2,64]{2,1,0:T(2,128)}, f32[8,2,64]{2,1,0:T(2,128)S(1)}, u32[]{:S(2)}) copy-start(f32[8,2,64]{2,1,0:T(2,128)S(1)} %fusion.69) | copy-start | bytes 12292
  72.4 11.7 %copy-start.17 = (f32[512]{0:T(512)S(1)}, f32[512]{0:T(512)}, u32[]{:S(2)}) copy-start(f32[512]{0:T(512)} %param.22) | copy-start | bytes 6148
  72.4 11.7 %copy-start.22 = (f32[8]{0:T(128)S(1)}, f32[8]{0:T(128)}, u32[]{:S(2)}) copy-start(f32[8]{0:T(128)} %multiply_multiply_fusion.1) | copy-start | bytes 100
  73.8 26.1 %copy-start.18 = (s32[16,64]{1,0:T(8,128)S(1)}, s32[16,64]{1,0:T(8,128)}, u32[]{:S(2)}) copy-start(s32[16,64]{1,0:T(8,128)} %param.23) | copy-start | bytes 12292
  73.8 27.9 %copy-start.4 = (f32[8,6,512]{2,0,1:T(8,128)S(1)}, f32[8,6,512]{2,0,1:T(8,128)}, u32[]{:S(2)}) copy-start(f32[8,6,512]{2,0,1:T(8,128)} %param.18) | copy-start | bytes 294916
  74.7 18.4 %all-to-all-start.1 = ((f32[16,1,1536]{2,1,0:T(1,128)}), f32[16,1,1536]{2,1,0:T(1,128)S(1)}, u32[]{:S(2)}, u32[]{:S(2)}) async-start(f32[16,1,1536]{2,1,0:T(1,128)} %reshape.323), calls=%async_computation.1 | async-start | bytes 196608 | tf_op jit(solution)/shard_map/all_to_all | solution.py:93
  95.1 8.3 %copy-start.1 = (f32[64,64]{1,0:T(8,128)S(1)}, f32[64,64]{1,0:T(8,128)}, u32[]{:S(2)}) copy-start(f32[64,64]{1,0:T(8,128)} %param.20) | copy-start | bytes 49156
  95.1 8.3 %copy-start.2 = (f32[64,64]{1,0:T(8,128)S(1)}, f32[64,64]{1,0:T(8,128)}, u32[]{:S(2)}) copy-start(f32[64,64]{1,0:T(8,128)} %param.21) | copy-start | bytes 49156
  96.3 5.4 %collective-permute-start.1 = (f32[8,6,256]{2,0,1:T(8,128)S(1)}, f32[8,6,256]{2,0,1:T(8,128)S(1)}, u32[]{:S(2)}, u32[]{:S(2)}) collective-permute-start(f32[8,6,256]{2,0,1:T(8,128)S(1)} %slice.213), channel_id=1, source_target_pairs={{1,0},{2,1},{3,2},{4,3},{5,4},{6,5},{7,6},{8,7},{9,8},{10,9},{11,1... | collective-permute-start | bytes 147464 | tf_op jit(solution)/shard_map/ppermute | solution.py:15
  103.5 14.0 %copy-start.21 = (s32[64]{0:T(128)S(1)}, s32[64]{0:T(128)}, u32[]{:S(2)}) copy-start(s32[64]{0:T(128)} %copy-done.20) | copy-start | bytes 772
  115.3 3.1 %collective-permute-start.2 = (f32[8,6,256]{2,0,1:T(8,128)S(1)}, f32[8,6,256]{2,0,1:T(8,128)S(1)}, u32[]{:S(2)}, u32[]{:S(2)}) collective-permute-start(f32[8,6,256]{2,0,1:T(8,128)S(1)} %copy.162), channel_id=1, source_target_pairs={{0,1},{1,2},{2,3},{3,4},{4,5},{5,6},{6,7},{7,8},{8,9},{9,10},{10,1... | collective-permute-start | bytes 147464 | tf_op jit(solution)/shard_map/ppermute | solution.py:15
  136.0 9.7 %copy-start.6 = (f32[8,6,512]{2,0,1:T(8,128)}, f32[8,6,512]{2,0,1:T(8,128)S(1)}, u32[]{:S(2)}) copy-start(f32[8,6,512]{2,0,1:T(8,128)S(1)} %multiply_add_fusion) | copy-start | bytes 294916
  140.9 46.6 %all-to-all-start.2 = ((f32[16,1,1536]{2,1,0:T(1,128)}), f32[16,1,1536]{2,1,0:T(1,128)}, u32[]{:S(2)}, u32[]{:S(2)}) async-start(f32[16,1,1536]{2,1,0:T(1,128)} %reshape.325), calls=%async_computation.2 | async-start | bytes 196608 | tf_op jit(solution)/shard_map/all_to_all | solution.py:91
  146.3 73.0 %collective-permute-start.3 = (f32[8,6,256]{2,0,1:T(8,128)}, f32[8,6,256]{2,0,1:T(8,128)S(1)}, u32[]{:S(2)}, u32[]{:S(2)}) collective-permute-start(f32[8,6,256]{2,0,1:T(8,128)} %slice.222), channel_id=1, source_target_pairs={{1,0},{2,1},{3,2},{4,3},{5,4},{6,5},{7,6},{8,7},{9,8},{10,9},{11,1... | collective-permute-start | bytes 147464 | tf_op jit(solution)/shard_map/ppermute | solution.py:15
  191.4 2.9 %copy-start.9 = (f32[3,256,32]{1,2,0:T(8,128)S(1)}, f32[3,256,32]{1,2,0:T(8,128)}, u32[]{:S(2)}) copy-start(f32[3,256,32]{1,2,0:T(8,128)} %copy-done.8) | copy-start | bytes 294916
  193.5 11.6 %copy-start.13 = (bf16[8,2,2048]{2,1,0:T(2,128)(2,1)S(1)}, bf16[8,2,2048]{2,1,0:T(2,128)(2,1)}, u32[]{:S(2)}) copy-start(bf16[8,2,2048]{2,1,0:T(2,128)(2,1)} %copy.180) | copy-start | bytes 196612
  195.8 18.3 %all-to-all-start.3 = ((f32[16,1,1536]{2,1,0:T(1,128)}), f32[16,1,1536]{2,1,0:T(1,128)S(1)}, u32[]{:S(2)}, u32[]{:S(2)}) async-start(f32[16,1,1536]{2,1,0:T(1,128)} %reshape.327), calls=%async_computation.3 | async-start | bytes 196608 | tf_op jit(solution)/shard_map/all_to_all | solution.py:93
  205.7 15.4 %copy-start.7 = (f32[8,6,512]{2,0,1:T(8,128)S(1)}, f32[8,6,512]{2,0,1:T(8,128)}, u32[]{:S(2)}) copy-start(f32[8,6,512]{2,0,1:T(8,128)} %copy-done.6) | copy-start | bytes 294916
  215.6 6.4 %copy-start.10 = (f32[48,768]{1,0:T(8,128)S(1)}, f32[48,768]{1,0:T(8,128)}, u32[]{:S(2)}) copy-start(f32[48,768]{1,0:T(8,128)} %custom-call.9) | copy-start | bytes 442372
  215.6 5.5 %collective-permute-start.4 = (f32[8,6,256]{2,0,1:T(8,128)S(1)}, f32[8,6,256]{2,0,1:T(8,128)S(1)}, u32[]{:S(2)}, u32[]{:S(2)}) collective-permute-start(f32[8,6,256]{2,0,1:T(8,128)S(1)} %slice.223), channel_id=1, source_target_pairs={{1,0},{2,1},{3,2},{4,3},{5,4},{6,5},{7,6},{8,7},{9,8},{10,9},{11,1... | collective-permute-start | bytes 147464 | tf_op jit(solution)/shard_map/ppermute | solution.py:15
  222.0 9.7 %copy-start.16 = (f32[8,2,64]{2,1,0:T(2,128)S(1)}, f32[8,2,64]{2,1,0:T(2,128)}, u32[]{:S(2)}) copy-start(f32[8,2,64]{2,1,0:T(2,128)} %copy-done.15) | copy-start | bytes 12292
  229.8 3.1 %collective-permute-start.5 = (f32[8,6,256]{2,0,1:T(8,128)S(1)}, f32[8,6,256]{2,0,1:T(8,128)S(1)}, u32[]{:S(2)}, u32[]{:S(2)}) collective-permute-start(f32[8,6,256]{2,0,1:T(8,128)S(1)} %copy.178), channel_id=1, source_target_pairs={{0,1},{1,2},{2,3},{3,4},{4,5},{5,6},{6,7},{7,8},{8,9},{9,10},{10,1... | collective-permute-start | bytes 147464 | tf_op jit(solution)/shard_map/ppermute | solution.py:15
  233.0 17.5 %copy-start.5 = (f32[8,6,512]{2,0,1:T(8,128)S(1)}, f32[8,6,512]{2,0,1:T(8,128)}, u32[]{:S(2)}) copy-start(f32[8,6,512]{2,0,1:T(8,128)} %param.18) | copy-start | bytes 294916
  (5 other events, 4.5 us)
where the time goes:
time: 255 us; the launch traced here: 251 us
  blocking collectives  73.5 us (29%)
  starting transfers between devices  52.5 us (21%)
  local copies, waits for them, and re-layouts  43.8 us (17%)
  other arithmetic  38.3 us (15%)
  waiting for transfers between devices  22 us (9%)
  matrix products  19.4 us (8%)
    all_gather x2, blocking collectives, rate(): whole = lax.all_gather(trace, 'mer', axis=2, tiled=True)  73.5 us
    all_to_all x2, starting transfers between devices, rate(): emf = lax.all_to_all(back, 'mode', split_axis=0, concat_axis=2, tiled=True)  18.6 us
    all_to_all x2, starting transfers between devices, rate(): lax.all_to_all(field, 'mode', split_axis=2, concat_axis=0, tiled=True)  17.6 us
    all_to_all x2, waiting for transfers between devices, rate(): emf = lax.all_to_all(back, 'mode', split_axis=0, concat_axis=2, tiled=True)  17.4 us
    ppermute x6, starting transfers between devices, from_behind(): return lax.ppermute(block, axis, route)  16.3 us
    unnamed x57, local copies, waits for them, and re-layouts  16 us
    scatter-add x2, other arithmetic, rate(): total = total.at[:, 5, wall_index].add(-0.5 * flux[:, 1])  14 us
    scatter-add x2, other arithmetic, rate(): total = total.at[:, 2, wall_index].add(-0.5 * flux[:, 0])  14 us
  transfers between devices with their start and end apart: 10, of which 6 were waited for; matrix products, arithmetic and copies ran while one was open for 12% of the time, Pallas kernels for 0%

commit v1 on v0

v1 whole, which is shorter than its diff:
```python
import numpy as np
import jax
import jax.numpy as jnp
from jax import lax
from jax.experimental import pallas as pl
from jax.experimental.pallas import tpu as pltpu
from jax.sharding import PartitionSpec as P


BF = jnp.bfloat16
F32 = jnp.float32
PARAMS = pltpu.CompilerParams(vmem_limit_bytes=56 * 2**20)


def nt(a, b):
    return lax.dot_general(a, b, (((1,), (1,)), ((), ())), preferred_element_type=F32)


def nn(a, b):
    return jnp.dot(a, b, preferred_element_type=F32)


def tables(modes, nphi, mode_dev):
    mode = np.arange(modes).reshape(-1, 1, mode_dev)
    k = np.arange(nphi).reshape(-1, 1, 1, 1)
    angle = 2.0 * np.pi * ((mode[None] * k) % nphi) / nphi
    fwd = np.concatenate([np.cos(angle), -np.sin(angle)], 2).reshape(nphi, 2 * modes)
    return fwd.astype(BF), (fwd.T / nphi).astype(BF)


def lane_group(shape):
    return lax.broadcasted_iota(jnp.int32, shape, len(shape) - 1) // 32


def pick(group, parts):
    out = parts[0]
    for g, part in enumerate(parts[1:], 1):
        out = jnp.where(group == g, part, out)
    return out


def shift(x, groups):
    return x if groups % 4 == 0 else pltpu.roll(x, 32 * (groups % 4), 1)


def pack(rows, out_ref):
    group = lane_group((8, 128))
    for v in range(4):
        tiles = {cp: r[:, 128 * v : 128 * v + 128] for cp, r in rows.items()}
        for q in range(4):
            halves = [
                pick(group, [shift(tiles[c % 3, p], c - q) for c in range(4)]) for p in range(2)
            ]
            out_ref[4 * v + q] = jnp.concatenate(halves, 0).astype(BF)


def unpack(ref, slots):
    group = lane_group((16, 128))
    cols = []
    for v in range(slots // 4):
        tiles = [ref[4 * v + q].astype(F32) for q in range(4)]
        cols.append(
            jnp.concatenate(
                [pick(group, [shift(tiles[q], q - c) for q in range(4)]) for c in range(3)], 0
            ).astype(BF)
        )
    return jnp.concatenate(cols, 1)


def wall_onehot(wall):
    nodes = lax.broadcasted_iota(jnp.int32, (512, 128), 0)
    return (nodes == wall).astype(F32).astype(BF)


def pack_kernel(field_ref, out_ref):
    pack({(c, p): field_ref[3 * p + c] for c in range(3) for p in range(2)}, out_ref)


def trace_kernel(field_ref, wall_ref, out_ref):
    last = jnp.concatenate([field_ref[2], field_ref[5]], 0).astype(BF)
    tr = nn(last, wall_onehot(wall_ref[...])).astype(BF)
    for j in range(out_ref.shape[0]):
        out_ref[j] = tr


def prep_kernel(vel_ref, stiff_ref, curl_ref, conn_ref, far_ref, *refs):
    va_ref, vb_ref, so_ref, sp_ref, co_ref, cp_ref, tall_ref, wide_ref, ws_ref, wc_ref = refs
    vel = [vel_ref[c].astype(F32) for c in range(3)]
    zero = jnp.zeros_like(vel[0])
    va_ref[...] = jnp.concatenate([vel[0], vel[1], vel[2], zero], 0).T
    vb_ref[...] = jnp.concatenate([vel[1], vel[2], vel[0], zero], 0).T
    row = lax.broadcasted_iota(jnp.int32, (256, 64), 0)
    col = lax.broadcasted_iota(jnp.int32, (256, 64), 1)
    spread = (row % 64 == col).astype(F32).astype(BF)
    near = lax.broadcasted_iota(jnp.int32, (256, 256), 0) // 64
    same = near == lax.broadcasted_iota(jnp.int32, (256, 256), 1) // 64

    def blocks(ref, sign):
        once = nt(spread, ref[...].astype(BF)).astype(BF)
        return jnp.where(same, sign * nt(once, spread), 0.0).astype(BF)

    stiff = blocks(stiff_ref, -1.0)
    curl = blocks(curl_ref, 1.0)

    def operator(conn, first, width, s_out, c_out):
        conn = conn.astype(F32)
        across = conn.T
        nodes = lax.broadcasted_iota(jnp.int32, (768, 128), 0).astype(F32)
        lanes = lax.broadcasted_iota(jnp.int32, (128, width), 1).astype(F32) + first
        for t in range(8):
            tall_ref[:, 128 * t : 128 * t + 128] = (nodes == conn[t : t + 1]).astype(F32).astype(BF)
            wide_ref[128 * t : 128 * t + 128, :width] = (
                (lanes == across[:, t : t + 1]).astype(F32).astype(BF)
            )
        for u in range(4):
            some = wide_ref[256 * u : 256 * u + 256, :width]
            ws_ref[256 * u : 256 * u + 256, :width] = nn(stiff, some).astype(BF)
            wc_ref[256 * u : 256 * u + 256, :width] = nn(curl, some).astype(BF)
        tall = tall_ref[...]
        return nn(tall, ws_ref[:, :width]), nn(tall, wc_ref[:, :width])

    s_far, c_far = operator(far_ref[...], 512.0, 256, None, None)
    sp_ref[...] = s_far[:512].astype(BF)
    cp_ref[...] = c_far[:512].astype(BF)
    s_own, c_own = operator(conn_ref[...], 0.0, 512, None, None)
    so_ref[...] = s_own.astype(BF)
    co_ref[...] = c_own.astype(BF)
    so_ref[:256, :256] = (s_own[:256, :256] + s_far[512:]).astype(BF)
    co_ref[:256, :256] = (c_own[:256, :256] + c_far[512:]).astype(BF)


def induce_kernel(moved_ref, va_ref, vb_ref, fwd_ref, inv_ref, out_ref):
    rows = moved_ref[...].reshape(256, 128)
    turned = pltpu.roll(rows.astype(F32), 96, 1).astype(BF)
    here = nn(fwd_ref[...], rows)
    after = nn(fwd_ref[...], turned)
    cross = va_ref[...] * after - vb_ref[...] * here
    back = nn(inv_ref[...], cross.astype(BF))
    out_ref[...] = back.astype(BF).reshape(16, 16, 128)


def section_rows(refs, mode_ref):
    (field_ref, fp_ref, fn_ref, emf_ref, ep_ref, en_ref, so_ref, sp_ref, co_ref, cp_ref) = refs[:10]
    tr_ref, dtn_ref, wall_ref, mass_ref = refs[10:14]
    order = [3 * p + c for c in range(3) for p in range(2)]
    field = jnp.concatenate([field_ref[s] for s in order], 0)
    f_own = jnp.concatenate([field.astype(BF), unpack(fn_ref, 8)], 1)
    e_own = jnp.concatenate([unpack(emf_ref, 16), unpack(en_ref, 8)], 1)
    total = nn(f_own, so_ref[...]) + nn(e_own, co_ref[...])
    low = nn(unpack(fp_ref, 16), sp_ref[...]) + nn(unpack(ep_ref, 16), cp_ref[...])
    total = jnp.concatenate([total[:, :256] + low, total[:, 256:]], 1)
    whole = jnp.concatenate([tr_ref[2 * a] + tr_ref[2 * a + 1] for a in range(16)], 1)
    every = nt(whole, dtn_ref[...].reshape(512, 2048))
    mine = lax.broadcasted_iota(jnp.int32, (16, 512), 0) % 8
    every = jnp.where(mine == lax.broadcasted_iota(jnp.int32, (16, 512), 1) // 64, every, 0.0)
    flux = every[:, :128] + every[:, 128:256] + every[:, 256:384] + every[:, 384:]
    flux = flux + pltpu.roll(flux, 64, 1)
    onehot = wall_onehot(wall_ref[...])
    upper = flux.astype(BF)
    added = nt(upper, onehot) + nt((flux - upper.astype(F32)).astype(BF), onehot)
    total = jnp.concatenate([total[:32], total[32:] - 0.5 * added], 0)
    number = lax.broadcasted_iota(jnp.int32, (48, 512), 0) % 8 + 8 * mode_ref[0]
    coef = (number.astype(F32) / 128.0) ** 2
    rate = total / mass_ref[...] - 4.0 * coef * field
    return rate, field, flux, onehot


def first_kernel(mode_ref, *refs):
    sect_ref, pack_ref, trace_ref, flux_ref = refs[14:]
    rate, field, flux, onehot = section_rows(refs, mode_ref)
    sect = field + 0.2 * rate
    flux_ref[...] = flux
    rows = {(c, p): sect[16 * c + 8 * p : 16 * c + 8 * p + 8] for c in range(3) for p in range(2)}
    for (c, p), r in rows.items():
        sect_ref[3 * p + c] = r
    pack(rows, pack_ref)
    tr = nn(sect[32:].astype(BF), onehot).astype(BF)
    for j in range(trace_ref.shape[0]):
        trace_ref[j] = tr


def second_kernel(mode_ref, *refs):
    start_ref, first_flux_ref, out_ref, flux_ref = refs[14:]
    rate, sect, flux, onehot = section_rows(refs, mode_ref)
    for c in range(3):
        for p in range(2):
            at = slice(16 * c + 8 * p, 16 * c + 8 * p + 8)
            out_ref[3 * p + c] = 0.5 * (start_ref[3 * p + c] + sect[at] + 0.2 * rate[at])
    for p in range(2):
        flux_ref[0, :, p, :] = first_flux_ref[8 * p : 8 * p + 8, :64]
        flux_ref[1, :, p, :] = flux[8 * p : 8 * p + 8, :64]


def shapes(*items):
    return [jax.ShapeDtypeStruct(s, d) for s, d in items]


def call(kernel, out, scratch=(), scalars=0, n_in=0, cost=None):
    vmem = pl.BlockSpec(memory_space=pltpu.VMEM)
    smem = pl.BlockSpec(memory_space=pltpu.SMEM)
    return pl.pallas_call(
        kernel,
        out_shape=out,
        in_specs=[smem] * scalars + [vmem] * (n_in - scalars),
        out_specs=jax.tree.map(lambda _: vmem, out),
        scratch_shapes=list(scratch),
        compiler_params=PARAMS,
        cost_estimate=cost,
    )


def body(field, velocity, stiffness, curl_matrix, mass, connect, wall_index, dtn):
    fwd, inv = tables(128, 256, 8)
    spots = lax.axis_size("mer")
    mine = lax.axis_index("mer")
    mode = lax.axis_index("mode").astype(jnp.int32).reshape(1)
    up = [(i, i + 1) for i in range(spots - 1)]
    down = [(i + 1, i) for i in range(spots - 1)]
    start = jnp.transpose(field, (1, 0, 2))
    conn = connect.reshape(8, 128)
    conn_far = lax.ppermute(conn, "mer", up)
    twice = jnp.concatenate([wall_index, wall_index])
    wall = jnp.where(jnp.arange(128) // 64 == mine % 2, twice, -1).reshape(1, 128)
    row = mass.reshape(1, 512)

    packed = call(pack_kernel, shapes(((16, 16, 128), BF))[0], n_in=1)(start)
    trace = call(trace_kernel, shapes(((spots, 16, 128), BF))[0], n_in=2)(start, wall)
    va, vb, s_own, s_far, c_own, c_far = call(
        prep_kernel,
        shapes(
            ((256, 128), F32), ((256, 128), F32),
            ((768, 512), BF), ((512, 256), BF), ((768, 512), BF), ((512, 256), BF),
        ),
        scratch=[pltpu.VMEM((768, 1024), BF)] + [pltpu.VMEM((1024, 512), BF)] * 3,
        n_in=5,
    )(jnp.transpose(velocity, (0, 2, 1)), stiffness, curl_matrix, conn, conn_far)

    def section(now, packed, trace, last):
        moved = lax.all_to_all(packed, "mode", 0, 0, tiled=True)
        f_prev = lax.ppermute(packed, "mer", up)
        f_next = lax.ppermute(packed, "mer", down)
        back = call(induce_kernel, shapes(((16, 16, 128), BF))[0], n_in=5)(moved, va, vb, fwd, inv)
        emf = lax.all_to_all(back, "mode", 0, 0, tiled=True)
        e_prev = lax.ppermute(emf, "mer", up)
        e_next = lax.ppermute(emf, "mer", down)
        whole = lax.all_to_all(trace, "mer", 0, 0, tiled=True)
        args = (mode, now, f_prev, f_next, emf, e_prev, e_next, s_own, s_far, c_own, c_far)
        args += (whole, dtn, wall, row)
        if last is None:
            out = shapes(((6, 8, 512), F32), ((16, 16, 128), BF), ((spots, 16, 128), BF), ((16, 128), F32))
            return call(first_kernel, out, scalars=1, n_in=len(args))(*args)
        out = shapes(((6, 8, 512), F32), ((2, 8, 2, 64), F32))
        return call(second_kernel, out, scalars=1, n_in=len(args) + 2)(*args, *last)

    sect, packed, trace, flux = section(start, packed, trace, None)
    done, fluxes = section(sect, packed, trace, (start, flux))
    return (jnp.transpose(done, (1, 0, 2)), fluxes)


def solution(mesh):
    placed = (
        P("mode", None, "mer"),
        P(None, None, ("mer", "mode")),
        P(),
        P(),
        P("mer"),
        P("mer", None),
        P("mer"),
        P("mode", "mer", None),
    )
    return jax.shard_map(
        body,
        mesh=mesh,
        in_specs=placed,
        out_specs=(P("mode", None, "mer"), P(None, "mode", None, "mer")),
        check_vma=False,
    )
```

time: 255 us -> 145 us (0.57)
  the two profiles are of different devices: /device:TPU:1 before, /device:TPU:32 now
where the time goes in v1:
time: 145 us; the launch traced here: 144 us
  starting transfers between devices  64.6 us (45%)
  blocking collectives  27.7 us (19%)
  waiting for transfers between devices  23.5 us (16%)
  Pallas kernels  23 us (16%)
  local copies, waits for them, and re-layouts  3.21 us (2%)
    all_to_all x2, starting transfers between devices, section(): whole = lax.all_to_all(trace, 'mer', 0, 0, tiled=True)  14.7 us
    all_to_all x1, blocking collectives, section(): moved = lax.all_to_all(packed, 'mode', 0, 0, tiled=True)  14.2 us
    all_to_all x1, blocking collectives, section(): emf = lax.all_to_all(back, 'mode', 0, 0, tiled=True)  13.5 us
    all_to_all x1, starting transfers between devices, section(): moved = lax.all_to_all(packed, 'mode', 0, 0, tiled=True)  12.9 us
    ppermute x2, starting transfers between devices, section(): e_next = lax.ppermute(emf, 'mer', down)  11.5 us
    ppermute x2, waiting for transfers between devices, section(): e_prev = lax.ppermute(emf, 'mer', up)  11.4 us
    all_to_all x1, starting transfers between devices, section(): emf = lax.all_to_all(back, 'mode', 0, 0, tiled=True)  9.62 us
    all_to_all x1, waiting for transfers between devices, section(): emf = lax.all_to_all(back, 'mode', 0, 0, tiled=True)  7.06 us
  transfers between devices with their start and end apart: 13, of which 4 were waited for; matrix products, arithmetic and copies ran while one was open for 1% of the time, Pallas kernels for 6%

profile of v1, /device:TPU:32, one launch (start us, length us, event | category | flops | bytes accessed | tf_op | source)
XLA Modules:
  0.0 144.3 jit_solution(6568304102265557467)
XLA Ops:
  0.6 1.6 %shard_map.113 = bf16[16,16,128]{2,1,0:T(8,128)(2,1)} custom-call(f32[6,8,512]{2,1,0:T(8,128)} %bitcast.6), custom_call_target="tpu_custom_call" | custom-call | tf_op jit(solution)/shard_map/pallas_call | solution.py:226
  2.3 12.9 %all-to-all-start = ((bf16[16,16,128]{2,1,0:T(8,128)(2,1)}), bf16[16,16,128]{2,1,0:T(8,128)(2,1)S(1)}, u32[]{:S(2)}, u32[]{:S(2)}) async-start(bf16[16,16,128]{2,1,0:T(8,128)(2,1)} %shard_map.113), calls=%async_computation | async-start | bytes 131072 | tf_op jit(solution)/shard_map/all_to_all | solution.py:239
  15.1 0.8 reshape.81.conn_ref
  15.9 1.9 %collective-permute-start.2 = (s32[8,128]{1,0:T(8,128)S(1)}, s32[8,128]{1,0:T(8,128)S(1)}, u32[]{:S(2)}, u32[]{:S(2)}) collective-permute-start(s32[8,128]{1,0:T(8,128)S(1)} %reshape.81.conn_ref), channel_id=1, source_target_pairs={{0,1},{1,2},{2,3},{3,4},{4,5},{5,6},{6,7},{7,8},{8,9},{9,10},{10,1... | collective-permute-start | bytes 12296 | tf_op jit(solution)/shard_map/ppermute | solution.py:221
  17.8 5.1 %collective-permute-done.2.far_ref = s32[8,128]{1,0:T(8,128)S(1)} collective-permute-done((s32[8,128]{1,0:T(8,128)S(1)}, s32[8,128]{1,0:T(8,128)S(1)}, u32[]{:S(2)}, u32[]{:S(2)}) %collective-permute-start.2) | collective-permute-done | bytes 4128 | tf_op jit(solution)/shard_map/ppermute | solution.py:221
  22.9 0.6 copy-done.14
  23.5 6.3 %shard_map.114 = (f32[256,128]{1,0:T(8,128)}, f32[256,128]{1,0:T(8,128)}, bf16[768,512]{1,0:T(8,128)(2,1)}, bf16[512,256]{1,0:T(8,128)(2,1)}, bf16[768,512]{1,0:T(8,128)(2,1)}, /*index=5*/bf16[512,256]{1,0:T(8,128)(2,1)}) custom-call(bf16[3,32,256]{2,1,0:T(8,128)(2,1)} %bitcast.10, f32[64,64]{1,0:T(8,128)} %stiff_ref.1, f32[64,64]{1,0:T(8,128)} %curl_ref.1, ...), custom_call_target="tpu_custom_call" | custom-call | tf_op jit(solution)/shard_map/pallas_call | solution.py:228
  29.8 0.6 copy-done.4
  30.4 2.2 %shard_map.115 = bf16[16,16,128]{2,1,0:T(8,128)(2,1)} custom-call(bf16[16,16,128]{2,1,0:T(8,128)(2,1)} %copy-done.4, f32[256,128]{1,0:T(8,128)} %get-tuple-element.14.va_ref, f32[256,128]{1,0:T(8,128)} %get-tuple-element.15.vb_ref, bf16[256,256]{1,0:T(8,128)(2,1)} %constant.43.clone.fwd_ref, bf16[256,256]{1,0:T(8,128)(2,1)} %constant.44.clone.inv_ref), custom_call_target="tpu_custom_call" | custom-call | tf_op jit(solution)/shard_map/pallas_call | solution.py:242
  32.6 9.6 %all-to-all-start.1 = ((bf16[16,16,128]{2,1,0:T(8,128)(2,1)}), bf16[16,16,128]{2,1,0:T(8,128)(2,1)S(1)}, u32[]{:S(2)}, u32[]{:S(2)}) async-start(bf16[16,16,128]{2,1,0:T(8,128)(2,1)} %shard_map.115), calls=%async_computation.1 | async-start | bytes 131072 | tf_op jit(solution)/shard_map/all_to_all | solution.py:243
  42.3 1.3 compare_select_fusion.wall_ref.refs_12_
  43.6 1.7 %shard_map.116 = bf16[32,16,128]{2,1,0:T(8,128)(2,1)} custom-call(f32[6,8,512]{2,1,0:T(8,128)} %bitcast.7, s32[1,128]{1,0:T(1,128)} %compare_select_fusion.wall_ref.refs_12_), custom_call_target="tpu_custom_call" | custom-call | tf_op jit(solution)/shard_map/pallas_call | solution.py:227
  45.3 7.1 %all-to-all-done.1.refs_3_ = bf16[16,16,128]{2,1,0:T(8,128)(2,1)S(1)} async-done(((bf16[16,16,128]{2,1,0:T(8,128)(2,1)}), bf16[16,16,128]{2,1,0:T(8,128)(2,1)S(1)}, u32[]{:S(2)}, u32[]{:S(2)}) %all-to-all-start.1) | async-done | bytes 65568 | tf_op jit(solution)/shard_map/all_to_all | solution.py:243
  52.3 7.4 %all-to-all-start.2 = ((bf16[32,16,128]{2,1,0:T(8,128)(2,1)}), bf16[32,16,128]{2,1,0:T(8,128)(2,1)S(1)}, u32[]{:S(2)}, u32[]{:S(2)}) async-start(bf16[32,16,128]{2,1,0:T(8,128)(2,1)} %shard_map.116), calls=%async_computation.2 | async-start | bytes 262144 | tf_op jit(solution)/shard_map/all_to_all | solution.py:246
  59.7 3.1 %collective-permute-start.1 = (bf16[16,16,128]{2,1,0:T(8,128)(2,1)}, bf16[16,16,128]{2,1,0:T(8,128)(2,1)S(1)}, u32[]{:S(2)}, u32[]{:S(2)}) collective-permute-start(bf16[16,16,128]{2,1,0:T(8,128)(2,1)} %shard_map.113), channel_id=1, source_target_pairs={{1,0},{2,1},{3,2},{4,3},{5,4},{6,5},{7,6},{8,7},{9,8},{10,9},{11,1... | collective-permute-start | bytes 196616 | tf_op jit(solution)/shard_map/ppermute | solution.py:241
  62.9 1.9 %collective-permute-start = (bf16[16,16,128]{2,1,0:T(8,128)(2,1)}, bf16[16,16,128]{2,1,0:T(8,128)(2,1)S(1)}, u32[]{:S(2)}, u32[]{:S(2)}) collective-permute-start(bf16[16,16,128]{2,1,0:T(8,128)(2,1)} %shard_map.113), channel_id=1, source_target_pairs={{0,1},{1,2},{2,3},{3,4},{4,5},{5,6},{6,7},{7,8},{8,9},{9,10},{10,1... | collective-permute-start | bytes 196616 | tf_op jit(solution)/shard_map/ppermute | solution.py:240
  64.8 5.8 %collective-permute-start.4 = (bf16[16,16,128]{2,1,0:T(8,128)(2,1)S(1)}, bf16[16,16,128]{2,1,0:T(8,128)(2,1)S(1)}, u32[]{:S(2)}, u32[]{:S(2)}) collective-permute-start(bf16[16,16,128]{2,1,0:T(8,128)(2,1)S(1)} %all-to-all-done.1.refs_3_), channel_id=1, source_target_pairs={{1,0},{2,1},{3,2},{4,3},{5,4},{6,5},{7,6},{8,7},{9,8},{10,9},{11,1... | collective-permute-start | bytes 196616 | tf_op jit(solution)/shard_map/ppermute | solution.py:245
  70.5 1.9 %collective-permute-start.3 = (bf16[16,16,128]{2,1,0:T(8,128)(2,1)S(1)}, bf16[16,16,128]{2,1,0:T(8,128)(2,1)S(1)}, u32[]{:S(2)}, u32[]{:S(2)}) collective-permute-start(bf16[16,16,128]{2,1,0:T(8,128)(2,1)S(1)} %all-to-all-done.1.refs_3_), channel_id=1, source_target_pairs={{0,1},{1,2},{2,3},{3,4},{4,5},{5,6},{6,7},{7,8},{8,9},{9,10},{10,1... | collective-permute-start | bytes 196616 | tf_op jit(solution)/shard_map/ppermute | solution.py:244
  72.6 5.7 %collective-permute-done.3.refs_4_ = bf16[16,16,128]{2,1,0:T(8,128)(2,1)S(1)} collective-permute-done((bf16[16,16,128]{2,1,0:T(8,128)(2,1)S(1)}, bf16[16,16,128]{2,1,0:T(8,128)(2,1)S(1)}, u32[]{:S(2)}, u32[]{:S(2)}) %collective-permute-start.3) | collective-permute-done | bytes 65568 | tf_op jit(solution)/shard_map/ppermute | solution.py:244
  78.3 0.6 copy-done.11
  78.9 4.6 %shard_map.117 = (f32[6,8,512]{2,1,0:T(8,128)}, bf16[16,16,128]{2,1,0:T(8,128)(2,1)}, bf16[32,16,128]{2,1,0:T(8,128)(2,1)}, f32[16,128]{1,0:T(8,128)}) custom-call(s32[1]{0:T(128)} %bitcast.mode_ref, f32[6,8,512]{2,1,0:T(8,128)} %bitcast.8, bf16[16,16,128]{2,1,0:T(8,128)(2,1)} %copy-done.7, bf16[16,16,128]{2,1,0:T(8,128)(2,1)} %copy-done.5, ...), custom_call_target="tpu_custom_call" | custom-call | tf_op jit(solution)/shard_map/pallas_call | solution.py:251
  83.4 14.2 %all_to_all.30.moved_ref = bf16[16,16,128]{2,1,0:T(8,128)(2,1)} all-to-all(bf16[16,16,128]{2,1,0:T(8,128)(2,1)} %get-tuple-element.21), channel_id=1, replica_groups=mesh['mode'=16,'mer'=32] {'mode'}, dimensions={0} | all-to-all | bytes 131072 | tf_op jit(solution)/shard_map/all_to_all | solution.py:239
  97.6 2.2 %shard_map.118 = bf16[16,16,128]{2,1,0:T(8,128)(2,1)} custom-call(bf16[16,16,128]{2,1,0:T(8,128)(2,1)} %all_to_all.30.moved_ref, f32[256,128]{1,0:T(8,128)} %get-tuple-element.14.va_ref, f32[256,128]{1,0:T(8,128)} %get-tuple-element.15.vb_ref, bf16[256,256]{1,0:T(8,128)(2,1)} %constant.43.clone.fwd_ref, bf16[256,256]{1,0:T(8,128)(2,1)} %constant.44.clone.inv_ref), custom_call_target="tpu_custom_call" | custom-call | tf_op jit(solution)/shard_map/pallas_call | solution.py:242
  99.8 13.5 %all_to_all.31.refs_3_ = bf16[16,16,128]{2,1,0:T(8,128)(2,1)S(1)} all-to-all(bf16[16,16,128]{2,1,0:T(8,128)(2,1)} %shard_map.118), channel_id=1, replica_groups=mesh['mode'=16,'mer'=32] {'mode'}, dimensions={0} | all-to-all | bytes 131072 | tf_op jit(solution)/shard_map/all_to_all | solution.py:243
  113.4 7.4 %all-to-all-start.5 = ((bf16[32,16,128]{2,1,0:T(8,128)(2,1)}), bf16[32,16,128]{2,1,0:T(8,128)(2,1)S(1)}, u32[]{:S(2)}, u32[]{:S(2)}) async-start(bf16[32,16,128]{2,1,0:T(8,128)(2,1)} %get-tuple-element.22), calls=%async_computation.5 | async-start | bytes 262144 | tf_op jit(solution)/shard_map/all_to_all | solution.py:246
  120.7 3.1 %collective-permute-start.6 = (bf16[16,16,128]{2,1,0:T(8,128)(2,1)}, bf16[16,16,128]{2,1,0:T(8,128)(2,1)S(1)}, u32[]{:S(2)}, u32[]{:S(2)}) collective-permute-start(bf16[16,16,128]{2,1,0:T(8,128)(2,1)} %get-tuple-element.21), channel_id=1, source_target_pairs={{1,0},{2,1},{3,2},{4,3},{5,4},{6,5},{7,6},{8,7},{9,8},{10,9},{11,1... | collective-permute-start | bytes 196616 | tf_op jit(solution)/shard_map/ppermute | solution.py:241
  123.9 1.9 %collective-permute-start.5 = (bf16[16,16,128]{2,1,0:T(8,128)(2,1)}, bf16[16,16,128]{2,1,0:T(8,128)(2,1)S(1)}, u32[]{:S(2)}, u32[]{:S(2)}) collective-permute-start(bf16[16,16,128]{2,1,0:T(8,128)(2,1)} %get-tuple-element.21), channel_id=1, source_target_pairs={{0,1},{1,2},{2,3},{3,4},{4,5},{5,6},{6,7},{7,8},{8,9},{9,10},{10,1... | collective-permute-start | bytes 196616 | tf_op jit(solution)/shard_map/ppermute | solution.py:240
  125.8 5.8 %collective-permute-start.8 = (bf16[16,16,128]{2,1,0:T(8,128)(2,1)S(1)}, bf16[16,16,128]{2,1,0:T(8,128)(2,1)S(1)}, u32[]{:S(2)}, u32[]{:S(2)}) collective-permute-start(bf16[16,16,128]{2,1,0:T(8,128)(2,1)S(1)} %all_to_all.31.refs_3_), channel_id=1, source_target_pairs={{1,0},{2,1},{3,2},{4,3},{5,4},{6,5},{7,6},{8,7},{9,8},{10,9},{11,1... | collective-permute-start | bytes 196616 | tf_op jit(solution)/shard_map/ppermute | solution.py:245
  131.6 1.9 %collective-permute-start.7 = (bf16[16,16,128]{2,1,0:T(8,128)(2,1)S(1)}, bf16[16,16,128]{2,1,0:T(8,128)(2,1)S(1)}, u32[]{:S(2)}, u32[]{:S(2)}) collective-permute-start(bf16[16,16,128]{2,1,0:T(8,128)(2,1)S(1)} %all_to_all.31.refs_3_), channel_id=1, source_target_pairs={{0,1},{1,2},{2,3},{3,4},{4,5},{5,6},{6,7},{7,8},{8,9},{9,10},{10,1... | collective-permute-start | bytes 196616 | tf_op jit(solution)/shard_map/ppermute | solution.py:244
  133.6 5.7 %collective-permute-done.7.refs_4_ = bf16[16,16,128]{2,1,0:T(8,128)(2,1)S(1)} collective-permute-done((bf16[16,16,128]{2,1,0:T(8,128)(2,1)S(1)}, bf16[16,16,128]{2,1,0:T(8,128)(2,1)S(1)}, u32[]{:S(2)}, u32[]{:S(2)}) %collective-permute-start.7) | collective-permute-done | bytes 65568 | tf_op jit(solution)/shard_map/ppermute | solution.py:244
  139.3 0.6 copy-done.12
  139.9 4.5 %shard_map.119 = (f32[6,8,512]{2,1,0:T(8,128)}, f32[2,8,2,64]{3,2,1,0:T(2,128)}) custom-call(s32[1]{0:T(128)} %bitcast.mode_ref, f32[6,8,512]{2,1,0:T(8,128)} %get-tuple-element.20.refs_0_, bf16[16,16,128]{2,1,0:T(8,128)(2,1)} %copy-done.8, bf16[16,16,128]{2,1,0:T(8,128)(2,1)} %copy-done.6, bf16[16,16,128]{2,1,0:T(8,128)(2,1)} %copy-done.3, ...), custom_call_target="tpu_custom_call" | custom-call | tf_op jit(solution)/shard_map/pallas_call | solution.py:253
  (35 shorter events, 0.1 us)
Async XLA Ops:
  2.3 27.5 %all-to-all-start = ((bf16[16,16,128]{2,1,0:T(8,128)(2,1)}), bf16[16,16,128]{2,1,0:T(8,128)(2,1)S(1)}, u32[]{:S(2)}, u32[]{:S(2)}) async-start(bf16[16,16,128]{2,1,0:T(8,128)(2,1)} %shard_map.113), calls=%async_computation | async-start | bytes 131072 | tf_op jit(solution)/shard_map/all_to_all | solution.py:239
  15.9 7.0 %copy-start.13 = (s32[8,128]{1,0:T(8,128)}, s32[8,128]{1,0:T(8,128)S(1)}, u32[]{:S(2)}) copy-start(s32[8,128]{1,0:T(8,128)S(1)} %reshape.81.conn_ref) | copy-start | bytes 12292
  15.9 7.0 %collective-permute-start.2 = (s32[8,128]{1,0:T(8,128)S(1)}, s32[8,128]{1,0:T(8,128)S(1)}, u32[]{:S(2)}, u32[]{:S(2)}) collective-permute-start(s32[8,128]{1,0:T(8,128)S(1)} %reshape.81.conn_ref), channel_id=1, source_target_pairs={{0,1},{1,2},{2,3},{3,4},{4,5},{5,6},{6,7},{7,8},{8,9},{9,10},{10,1... | collective-permute-start | bytes 12296 | tf_op jit(solution)/shard_map/ppermute | solution.py:221
  22.9 0.6 copy-start.14
  29.8 0.6 copy-start.4
  32.6 19.7 %all-to-all-start.1 = ((bf16[16,16,128]{2,1,0:T(8,128)(2,1)}), bf16[16,16,128]{2,1,0:T(8,128)(2,1)S(1)}, u32[]{:S(2)}, u32[]{:S(2)}) async-start(bf16[16,16,128]{2,1,0:T(8,128)(2,1)} %shard_map.115), calls=%async_computation.1 | async-start | bytes 131072 | tf_op jit(solution)/shard_map/all_to_all | solution.py:243
  52.3 25.9 %copy-start.2 = (bf16[16,16,128]{2,1,0:T(8,128)(2,1)}, bf16[16,16,128]{2,1,0:T(8,128)(2,1)S(1)}, u32[]{:S(2)}) copy-start(bf16[16,16,128]{2,1,0:T(8,128)(2,1)S(1)} %all-to-all-done.1.refs_3_) | copy-start | bytes 196612
  52.3 20.2 %all-to-all-start.2 = ((bf16[32,16,128]{2,1,0:T(8,128)(2,1)}), bf16[32,16,128]{2,1,0:T(8,128)(2,1)S(1)}, u32[]{:S(2)}, u32[]{:S(2)}) async-start(bf16[32,16,128]{2,1,0:T(8,128)(2,1)} %shard_map.116), calls=%async_computation.2 | async-start | bytes 262144 | tf_op jit(solution)/shard_map/all_to_all | solution.py:246
  59.7 12.8 %collective-permute-start.1 = (bf16[16,16,128]{2,1,0:T(8,128)(2,1)}, bf16[16,16,128]{2,1,0:T(8,128)(2,1)S(1)}, u32[]{:S(2)}, u32[]{:S(2)}) collective-permute-start(bf16[16,16,128]{2,1,0:T(8,128)(2,1)} %shard_map.113), channel_id=1, source_target_pairs={{1,0},{2,1},{3,2},{4,3},{5,4},{6,5},{7,6},{8,7},{9,8},{10,9},{11,1... | collective-permute-start | bytes 196616 | tf_op jit(solution)/shard_map/ppermute | solution.py:241
  62.9 9.6 %collective-permute-start = (bf16[16,16,128]{2,1,0:T(8,128)(2,1)}, bf16[16,16,128]{2,1,0:T(8,128)(2,1)S(1)}, u32[]{:S(2)}, u32[]{:S(2)}) collective-permute-start(bf16[16,16,128]{2,1,0:T(8,128)(2,1)} %shard_map.113), channel_id=1, source_target_pairs={{0,1},{1,2},{2,3},{3,4},{4,5},{5,6},{6,7},{7,8},{8,9},{9,10},{10,1... | collective-permute-start | bytes 196616 | tf_op jit(solution)/shard_map/ppermute | solution.py:240
  64.8 7.8 %collective-permute-start.4 = (bf16[16,16,128]{2,1,0:T(8,128)(2,1)S(1)}, bf16[16,16,128]{2,1,0:T(8,128)(2,1)S(1)}, u32[]{:S(2)}, u32[]{:S(2)}) collective-permute-start(bf16[16,16,128]{2,1,0:T(8,128)(2,1)S(1)} %all-to-all-done.1.refs_3_), channel_id=1, source_target_pairs={{1,0},{2,1},{3,2},{4,3},{5,4},{6,5},{7,6},{8,7},{9,8},{10,9},{11,1... | collective-permute-start | bytes 196616 | tf_op jit(solution)/shard_map/ppermute | solution.py:245
  70.5 7.7 %collective-permute-start.3 = (bf16[16,16,128]{2,1,0:T(8,128)(2,1)S(1)}, bf16[16,16,128]{2,1,0:T(8,128)(2,1)S(1)}, u32[]{:S(2)}, u32[]{:S(2)}) collective-permute-start(bf16[16,16,128]{2,1,0:T(8,128)(2,1)S(1)} %all-to-all-done.1.refs_3_), channel_id=1, source_target_pairs={{0,1},{1,2},{2,3},{3,4},{4,5},{5,6},{6,7},{7,8},{8,9},{9,10},{10,1... | collective-permute-start | bytes 196616 | tf_op jit(solution)/shard_map/ppermute | solution.py:244
  72.5 5.8 %copy-start.5 = (bf16[16,16,128]{2,1,0:T(8,128)(2,1)}, bf16[16,16,128]{2,1,0:T(8,128)(2,1)S(1)}, u32[]{:S(2)}) copy-start(bf16[16,16,128]{2,1,0:T(8,128)(2,1)S(1)} %collective-permute-done.1.refs_2_) | copy-start | bytes 196612
  72.5 5.7 %copy-start.7 = (bf16[16,16,128]{2,1,0:T(8,128)(2,1)}, bf16[16,16,128]{2,1,0:T(8,128)(2,1)S(1)}, u32[]{:S(2)}) copy-start(bf16[16,16,128]{2,1,0:T(8,128)(2,1)S(1)} %collective-permute-done.refs_1_) | copy-start | bytes 196612
  72.5 5.7 %copy-start = (bf16[32,16,128]{2,1,0:T(8,128)(2,1)}, bf16[32,16,128]{2,1,0:T(8,128)(2,1)S(1)}, u32[]{:S(2)}) copy-start(bf16[32,16,128]{2,1,0:T(8,128)(2,1)S(1)} %all-to-all-done.2.refs_10_) | copy-start | bytes 393220
  72.5 5.7 %copy-start.9 = (bf16[16,16,128]{2,1,0:T(8,128)(2,1)}, bf16[16,16,128]{2,1,0:T(8,128)(2,1)S(1)}, u32[]{:S(2)}) copy-start(bf16[16,16,128]{2,1,0:T(8,128)(2,1)S(1)} %collective-permute-done.4.refs_5_) | copy-start | bytes 196612
  78.2 0.6 copy-start.11
  113.4 25.9 %copy-start.3 = (bf16[16,16,128]{2,1,0:T(8,128)(2,1)}, bf16[16,16,128]{2,1,0:T(8,128)(2,1)S(1)}, u32[]{:S(2)}) copy-start(bf16[16,16,128]{2,1,0:T(8,128)(2,1)S(1)} %all_to_all.31.refs_3_) | copy-start | bytes 196612
  113.4 20.2 %all-to-all-start.5 = ((bf16[32,16,128]{2,1,0:T(8,128)(2,1)}), bf16[32,16,128]{2,1,0:T(8,128)(2,1)S(1)}, u32[]{:S(2)}, u32[]{:S(2)}) async-start(bf16[32,16,128]{2,1,0:T(8,128)(2,1)} %get-tuple-element.22), calls=%async_computation.5 | async-start | bytes 262144 | tf_op jit(solution)/shard_map/all_to_all | solution.py:246
  120.7 12.7 %collective-permute-start.6 = (bf16[16,16,128]{2,1,0:T(8,128)(2,1)}, bf16[16,16,128]{2,1,0:T(8,128)(2,1)S(1)}, u32[]{:S(2)}, u32[]{:S(2)}) collective-permute-start(bf16[16,16,128]{2,1,0:T(8,128)(2,1)} %get-tuple-element.21), channel_id=1, source_target_pairs={{1,0},{2,1},{3,2},{4,3},{5,4},{6,5},{7,6},{8,7},{9,8},{10,9},{11,1... | collective-permute-start | bytes 196616 | tf_op jit(solution)/shard_map/ppermute | solution.py:241
  123.9 9.6 %collective-permute-start.5 = (bf16[16,16,128]{2,1,0:T(8,128)(2,1)}, bf16[16,16,128]{2,1,0:T(8,128)(2,1)S(1)}, u32[]{:S(2)}, u32[]{:S(2)}) collective-permute-start(bf16[16,16,128]{2,1,0:T(8,128)(2,1)} %get-tuple-element.21), channel_id=1, source_target_pairs={{0,1},{1,2},{2,3},{3,4},{4,5},{5,6},{6,7},{7,8},{8,9},{9,10},{10,1... | collective-permute-start | bytes 196616 | tf_op jit(solution)/shard_map/ppermute | solution.py:240
  125.8 7.8 %collective-permute-start.8 = (bf16[16,16,128]{2,1,0:T(8,128)(2,1)S(1)}, bf16[16,16,128]{2,1,0:T(8,128)(2,1)S(1)}, u32[]{:S(2)}, u32[]{:S(2)}) collective-permute-start(bf16[16,16,128]{2,1,0:T(8,128)(2,1)S(1)} %all_to_all.31.refs_3_), channel_id=1, source_target_pairs={{1,0},{2,1},{3,2},{4,3},{5,4},{6,5},{7,6},{8,7},{9,8},{10,9},{11,1... | collective-permute-start | bytes 196616 | tf_op jit(solution)/shard_map/ppermute | solution.py:245
  131.6 7.7 %collective-permute-start.7 = (bf16[16,16,128]{2,1,0:T(8,128)(2,1)S(1)}, bf16[16,16,128]{2,1,0:T(8,128)(2,1)S(1)}, u32[]{:S(2)}, u32[]{:S(2)}) collective-permute-start(bf16[16,16,128]{2,1,0:T(8,128)(2,1)S(1)} %all_to_all.31.refs_3_), channel_id=1, source_target_pairs={{0,1},{1,2},{2,3},{3,4},{4,5},{5,6},{6,7},{7,8},{8,9},{9,10},{10,1... | collective-permute-start | bytes 196616 | tf_op jit(solution)/shard_map/ppermute | solution.py:244
  133.5 5.8 %copy-start.6 = (bf16[16,16,128]{2,1,0:T(8,128)(2,1)}, bf16[16,16,128]{2,1,0:T(8,128)(2,1)S(1)}, u32[]{:S(2)}) copy-start(bf16[16,16,128]{2,1,0:T(8,128)(2,1)S(1)} %collective-permute-done.6.refs_2_) | copy-start | bytes 196612
  133.5 5.7 %copy-start.8 = (bf16[16,16,128]{2,1,0:T(8,128)(2,1)}, bf16[16,16,128]{2,1,0:T(8,128)(2,1)S(1)}, u32[]{:S(2)}) copy-start(bf16[16,16,128]{2,1,0:T(8,128)(2,1)S(1)} %collective-permute-done.5.refs_1_) | copy-start | bytes 196612
  133.5 5.7 %copy-start.1 = (bf16[32,16,128]{2,1,0:T(8,128)(2,1)}, bf16[32,16,128]{2,1,0:T(8,128)(2,1)S(1)}, u32[]{:S(2)}) copy-start(bf16[32,16,128]{2,1,0:T(8,128)(2,1)S(1)} %all-to-all-done.5.refs_10_) | copy-start | bytes 393220
  133.6 5.7 %copy-start.10 = (bf16[16,16,128]{2,1,0:T(8,128)(2,1)}, bf16[16,16,128]{2,1,0:T(8,128)(2,1)S(1)}, u32[]{:S(2)}) copy-start(bf16[16,16,128]{2,1,0:T(8,128)(2,1)S(1)} %collective-permute-done.8.refs_5_) | copy-start | bytes 196612
  139.2 0.6 copy-start.12

commit v2 on v1

v2 whole, which is shorter than its diff:
```python
import numpy as np
import jax
import jax.numpy as jnp
from jax import lax
from jax.experimental import pallas as pl
from jax.experimental.pallas import tpu as pltpu
from jax.sharding import PartitionSpec as P


BF = jnp.bfloat16
F32 = jnp.float32


def nt(a, b):
    return lax.dot_general(a, b, (((1,), (1,)), ((), ())), preferred_element_type=F32)


def nn(a, b):
    return jnp.dot(a, b, preferred_element_type=F32)


def tables(modes, nphi, mode_dev):
    mode = np.arange(modes).reshape(-1, 1, mode_dev)
    k = np.arange(nphi).reshape(-1, 1, 1, 1)
    angle = 2.0 * np.pi * ((mode[None] * k) % nphi) / nphi
    fwd = np.concatenate([np.cos(angle), -np.sin(angle)], 2).reshape(nphi, 2 * modes)
    return fwd.astype(BF), (fwd.T / nphi).astype(BF)


def lane_group(shape):
    return lax.broadcasted_iota(jnp.int32, shape, len(shape) - 1) // 32


def pick(group, parts):
    out = parts[0]
    for g, part in enumerate(parts[1:], 1):
        out = jnp.where(group == g, part, out)
    return out


def shift(x, groups):
    return x if groups % 4 == 0 else pltpu.roll(x, 32 * (groups % 4), 1)


def pack(rows, out_ref):
    group = lane_group((8, 128))
    for v in range(4):
        tiles = {cp: r[:, 128 * v : 128 * v + 128] for cp, r in rows.items()}
        for q in range(4):
            halves = [
                pick(group, [shift(tiles[c % 3, p], c - q) for c in range(4)]) for p in range(2)
            ]
            out_ref[4 * v + q] = jnp.concatenate(halves, 0).astype(BF)


def unpack(tile, slots):
    group = lane_group((16, 128))
    cols = []
    for v in range(slots // 4):
        tiles = [tile(4 * v + q).astype(F32) for q in range(4)]
        cols.append(
            jnp.concatenate(
                [pick(group, [shift(tiles[q], q - c) for q in range(4)]) for c in range(3)], 0
            ).astype(BF)
        )
    return jnp.concatenate(cols, 1)


def wall_onehot(wall_ref, mer):
    twice = jnp.concatenate([wall_ref[...], wall_ref[...]], 1)
    nodes = lax.broadcasted_iota(jnp.int32, (512, 128), 0)
    half = lax.broadcasted_iota(jnp.int32, (512, 128), 1) // 64
    return jnp.where(half == mer % 2, (nodes == twice).astype(F32), 0.0).astype(BF)


def two_by_two(conn_ref):
    return jnp.concatenate([conn_ref[pl.ds(0, 8, 2), :], conn_ref[pl.ds(1, 8, 2), :]], 1)


def open_kernel(mer_ref, field_ref, wall_ref, conn_ref, pack_ref, out_ref):
    pack({(c, p): field_ref[3 * p + c] for c in range(3) for p in range(2)}, pack_ref)
    last = jnp.concatenate([field_ref[2], field_ref[5]], 0).astype(BF)
    tr = nn(last, wall_onehot(wall_ref, mer_ref[0]))
    conn = two_by_two(conn_ref)
    parts = [tr, (conn // 32).astype(F32), (conn % 32).astype(F32)]
    parts = jnp.concatenate(parts, 0).astype(BF)
    for j in range(out_ref.shape[0]):
        out_ref[j] = parts


def element_blocks(ref, sign):
    row = lax.broadcasted_iota(jnp.int32, (256, 64), 0)
    col = lax.broadcasted_iota(jnp.int32, (256, 64), 1)
    spread = (row % 64 == col).astype(F32).astype(BF)
    near = lax.broadcasted_iota(jnp.int32, (256, 256), 0) // 64
    same = near == lax.broadcasted_iota(jnp.int32, (256, 256), 1) // 64
    once = nt(spread, ref[...].astype(BF)).astype(BF)
    return jnp.where(same, sign * nt(once, spread), 0.0).astype(BF)


def operators(conn, first, width, stiff_ref, curl_ref, tall_ref, work_ref):
    across = conn.T
    nodes = lax.broadcasted_iota(jnp.int32, (768, 128), 0).astype(F32)
    lanes = lax.broadcasted_iota(jnp.int32, (128, width), 1).astype(F32) + first
    mats = [element_blocks(stiff_ref, -1.0), element_blocks(curl_ref, 1.0)]
    for t in range(8):
        tall_ref[:, 128 * t : 128 * t + 128] = (nodes == conn[t : t + 1]).astype(F32).astype(BF)
    for u in range(4):
        picks = [
            (lanes == across[:, t : t + 1]).astype(F32).astype(BF) for t in (2 * u, 2 * u + 1)
        ]
        picks = jnp.concatenate(picks, 0)
        for k, mat in enumerate(mats):
            work_ref[k, 256 * u : 256 * u + 256] = nn(mat, picks).astype(BF)
    return nn(tall_ref[...], work_ref[0]), nn(tall_ref[...], work_ref[1])


def own_kernel(vel_ref, stiff_ref, curl_ref, conn_ref, va_ref, vb_ref, s_ref, near_ref, tall_ref, work_ref):
    vel = [vel_ref[c].astype(F32) for c in range(3)]
    zero = jnp.zeros_like(vel[0])
    va_ref[...] = jnp.concatenate([vel[0], vel[1], vel[2], zero], 0).T.astype(BF)
    vb_ref[...] = jnp.concatenate([vel[1], vel[2], vel[0], zero], 0).T.astype(BF)
    conn = two_by_two(conn_ref).astype(F32)
    s, c = operators(conn, 0.0, 512, stiff_ref, curl_ref, tall_ref, work_ref)
    s_ref[...] = s[:512].astype(BF)
    near_ref[:768] = c.astype(BF)
    near_ref[768:] = s[512:].astype(BF)


def far_kernel(mer_ref, whole_ref, stiff_ref, curl_ref, far_ref, tall_ref, work_ref):
    code = whole_ref[jnp.maximum(mer_ref[0] - 1, 0)].astype(F32)
    conn = 32.0 * code[16:24] + code[24:32]
    s, c = operators(conn, 512.0, 256, stiff_ref, curl_ref, tall_ref, work_ref)
    there = jnp.where(mer_ref[0] > 0, 1.0, 0.0)
    far_ref[:768] = (c * there).astype(BF)
    far_ref[768:] = (s * there).astype(BF)


def induce_kernel(moved_ref, va_ref, vb_ref, fwd_ref, inv_ref, out_ref):
    moved = moved_ref[...]
    rows = moved.reshape(256, 128)
    turned = pltpu.roll(rows.astype(F32), 96, 1).astype(BF)
    here = nn(fwd_ref[...], rows)
    after = nn(fwd_ref[...], turned)
    cross = va_ref[...].astype(F32) * after - vb_ref[...].astype(F32) * here
    back = nn(inv_ref[...], cross.astype(BF))
    out_ref[:, :16] = back.astype(BF).reshape(16, 16, 128)
    out_ref[:, 16:] = moved


ORDER = [3 * p + c for c in range(3) for p in range(2)]


def stiff_kernel(field_ref, s_ref, out_ref):
    field = jnp.concatenate([field_ref[s] for s in ORDER], 0)
    out_ref[...] = nn(field.astype(BF), s_ref[...])


def section_rows(refs, scratch):
    mode_ref, mer_ref, field_ref, part_ref, emf_ref, pa_ref, pb_ref, whole_ref, wall_ref, mass_ref = refs[:10]
    near_ref, far_ref, dtn_ref = refs[10:13]
    near_buf, far_buf, dtn_buf, sems = scratch
    copies = [
        pltpu.make_async_copy(a, b, sems.at[k])
        for k, (a, b) in enumerate(((near_ref, near_buf), (far_ref, far_buf), (dtn_ref, dtn_buf)))
    ]
    for copy in copies:
        copy.start()
    odd = (jnp.zeros((16, 128), jnp.int32) + mer_ref[0] % 2) == 1

    def before(part):
        rows = slice(16 * part, 16 * part + 16)
        return lambda s: jnp.where(odd, pa_ref[s, rows].astype(F32), pb_ref[s, rows].astype(F32))

    def behind(part):
        rows = slice(16 * part, 16 * part + 16)
        return lambda s: jnp.where(odd, pb_ref[s, rows].astype(F32), pa_ref[s, rows].astype(F32))

    field = jnp.concatenate([field_ref[s] for s in ORDER], 0)
    own = unpack(lambda s: emf_ref[s, :16], 16)
    near = jnp.concatenate([own, unpack(behind(0), 8), unpack(behind(1), 8)], 1)
    far = jnp.concatenate([unpack(before(0), 16), own[:, :256], unpack(before(1), 16), field[:, :256].astype(BF)], 1)
    copies[0].wait()
    total = part_ref[...] + nn(near, near_buf[...])
    copies[1].wait()
    low = nn(far, far_buf[...])
    total = jnp.concatenate([total[:, :256] + low, total[:, 256:]], 1)
    whole = jnp.concatenate([whole_ref[2 * a, :16] + whole_ref[2 * a + 1, :16] for a in range(16)], 1)
    copies[2].wait()
    every = nt(whole, dtn_buf[...].reshape(512, 2048))
    mine = lax.broadcasted_iota(jnp.int32, (16, 512), 0) % 8
    every = jnp.where(mine == lax.broadcasted_iota(jnp.int32, (16, 512), 1) // 64, every, 0.0)
    flux = every[:, :128] + every[:, 128:256] + every[:, 256:384] + every[:, 384:]
    flux = flux + pltpu.roll(flux, 64, 1)
    onehot = wall_onehot(wall_ref, mer_ref[0])
    upper = flux.astype(BF)
    added = nt(upper, onehot) + nt((flux - upper.astype(F32)).astype(BF), onehot)
    total = jnp.concatenate([total[:32], total[32:] - 0.5 * added], 0)
    number = lax.broadcasted_iota(jnp.int32, (48, 512), 0) % 8 + 8 * mode_ref[0]
    coef = (number.astype(F32) / 128.0) ** 2
    rate = total / mass_ref[...] - 4.0 * coef * field
    return rate, field, flux, onehot


def first_kernel(*refs):
    sect_ref, pack_ref, trace_ref, flux_ref = refs[13:17]
    rate, field, flux, onehot = section_rows(refs, refs[17:])
    sect = field + 0.2 * rate
    flux_ref[...] = flux
    rows = {(c, p): sect[16 * c + 8 * p : 16 * c + 8 * p + 8] for c in range(3) for p in range(2)}
    for (c, p), r in rows.items():
        sect_ref[3 * p + c] = r
    pack(rows, pack_ref)
    tr = nn(sect[32:].astype(BF), onehot).astype(BF)
    for j in range(trace_ref.shape[0]):
        trace_ref[j] = tr


def second_kernel(*refs):
    start_ref, first_flux_ref, out_ref, flux_ref = refs[13:17]
    rate, sect, flux, onehot = section_rows(refs, refs[17:])
    for c in range(3):
        for p in range(2):
            at = slice(16 * c + 8 * p, 16 * c + 8 * p + 8)
            out_ref[3 * p + c] = 0.5 * (start_ref[3 * p + c] + sect[at] + 0.2 * rate[at])
    for p in range(2):
        flux_ref[0, :, p, :] = first_flux_ref[8 * p : 8 * p + 8, :64]
        flux_ref[1, :, p, :] = flux[8 * p : 8 * p + 8, :64]


def call(kernel, out, where, scratch=(), limit=16):
    spec = {k: pl.BlockSpec(memory_space=pltpu.VMEM) for k in "vc"}
    spec["s"] = pl.BlockSpec(memory_space=pltpu.SMEM)
    spec["h"] = pl.BlockSpec(memory_space=pl.ANY)
    made = pl.pallas_call(
        kernel,
        out_shape=[pltpu.VMEM(s, d) if near else jax.ShapeDtypeStruct(s, d) for s, d, near in out],
        in_specs=[spec[k] for k in where],
        out_specs=[spec["v"]] * len(out),
        scratch_shapes=list(scratch),
        compiler_params=pltpu.CompilerParams(vmem_limit_bytes=limit * 2**20),
    )

    def run(*args):
        return made(
            *[
                pltpu.with_memory_space_constraint(a, pltpu.VMEM) if k == "v" else a
                for k, a in zip(where, args, strict=True)
            ]
        )

    return run


def body(field, velocity, stiffness, curl_matrix, mass, connect, wall_index, dtn):
    fwd, inv = tables(128, 256, 8)
    spots = lax.axis_size("mer")
    mer = lax.axis_index("mer").astype(jnp.int32).reshape(1)
    mode = lax.axis_index("mode").astype(jnp.int32).reshape(1)
    start = jnp.transpose(field, (1, 0, 2))
    wall = wall_index.reshape(1, 64)
    row = mass.reshape(1, 512)
    works = [pltpu.VMEM((768, 1024), BF), pltpu.VMEM((2, 1024, 512), BF)]

    packed, trace = call(
        open_kernel, [((16, 16, 128), BF, True), ((spots, 32, 128), BF, True)], "sccc"
    )(mer, start, wall, connect)
    va, vb, s_own, near = call(
        own_kernel,
        [((256, 128), BF, False)] * 2 + [((512, 512), BF, False), ((1024, 512), BF, False)],
        "cccc",
        works,
        32,
    )(jnp.transpose(velocity, (0, 2, 1)), stiffness, curl_matrix, connect)

    twins = [(i, i ^ 1) for i in range(spots)]
    others = [(i, ((i + 1) ^ 1) - 1) for i in range(1, spots - 1)]

    def section(now, packed, trace, far, last):
        whole = lax.all_to_all(trace, "mer", 0, 0, tiled=True)
        if far is None:
            works[1] = pltpu.VMEM((2, 1024, 256), BF)
            (far,) = call(far_kernel, [((1536, 256), BF, False)], "sccc", works, 32)(
                mer, whole, stiffness, curl_matrix
            )
        moved = lax.all_to_all(packed, "mode", 0, 0, tiled=True)
        (back,) = call(induce_kernel, [((16, 32, 128), BF, True)], "vvvvv")(moved, va, vb, fwd, inv)
        emf = lax.all_to_all(back, "mode", 0, 0, tiled=True)
        (part,) = call(stiff_kernel, [((48, 512), F32, True)], "cc")(now, s_own)
        e_twin = lax.ppermute(emf, "mer", twins)
        e_other = lax.ppermute(emf, "mer", others)
        args = (mode, mer, now, part, emf, e_twin, e_other, whole, wall, row, near, far, dtn)
        kinds = "ss" + ("c" if last is None else "v") + "vvvvvcchhh"
        bufs = [
            pltpu.VMEM((1024, 512), BF),
            pltpu.VMEM((1536, 256), BF),
            pltpu.VMEM((8, 64, 2048), BF),
            pltpu.SemaphoreType.DMA((3,)),
        ]
        if last is None:
            out = [((6, 8, 512), F32, True), ((16, 16, 128), BF, True)]
            out += [((spots, 16, 128), BF, True), ((16, 128), F32, False)]
            return far, call(first_kernel, out, kinds, bufs)(*args)
        out = [((6, 8, 512), F32, False), ((2, 8, 2, 64), F32, False)]
        return far, call(second_kernel, out, kinds + "cc", bufs)(*args, *last)

    far, (sect, packed, trace, flux) = section(start, packed, trace, None, None)
    far, (done, fluxes) = section(sect, packed, trace, far, (start, flux))
    return (jnp.transpose(done, (1, 0, 2)), fluxes)


def solution(mesh):
    placed = (
        P("mode", None, "mer"),
        P(None, None, ("mer", "mode")),
        P(),
        P(),
        P("mer"),
        P("mer", None),
        P("mer"),
        P("mode", "mer", None),
    )
    return jax.shard_map(
        body,
        mesh=mesh,
        in_specs=placed,
        out_specs=(P("mode", None, "mer"), P(None, "mode", None, "mer")),
        check_vma=False,
    )
```

time: 145 us -> 126 us (0.87)
  the two profiles are of different devices: /device:TPU:32 before, /device:TPU:1 now
where the time goes in v2:
time: 126 us; the launch traced here: 125 us
  starting transfers between devices  42.8 us (34%)
  blocking collectives  40.1 us (32%)
  local copies, waits for them, and re-layouts  17.9 us (14%)
  Pallas kernels  13.3 us (11%)
  waiting for transfers between devices  9.75 us (8%)
    all_to_all x2, blocking collectives, section(): emf = lax.all_to_all(back, 'mode', 0, 0, tiled=True)  28.2 us
    all_to_all x2, starting transfers between devices, section(): whole = lax.all_to_all(trace, 'mer', 0, 0, tiled=True)  18.4 us
    unnamed x64, local copies, waits for them, and re-layouts  17.9 us
    all_to_all x1, starting transfers between devices, section(): moved = lax.all_to_all(packed, 'mode', 0, 0, tiled=True)  13.4 us
    pallas_call x9, Pallas kernels, run(): made(*[pltpu.with_memory_space_constraint(a, pltpu.VMEM) if k == 'v' else...  13.3 us
    all_to_all x1, blocking collectives, section(): moved = lax.all_to_all(packed, 'mode', 0, 0, tiled=True)  11.9 us
    all_to_all x2, waiting for transfers between devices, section(): whole = lax.all_to_all(trace, 'mer', 0, 0, tiled=True)  7.53 us
    ppermute x2, starting transfers between devices, section(): e_other = lax.ppermute(emf, 'mer', others)  7.09 us
  transfers between devices with their start and end apart: 7, of which 3 were waited for; matrix products, arithmetic and copies ran while one was open for 0% of the time, Pallas kernels for 4%

profile of v2, /device:TPU:1, one launch (start us, length us, event | category | flops | bytes accessed | tf_op | source)
XLA Modules:
  0.0 124.7 jit_solution(15726320866729783959)
XLA Ops:
  0.7 1.0 copy-done.6
  3.0 0.8 shard_map.115
  4.5 13.4 %all-to-all-start = ((bf16[16,16,128]{2,1,0:T(8,128)(2,1)}), bf16[16,16,128]{2,1,0:T(8,128)(2,1)S(1)}, u32[]{:S(2)}, u32[]{:S(2)}) async-start(bf16[16,16,128]{2,1,0:T(8,128)(2,1)} %get-tuple-element.15), calls=%async_computation | async-start | bytes 131072 | tf_op jit(solution)/shard_map/all_to_all | solution.py:286
  18.7 0.8 copy-done.22
  19.4 0.8 copy-done.24
  20.9 2.7 %shard_map.113 = (bf16[256,128]{1,0:T(8,128)(2,1)S(1)}, bf16[256,128]{1,0:T(8,128)(2,1)S(1)}, bf16[512,512]{1,0:T(8,128)(2,1)S(1)}, bf16[1024,512]{1,0:T(8,128)(2,1)S(1)}) custom-call(bf16[3,32,256]{2,1,0:T(8,128)(2,1)S(1)} %bitcast.11, f32[64,64]{1,0:T(8,128)S(1)} %copy-done.20, f32[64,64]{1,0:T(8,128)S(1)} %copy-done.22, s32[16,64]{1,0:T(8,128)S(1)} %copy-done.26), custom_call_target="tpu_custom_call" | custom-call | tf_op jit(solution)/shard_map/pallas_call | solution.py:245
  23.7 1.0 copy-done.1
  24.7 2.2 %all-to-all-done.moved_ref = bf16[16,16,128]{2,1,0:T(8,128)(2,1)S(1)} async-done(((bf16[16,16,128]{2,1,0:T(8,128)(2,1)}), bf16[16,16,128]{2,1,0:T(8,128)(2,1)S(1)}, u32[]{:S(2)}, u32[]{:S(2)}) %all-to-all-start) | async-done | bytes 65568 | tf_op jit(solution)/shard_map/all_to_all | solution.py:286
  26.9 0.9 copy-done.10
  27.8 0.9 copy-done.12
  29.2 16.1 %all_to_all.30.refs_4_ = bf16[16,32,128]{2,1,0:T(8,128)(2,1)S(1)} all-to-all(bf16[16,32,128]{2,1,0:T(8,128)(2,1)S(1)} %shard_map.116), channel_id=1, replica_groups=mesh['mode'=16,'mer'=32] {'mode'}, dimensions={0} | all-to-all | bytes 262144 | tf_op jit(solution)/shard_map/all_to_all | solution.py:288
  45.3 10.7 %all-to-all-start.2 = ((bf16[32,32,128]{2,1,0:T(8,128)(2,1)}), bf16[32,32,128]{2,1,0:T(8,128)(2,1)S(1)}, u32[]{:S(2)}, u32[]{:S(2)}) async-start(bf16[32,32,128]{2,1,0:T(8,128)(2,1)} %copy-done.18), calls=%async_computation.2 | async-start | bytes 524288 | tf_op jit(solution)/shard_map/all_to_all | solution.py:280
  56.0 3.5 %collective-permute-start.1 = (bf16[16,32,128]{2,1,0:T(8,128)(2,1)S(1)}, bf16[16,32,128]{2,1,0:T(8,128)(2,1)}, u32[]{:S(2)}, u32[]{:S(2)}) collective-permute-start(bf16[16,32,128]{2,1,0:T(8,128)(2,1)S(1)} %all_to_all.30.refs_4_), channel_id=1, source_target_pairs={{1,2},{2,1},{3,4},{4,3},{5,6},{6,5},{7,8},{8,7},{9,10},{10,9},{11,... | collective-permute-start | bytes 393224 | tf_op jit(solution)/shard_map/ppermute | solution.py:291
  59.5 1.9 %collective-permute-start = (bf16[16,32,128]{2,1,0:T(8,128)(2,1)S(1)}, bf16[16,32,128]{2,1,0:T(8,128)(2,1)}, u32[]{:S(2)}, u32[]{:S(2)}) collective-permute-start(bf16[16,32,128]{2,1,0:T(8,128)(2,1)S(1)} %all_to_all.30.refs_4_), channel_id=1, source_target_pairs={{0,1},{1,0},{2,3},{3,2},{4,5},{5,4},{6,7},{7,6},{8,9},{9,8},{10,11... | collective-permute-start | bytes 393224 | tf_op jit(solution)/shard_map/ppermute | solution.py:290
  61.5 0.9 copy-done.7
  62.6 4.8 %all-to-all-done.2.whole_ref.refs_7_ = bf16[32,32,128]{2,1,0:T(8,128)(2,1)S(1)} async-done(((bf16[32,32,128]{2,1,0:T(8,128)(2,1)}), bf16[32,32,128]{2,1,0:T(8,128)(2,1)S(1)}, u32[]{:S(2)}, u32[]{:S(2)}) %all-to-all-start.2) | async-done | bytes 262176 | tf_op jit(solution)/shard_map/all_to_all | solution.py:280
  67.4 0.8 copy-done.21
  68.1 0.8 copy-done.23
  68.9 1.5 %shard_map.117.refs_11_ = bf16[1536,256]{1,0:T(8,128)(2,1)S(1)} custom-call(s32[1]{0:T(128)} %bitcast.1.mer_ref.refs_1_, bf16[32,32,128]{2,1,0:T(8,128)(2,1)S(1)} %all-to-all-done.2.whole_ref.refs_7_, f32[64,64]{1,0:T(8,128)S(1)} %copy-done.21, f32[64,64]{1,0:T(8,128)S(1)} %copy-done.23), custom_call_target="tpu_custom_call" | custom-call | tf_op jit(solution)/shard_map/pallas_call | solution.py:245
  70.5 1.2 copy-done.2
  71.7 0.9 copy-done.8
  72.6 0.9 copy-done.15
  74.8 3.3 %shard_map.118 = (f32[6,8,512]{2,1,0:T(8,128)S(1)}, bf16[16,16,128]{2,1,0:T(8,128)(2,1)S(1)}, bf16[32,16,128]{2,1,0:T(8,128)(2,1)S(1)}, f32[16,128]{1,0:T(8,128)S(1)}) custom-call(s32[1]{0:T(128)} %bitcast.refs_0_, s32[1]{0:T(128)} %bitcast.1.mer_ref.refs_1_, f32[6,8,512]{2,1,0:T(8,128)S(1)} %bitcast.9, f32[48,512]{1,0:T(8,128)S(1)} %copy-done.15, ...), custom_call_target="tpu_custom_call" | custom-call | tf_op jit(solution)/shard_map/pallas_call | solution.py:245
  78.1 11.9 %all_to_all.31.moved_ref = bf16[16,16,128]{2,1,0:T(8,128)(2,1)S(1)} all-to-all(bf16[16,16,128]{2,1,0:T(8,128)(2,1)S(1)} %get-tuple-element.21), channel_id=1, replica_groups=mesh['mode'=16,'mer'=32] {'mode'}, dimensions={0} | all-to-all | bytes 131072 | tf_op jit(solution)/shard_map/all_to_all | solution.py:286
  90.5 12.1 %all_to_all.32.refs_4_ = bf16[16,32,128]{2,1,0:T(8,128)(2,1)S(1)} all-to-all(bf16[16,32,128]{2,1,0:T(8,128)(2,1)S(1)} %shard_map.120), channel_id=1, replica_groups=mesh['mode'=16,'mer'=32] {'mode'}, dimensions={0} | all-to-all | bytes 262144 | tf_op jit(solution)/shard_map/all_to_all | solution.py:288
  102.5 7.7 %all-to-all-start.5 = ((bf16[32,16,128]{2,1,0:T(8,128)(2,1)}), bf16[32,16,128]{2,1,0:T(8,128)(2,1)S(1)}, u32[]{:S(2)}, u32[]{:S(2)}) async-start(bf16[32,16,128]{2,1,0:T(8,128)(2,1)} %copy-done.19), calls=%async_computation.5 | async-start | bytes 262144 | tf_op jit(solution)/shard_map/all_to_all | solution.py:280
  110.3 3.5 %collective-permute-start.3 = (bf16[16,32,128]{2,1,0:T(8,128)(2,1)S(1)}, bf16[16,32,128]{2,1,0:T(8,128)(2,1)}, u32[]{:S(2)}, u32[]{:S(2)}) collective-permute-start(bf16[16,32,128]{2,1,0:T(8,128)(2,1)S(1)} %all_to_all.32.refs_4_), channel_id=1, source_target_pairs={{1,2},{2,1},{3,4},{4,3},{5,6},{6,5},{7,8},{8,7},{9,10},{10,9},{11,... | collective-permute-start | bytes 393224 | tf_op jit(solution)/shard_map/ppermute | solution.py:291
  113.8 1.9 %collective-permute-start.2 = (bf16[16,32,128]{2,1,0:T(8,128)(2,1)S(1)}, bf16[16,32,128]{2,1,0:T(8,128)(2,1)}, u32[]{:S(2)}, u32[]{:S(2)}) collective-permute-start(bf16[16,32,128]{2,1,0:T(8,128)(2,1)S(1)} %all_to_all.32.refs_4_), channel_id=1, source_target_pairs={{0,1},{1,0},{2,3},{3,2},{4,5},{5,4},{6,7},{7,6},{8,9},{9,8},{10,11... | collective-permute-start | bytes 393224 | tf_op jit(solution)/shard_map/ppermute | solution.py:290
  115.8 1.0 copy-done.5
  117.0 2.8 %all-to-all-done.5.refs_7_ = bf16[32,16,128]{2,1,0:T(8,128)(2,1)S(1)} async-done(((bf16[32,16,128]{2,1,0:T(8,128)(2,1)}), bf16[32,16,128]{2,1,0:T(8,128)(2,1)S(1)}, u32[]{:S(2)}, u32[]{:S(2)}) %all-to-all-start.5) | async-done | bytes 131104 | tf_op jit(solution)/shard_map/all_to_all | solution.py:280
  119.8 1.2 copy-done.3
  121.0 3.7 %shard_map.121 = (f32[6,8,512]{2,1,0:T(8,128)}, f32[2,8,2,64]{3,2,1,0:T(2,128)}) custom-call(s32[1]{0:T(128)} %bitcast.refs_0_, s32[1]{0:T(128)} %bitcast.1.mer_ref.refs_1_, f32[6,8,512]{2,1,0:T(8,128)S(1)} %get-tuple-element.20.field_ref.refs_2_, f32[48,512]{1,0:T(8,128)S(1)} %shard_map.119.refs_3_, bf16[16,32,128]{2,1,0:T(8,128)(2,1)S(1)} %all_to_all.32.refs_4_, ...), custom_call_target="tpu_custom_call" | custom-call | tf_op jit(solution)/shard_map/pallas_call | solution.py:245
  (58 shorter events, 6.2 us)
Async XLA Ops:
  0.6 69.8 %copy-start = (bf16[8,64,2048]{2,1,0:T(8,128)(2,1)S(1)}, bf16[8,64,2048]{2,1,0:T(8,128)(2,1)}, u32[]{:S(2)}) copy-start(bf16[8,64,2048]{2,1,0:T(8,128)(2,1)} %refs_12_.3) | copy-start | bytes 6291460
  0.6 1.0 copy-start.6
  4.5 22.4 %all-to-all-start = ((bf16[16,16,128]{2,1,0:T(8,128)(2,1)}), bf16[16,16,128]{2,1,0:T(8,128)(2,1)S(1)}, u32[]{:S(2)}, u32[]{:S(2)}) async-start(bf16[16,16,128]{2,1,0:T(8,128)(2,1)} %get-tuple-element.15), calls=%async_computation | async-start | bytes 131072 | tf_op jit(solution)/shard_map/all_to_all | solution.py:286
  17.9 0.8 copy-start.20
  18.7 0.8 copy-start.22
  19.4 0.8 copy-start.24
  23.7 1.0 copy-start.1
  24.7 37.9 %copy-start.4 = (bf16[512,512]{1,0:T(8,128)(2,1)}, bf16[512,512]{1,0:T(8,128)(2,1)S(1)}, u32[]{:S(2)}) copy-start(bf16[512,512]{1,0:T(8,128)(2,1)S(1)} %get-tuple-element.14.s_ref) | copy-start | bytes 1572868
  24.7 37.9 %copy-start.16 = (bf16[256,128]{1,0:T(8,128)(2,1)}, bf16[256,128]{1,0:T(8,128)(2,1)S(1)}, u32[]{:S(2)}) copy-start(bf16[256,128]{1,0:T(8,128)(2,1)S(1)} %get-tuple-element.17.vb_ref) | copy-start | bytes 196612
  26.9 0.9 copy-start.10
  27.8 0.9 copy-start.12
  45.3 22.1 %all-to-all-start.2 = ((bf16[32,32,128]{2,1,0:T(8,128)(2,1)}), bf16[32,32,128]{2,1,0:T(8,128)(2,1)S(1)}, u32[]{:S(2)}, u32[]{:S(2)}) async-start(bf16[32,32,128]{2,1,0:T(8,128)(2,1)} %copy-done.18), calls=%async_computation.2 | async-start | bytes 524288 | tf_op jit(solution)/shard_map/all_to_all | solution.py:280
  56.0 14.5 %collective-permute-start.1 = (bf16[16,32,128]{2,1,0:T(8,128)(2,1)S(1)}, bf16[16,32,128]{2,1,0:T(8,128)(2,1)}, u32[]{:S(2)}, u32[]{:S(2)}) collective-permute-start(bf16[16,32,128]{2,1,0:T(8,128)(2,1)S(1)} %all_to_all.30.refs_4_), channel_id=1, source_target_pairs={{1,2},{2,1},{3,4},{4,3},{5,6},{6,5},{7,8},{8,7},{9,10},{10,9},{11,... | collective-permute-start | bytes 393224 | tf_op jit(solution)/shard_map/ppermute | solution.py:291
  59.5 10.9 %collective-permute-start = (bf16[16,32,128]{2,1,0:T(8,128)(2,1)S(1)}, bf16[16,32,128]{2,1,0:T(8,128)(2,1)}, u32[]{:S(2)}, u32[]{:S(2)}) collective-permute-start(bf16[16,32,128]{2,1,0:T(8,128)(2,1)S(1)} %all_to_all.30.refs_4_), channel_id=1, source_target_pairs={{0,1},{1,0},{2,3},{3,2},{4,5},{5,4},{6,7},{7,6},{8,9},{9,8},{10,11... | collective-permute-start | bytes 393224 | tf_op jit(solution)/shard_map/ppermute | solution.py:290
  61.4 0.9 copy-start.7
  62.6 7.9 %copy-start.14 = (f32[48,512]{1,0:T(8,128)}, f32[48,512]{1,0:T(8,128)S(1)}, u32[]{:S(2)}) copy-start(f32[48,512]{1,0:T(8,128)S(1)} %shard_map.114.refs_3_) | copy-start | bytes 294916
  67.3 0.8 copy-start.21
  70.4 1.2 copy-start.2
  71.7 0.9 copy-start.8
  72.6 0.9 copy-start.15
  74.8 15.2 %copy-start.11 = (bf16[256,256]{1,0:T(8,128)(2,1)S(1)}, bf16[256,256]{1,0:T(8,128)(2,1)}, u32[]{:S(2)}) copy-start(bf16[256,256]{1,0:T(8,128)(2,1)} %constant.14.clone.inv_ref) | copy-start | bytes 393220
  74.8 15.2 %copy-start.13 = (bf16[256,256]{1,0:T(8,128)(2,1)S(1)}, bf16[256,256]{1,0:T(8,128)(2,1)}, u32[]{:S(2)}) copy-start(bf16[256,256]{1,0:T(8,128)(2,1)} %constant.13.clone.fwd_ref) | copy-start | bytes 393220
  74.8 15.2 %copy-start.17 = (bf16[256,128]{1,0:T(8,128)(2,1)S(1)}, bf16[256,128]{1,0:T(8,128)(2,1)}, u32[]{:S(2)}) copy-start(bf16[256,128]{1,0:T(8,128)(2,1)} %copy-done.16) | copy-start | bytes 196612
  74.8 45.0 %copy-start.9 = (f32[8,6,512]{2,0,1:T(8,128)S(1)}, f32[8,6,512]{2,0,1:T(8,128)}, u32[]{:S(2)}) copy-start(f32[8,6,512]{2,0,1:T(8,128)} %param.10) | copy-start | bytes 294916
  74.8 45.0 %copy-start.28 = (f32[512]{0:T(512)S(1)}, f32[512]{0:T(512)}, u32[]{:S(2)}) copy-start(f32[512]{0:T(512)} %param.14) | copy-start | bytes 6148
  74.8 45.0 %copy-start.31 = (s32[64]{0:T(128)S(1)}, s32[64]{0:T(128)}, u32[]{:S(2)}) copy-start(s32[64]{0:T(128)} %param.16) | copy-start | bytes 772
  78.1 24.4 %copy-start.19 = (bf16[32,16,128]{2,1,0:T(8,128)(2,1)}, bf16[32,16,128]{2,1,0:T(8,128)(2,1)S(1)}, u32[]{:S(2)}) copy-start(bf16[32,16,128]{2,1,0:T(8,128)(2,1)S(1)} %get-tuple-element.22) | copy-start | bytes 393220
  102.5 17.2 %all-to-all-start.5 = ((bf16[32,16,128]{2,1,0:T(8,128)(2,1)}), bf16[32,16,128]{2,1,0:T(8,128)(2,1)S(1)}, u32[]{:S(2)}, u32[]{:S(2)}) async-start(bf16[32,16,128]{2,1,0:T(8,128)(2,1)} %copy-done.19), calls=%async_computation.5 | async-start | bytes 262144 | tf_op jit(solution)/shard_map/all_to_all | solution.py:280
  110.3 9.5 %collective-permute-start.3 = (bf16[16,32,128]{2,1,0:T(8,128)(2,1)S(1)}, bf16[16,32,128]{2,1,0:T(8,128)(2,1)}, u32[]{:S(2)}, u32[]{:S(2)}) collective-permute-start(bf16[16,32,128]{2,1,0:T(8,128)(2,1)S(1)} %all_to_all.32.refs_4_), channel_id=1, source_target_pairs={{1,2},{2,1},{3,4},{4,3},{5,6},{6,5},{7,8},{8,7},{9,10},{10,9},{11,... | collective-permute-start | bytes 393224 | tf_op jit(solution)/shard_map/ppermute | solution.py:291
  113.8 5.9 %collective-permute-start.2 = (bf16[16,32,128]{2,1,0:T(8,128)(2,1)S(1)}, bf16[16,32,128]{2,1,0:T(8,128)(2,1)}, u32[]{:S(2)}, u32[]{:S(2)}) collective-permute-start(bf16[16,32,128]{2,1,0:T(8,128)(2,1)S(1)} %all_to_all.32.refs_4_), channel_id=1, source_target_pairs={{0,1},{1,0},{2,3},{3,2},{4,5},{5,4},{6,7},{7,6},{8,9},{9,8},{10,11... | collective-permute-start | bytes 393224 | tf_op jit(solution)/shard_map/ppermute | solution.py:290
  115.8 1.0 copy-start.5
  119.8 1.2 copy-start.3
  (7 other events, 4.8 us)

commit v3 on v2

v3 whole, which is shorter than its diff:
```python
import numpy as np
import jax
import jax.numpy as jnp
from jax import lax
from jax.experimental import pallas as pl
from jax.experimental.pallas import tpu as pltpu
from jax.sharding import PartitionSpec as P


BF = jnp.bfloat16
F32 = jnp.float32


def nt(a, b):
    return lax.dot_general(a, b, (((1,), (1,)), ((), ())), preferred_element_type=F32)


def nn(a, b):
    return jnp.dot(a, b, preferred_element_type=F32)


def tables(modes, nphi, mode_dev):
    mode = np.arange(modes).reshape(-1, 1, mode_dev)
    k = np.arange(nphi).reshape(-1, 1, 1, 1)
    angle = 2.0 * np.pi * ((mode[None] * k) % nphi) / nphi
    fwd = np.concatenate([np.cos(angle), -np.sin(angle)], 2).reshape(nphi, 2 * modes)
    return fwd.astype(BF), (fwd.T / nphi).astype(BF)


def lane_group(shape):
    return lax.broadcasted_iota(jnp.int32, shape, len(shape) - 1) // 32


def pick(group, parts):
    out = parts[0]
    for g, part in enumerate(parts[1:], 1):
        out = jnp.where(group == g, part, out)
    return out


def shift(x, groups):
    return x if groups % 4 == 0 else pltpu.roll(x, 32 * (groups % 4), 1)


def pack(rows, out_ref):
    group = lane_group((8, 128))
    for v in range(4):
        tiles = {cp: r[:, 128 * v : 128 * v + 128] for cp, r in rows.items()}
        for q in range(4):
            halves = [
                pick(group, [shift(tiles[c % 3, p], c - q) for c in range(4)]) for p in range(2)
            ]
            out_ref[4 * v + q] = jnp.concatenate(halves, 0).astype(BF)


def unpack(tile, slots):
    group = lane_group((16, 128))
    cols = []
    for v in range(slots // 4):
        tiles = [tile(4 * v + q).astype(F32) for q in range(4)]
        cols.append(
            jnp.concatenate(
                [pick(group, [shift(tiles[q], q - c) for q in range(4)]) for c in range(3)], 0
            ).astype(BF)
        )
    return jnp.concatenate(cols, 1)


def wall_onehot(wall_ref, mer):
    twice = jnp.concatenate([wall_ref[...], wall_ref[...]], 1)
    nodes = lax.broadcasted_iota(jnp.int32, (512, 128), 0)
    half = lax.broadcasted_iota(jnp.int32, (512, 128), 1) // 64
    return jnp.where(half == mer % 2, (nodes == twice).astype(F32), 0.0).astype(BF)


def two_by_two(conn_ref):
    return jnp.concatenate([conn_ref[pl.ds(0, 8, 2), :], conn_ref[pl.ds(1, 8, 2), :]], 1)


def open_kernel(mer_ref, field, wall, conn, pack_ref, out_ref):
    onehot = wall_onehot(wall(), mer_ref[0])
    conn = two_by_two(conn())
    field_ref = field()
    pack({(c, p): field_ref[3 * p + c] for c in range(3) for p in range(2)}, pack_ref)
    last = jnp.concatenate([field_ref[2], field_ref[5]], 0).astype(BF)
    tr = nn(last, onehot)
    parts = [tr, (conn // 32).astype(F32), (conn % 32).astype(F32)]
    parts = jnp.concatenate(parts, 0).astype(BF)
    for j in range(out_ref.shape[0]):
        out_ref[j] = parts


def gate_kernel(packed_ref, whole_ref, near_ref, out_ref):
    out_ref[...] = packed_ref[...]


def element_blocks(ref, sign):
    row = lax.broadcasted_iota(jnp.int32, (256, 64), 0)
    col = lax.broadcasted_iota(jnp.int32, (256, 64), 1)
    spread = (row % 64 == col).astype(F32).astype(BF)
    near = lax.broadcasted_iota(jnp.int32, (256, 256), 0) // 64
    same = near == lax.broadcasted_iota(jnp.int32, (256, 256), 1) // 64
    once = nt(spread, ref[...].astype(BF)).astype(BF)
    return jnp.where(same, sign * nt(once, spread), 0.0).astype(BF)


def operators(conn, first, width, stiff_ref, curl_ref, tall_ref, work_ref):
    across = conn.T
    nodes = lax.broadcasted_iota(jnp.int32, (768, 128), 0).astype(F32)
    lanes = lax.broadcasted_iota(jnp.int32, (128, width), 1).astype(F32) + first
    mats = [element_blocks(stiff_ref, -1.0), element_blocks(curl_ref, 1.0)]
    for t in range(8):
        tall_ref[:, 128 * t : 128 * t + 128] = (nodes == conn[t : t + 1]).astype(F32).astype(BF)
    for u in range(4):
        picks = [
            (lanes == across[:, t : t + 1]).astype(F32).astype(BF) for t in (2 * u, 2 * u + 1)
        ]
        picks = jnp.concatenate(picks, 0)
        for k, mat in enumerate(mats):
            work_ref[k, 256 * u : 256 * u + 256] = nn(mat, picks).astype(BF)
    return nn(tall_ref[...], work_ref[0]), nn(tall_ref[...], work_ref[1])


def own_kernel(vel, stiff, curl, conn, fwd, inv, *refs):
    va_ref, vb_ref, fwd_ref, inv_ref, near_out, near_ref, tall_ref, work_ref, sem = refs
    conn = two_by_two(conn()).astype(F32)
    s, c = operators(conn, 0.0, 512, stiff(), curl(), tall_ref, work_ref)
    near_ref[:768] = c.astype(BF)
    near_ref[768:] = s.astype(BF)
    copy = pltpu.make_async_copy(near_ref, near_out, sem)
    copy.start()
    vel_ref = vel()
    vel = [vel_ref[c].astype(F32) for c in range(3)]
    zero = jnp.zeros_like(vel[0])
    va_ref[...] = jnp.concatenate([vel[0], vel[1], vel[2], zero], 0).T.astype(BF)
    vb_ref[...] = jnp.concatenate([vel[1], vel[2], vel[0], zero], 0).T.astype(BF)
    fwd_ref[...] = fwd()[...]
    inv_ref[...] = inv()[...]
    copy.wait()


def far_kernel(mer_ref, whole_ref, stiff, curl, far_out, far_ref, tall_ref, work_ref, sem):
    code = whole_ref[jnp.maximum(mer_ref[0] - 1, 0)].astype(F32)
    conn = 32.0 * code[16:24] + code[24:32]
    s, c = operators(conn, 512.0, 256, stiff(), curl(), tall_ref, work_ref)
    there = jnp.where(mer_ref[0] > 0, 1.0, 0.0)
    far_ref[:768] = (c * there).astype(BF)
    far_ref[768:] = (s * there).astype(BF)
    copy = pltpu.make_async_copy(far_ref, far_out, sem)
    copy.start()
    copy.wait()


def induce_kernel(moved_ref, va_ref, vb_ref, fwd_ref, inv_ref, far_ref, out_ref):
    moved = moved_ref[...]
    rows = moved.reshape(256, 128)
    turned = pltpu.roll(rows.astype(F32), 96, 1).astype(BF)
    here = nn(fwd_ref[...], rows)
    after = nn(fwd_ref[...], turned)
    cross = va_ref[...].astype(F32) * after - vb_ref[...].astype(F32) * here
    back = nn(inv_ref[...], cross.astype(BF))
    out_ref[:, :16] = back.astype(BF).reshape(16, 16, 128)
    out_ref[:, 16:] = moved


ORDER = [3 * p + c for c in range(3) for p in range(2)]


def rows_of(field):
    field_ref = field() if callable(field) else field
    return jnp.concatenate([field_ref[s] for s in ORDER], 0)


def operator_kernel(mer_ref, now, emf_ref, pa_ref, pb_ref, near, far, out_ref):
    odd = (jnp.zeros((16, 128), jnp.int32) + mer_ref[0] % 2) == 1

    def before(part):
        rows = slice(16 * part, 16 * part + 16)
        return lambda s: jnp.where(odd, pa_ref[s, rows].astype(F32), pb_ref[s, rows].astype(F32))

    def behind(part):
        rows = slice(16 * part, 16 * part + 16)
        return lambda s: jnp.where(odd, pb_ref[s, rows].astype(F32), pa_ref[s, rows].astype(F32))

    own = unpack(lambda s: emf_ref[s, :16], 16)
    e_next, f_next = unpack(behind(0), 8), unpack(behind(1), 8)
    e_prev, f_prev = unpack(before(0), 16), unpack(before(1), 16)
    field = rows_of(now).astype(BF)
    total = nn(jnp.concatenate([own, e_next, field, f_next], 1), near()[...])
    low = nn(jnp.concatenate([e_prev, own[:, :256], f_prev, field[:, :256]], 1), far()[...])
    out_ref[...] = jnp.concatenate([total[:, :256] + low, total[:, 256:]], 1)


def finish(mode_ref, mer_ref, now, total_ref, whole_ref, wall, mass, dtn):
    onehot = wall_onehot(wall(), mer_ref[0])
    field = rows_of(now)
    number = lax.broadcasted_iota(jnp.int32, (48, 512), 0) % 8 + 8 * mode_ref[0]
    coef = (number.astype(F32) / 128.0) ** 2
    whole = jnp.concatenate([whole_ref[2 * a, :16] + whole_ref[2 * a + 1, :16] for a in range(16)], 1)
    weight = 1.0 / mass()[...]
    every = nt(whole, dtn()[...].reshape(512, 2048))
    mine = lax.broadcasted_iota(jnp.int32, (16, 512), 0) % 8
    every = jnp.where(mine == lax.broadcasted_iota(jnp.int32, (16, 512), 1) // 64, every, 0.0)
    flux = every[:, :128] + every[:, 128:256] + every[:, 256:384] + every[:, 384:]
    flux = flux + pltpu.roll(flux, 64, 1)
    upper = flux.astype(BF)
    added = nt(upper, onehot) + nt((flux - upper.astype(F32)).astype(BF), onehot)
    total = total_ref[...]
    total = jnp.concatenate([total[:32], total[32:] - 0.5 * added], 0)
    rate = total * weight - 4.0 * coef * field
    return rate, field, flux, onehot


def first_kernel(*refs):
    sect_ref, pack_ref, trace_ref, flux_ref = refs[8:]
    rate, field, flux, onehot = finish(*refs[:8])
    sect = field + 0.2 * rate
    flux_ref[...] = flux
    rows = {(c, p): sect[16 * c + 8 * p : 16 * c + 8 * p + 8] for c in range(3) for p in range(2)}
    for (c, p), r in rows.items():
        sect_ref[3 * p + c] = r
    pack(rows, pack_ref)
    tr = nn(sect[32:].astype(BF), onehot).astype(BF)
    for j in range(trace_ref.shape[0]):
        trace_ref[j] = tr


def second_kernel(*refs):
    start, first_flux_ref, out_ref, flux_ref = refs[8:]
    rate, sect, flux, onehot = finish(*refs[:8])
    start_ref = start()
    for c in range(3):
        for p in range(2):
            at = slice(16 * c + 8 * p, 16 * c + 8 * p + 8)
            out_ref[3 * p + c] = 0.5 * (start_ref[3 * p + c] + sect[at] + 0.2 * rate[at])
    for p in range(2):
        flux_ref[0, :, p, :] = first_flux_ref[8 * p : 8 * p + 8, :64]
        flux_ref[1, :, p, :] = flux[8 * p : 8 * p + 8, :64]


def call(kernel, out, where, args, scratch=(), limit=16):
    count = len(where)
    brought = [a for a, k in zip(args, where, strict=True) if k == "c"]

    def run(*refs):
        inner, sems, bufs = refs, None, []
        if brought:
            inner, sems = refs[: -len(brought) - 1], refs[-len(brought) - 1]
            bufs = refs[-len(brought) :]
        near, copies = [], []
        for ref, k in zip(inner[:count], where, strict=True):
            if k == "c":
                n = len(copies)
                copies.append(pltpu.make_async_copy(ref, bufs[n], sems.at[n]))
                copies[n].start()
                near.append(later(copies[n], bufs[n]))
            else:
                near.append(ref)
        kernel(*near, *inner[count:])

    spaces = {"s": pltpu.SMEM, "v": pltpu.VMEM, "c": pltpu.HBM, "h": pltpu.HBM}
    extra = [pltpu.SemaphoreType.DMA((len(brought),))] if brought else []
    extra += [pltpu.VMEM(a.shape, a.dtype) for a in brought]
    return pl.pallas_call(
        run,
        out_shape=[space(s, d) if space else jax.ShapeDtypeStruct(s, d) for s, d, space in out],
        in_specs=[pl.BlockSpec(memory_space=spaces[k]) for k in where],
        out_specs=[pl.BlockSpec(memory_space=space or pltpu.VMEM) for _, _, space in out],
        scratch_shapes=[*scratch, *extra],
        compiler_params=pltpu.CompilerParams(vmem_limit_bytes=limit * 2**20),
    )(
        *[
            a if k == "s" else pltpu.with_memory_space_constraint(a, spaces[k])
            for k, a in zip(where, args, strict=True)
        ]
    )


def later(copy, buf):
    arrived = []

    def get():
        if not arrived:
            copy.wait()
            arrived.append(True)
        return buf

    return get


def body(field, velocity, stiffness, curl_matrix, mass, connect, wall_index, dtn):
    fwd, inv = tables(128, 256, 8)
    near_space, far_space = pltpu.VMEM, pltpu.HBM
    spots = lax.axis_size("mer")
    mer = lax.axis_index("mer").astype(jnp.int32).reshape(1)
    mode = lax.axis_index("mode").astype(jnp.int32).reshape(1)
    start = jnp.transpose(field, (1, 0, 2))
    wall = wall_index.reshape(1, 64)
    row = mass.reshape(1, 512)
    chunk = ((16, 16, 128), BF, near_space)

    def works(rows, width):
        return [
            pltpu.VMEM((rows, width), BF),
            pltpu.VMEM((768, 1024), BF),
            pltpu.VMEM((2, 1024, width), BF),
            pltpu.SemaphoreType.DMA,
        ]

    packed, trace = call(
        open_kernel, [chunk, ((spots, 32, 128), BF, near_space)], "sccc", (mer, start, wall, connect)
    )
    table = [((256, 128), BF, near_space)] * 2 + [((256, 256), BF, near_space)] * 2
    *table, near = call(
        own_kernel,
        table + [((1536, 512), BF, far_space)],
        "cccccc",
        (jnp.transpose(velocity, (0, 2, 1)), stiffness, curl_matrix, connect, fwd, inv),
        works(1536, 512),
        32,
    )

    twins = [(i, i ^ 1) for i in range(spots)]
    others = [(i, ((i + 1) ^ 1) - 1) for i in range(1, spots - 1)]

    def section(now, packed, whole, far, last):
        moved = lax.all_to_all(packed, "mode", 0, 0, tiled=True)
        (back,) = call(
            induce_kernel, [((16, 32, 128), BF, near_space)], "vvvvvh", (moved, *table, far)
        )
        emf = lax.all_to_all(back, "mode", 0, 0, tiled=True)
        e_twin = lax.ppermute(emf, "mer", twins)
        e_other = lax.ppermute(emf, "mer", others)
        held = "c" if last is None else "v"
        if last is not None:
            whole = lax.all_to_all(whole, "mer", 0, 0, tiled=True)
        (total,) = call(
            operator_kernel,
            [((48, 512), F32, near_space)],
            "s" + held + "vvvcc",
            (mer, now, emf, e_twin, e_other, near, far),
        )
        args = (mode, mer, now, total, whole, wall, row, dtn)
        kinds = "ss" + held + "vvccc"
        if last is None:
            out = [((6, 8, 512), F32, near_space), chunk]
            out += [((spots, 16, 128), BF, near_space), ((16, 128), F32, near_space)]
            return call(first_kernel, out, kinds, args)
        out = [((6, 8, 512), F32, None), ((2, 8, 2, 64), F32, None)]
        return call(second_kernel, out, kinds + "cv", (*args, *last))

    whole = lax.all_to_all(trace, "mer", 0, 0, tiled=True)
    (far,) = call(
        far_kernel,
        [((1536, 256), BF, far_space)],
        "svcc",
        (mer, whole, stiffness, curl_matrix),
        works(1536, 256),
        32,
    )
    (packed,) = call(gate_kernel, [chunk], "vvh", (packed, whole, near))
    sect, packed, trace, flux = section(start, packed, whole, far, None)
    done, fluxes = section(sect, packed, trace, far, (start, flux))
    return (jnp.transpose(done, (1, 0, 2)), fluxes)


def solution(mesh):
    placed = (
        P("mode", None, "mer"),
        P(None, None, ("mer", "mode")),
        P(),
        P(),
        P("mer"),
        P("mer", None),
        P("mer"),
        P("mode", "mer", None),
    )
    return jax.shard_map(
        body,
        mesh=mesh,
        in_specs=placed,
        out_specs=(P("mode", None, "mer"), P(None, "mode", None, "mer")),
        check_vma=False,
    )
```

time: 126 us -> 120 us (0.952)
  local copies, waits for them, and re-layouts: 17.9 us -> 0 us
  Pallas kernels: 13.3 us -> 22.6 us
  waiting for transfers between devices: 9.75 us -> 15.9 us
  blocking collectives: 40.1 us -> 36.2 us
    unnamed x64 -> x0, local copies, waits for them, and re-layouts: 17.9 us -> none
    pallas_call x9 -> x10, Pallas kernels: 13.3 us -> 22.6 us  [call(): pl.pallas_call(run, out_shape=[space(s, d) if space else jax.ShapeDtypeSt...]
    all_to_all x2, blocking collectives: 28.2 us -> 24.2 us  [section(): emf = lax.all_to_all(back, 'mode', 0, 0, tiled=True)]
    all_to_all x1, waiting for transfers between devices: 2.2 us -> 5.92 us  [section(): moved = lax.all_to_all(packed, 'mode', 0, 0, tiled=True)]
    ppermute x2, waiting for transfers between devices: 0.01 us -> 2.92 us  [section(): e_other = lax.ppermute(emf, 'mer', others)]
    ppermute x2, starting transfers between devices: 7.09 us -> 9.79 us  [section(): e_other = lax.ppermute(emf, 'mer', others)]
    all_to_all x1, starting transfers between devices: 13.4 us -> 11.7 us  [section(): moved = lax.all_to_all(packed, 'mode', 0, 0, tiled=True)]
  transfers between devices with their start and end apart: 7 -> 7, of which waited for: 3 -> 5; matrix products, arithmetic and copies ran while one was open for 0% -> 0% of each run, Pallas kernels for 4% -> 9%
where the time goes in v3:
time: 120 us; the launch traced here: 118 us
  starting transfers between devices  43 us (36%)
  blocking collectives  36.2 us (30%)
  Pallas kernels  22.6 us (19%)
  waiting for transfers between devices  15.9 us (13%)
    all_to_all x2, blocking collectives, section(): emf = lax.all_to_all(back, 'mode', 0, 0, tiled=True)  24.2 us
    pallas_call x10, Pallas kernels, call(): pl.pallas_call(run, out_shape=[space(s, d) if space else jax.ShapeDtypeSt...  22.6 us
    all_to_all x1, blocking collectives, section(): moved = lax.all_to_all(packed, 'mode', 0, 0, tiled=True)  11.9 us
    all_to_all x1, starting transfers between devices, section(): moved = lax.all_to_all(packed, 'mode', 0, 0, tiled=True)  11.7 us
    all_to_all x1, starting transfers between devices, body(): whole = lax.all_to_all(trace, 'mer', 0, 0, tiled=True)  10.6 us
    ppermute x2, starting transfers between devices, section(): e_other = lax.ppermute(emf, 'mer', others)  9.79 us
    all_to_all x1, starting transfers between devices, section(): whole = lax.all_to_all(whole, 'mer', 0, 0, tiled=True)  7.15 us
    all_to_all x1, waiting for transfers between devices, body(): whole = lax.all_to_all(trace, 'mer', 0, 0, tiled=True)  6.71 us
  transfers between devices with their start and end apart: 7, of which 5 were waited for; matrix products, arithmetic and copies ran while one was open for 0% of the time, Pallas kernels for 9%

profile of v3, /device:TPU:1, one launch (start us, length us, event | category | flops | bytes accessed | tf_op | source)
XLA Modules:
  0.0 118.5 jit_solution(17847138291073037627)
XLA Ops:
  0.6 1.8 %shard_map.113 = (bf16[16,16,128]{2,1,0:T(8,128)(2,1)S(1)}, bf16[32,32,128]{2,1,0:T(8,128)(2,1)}) custom-call(s32[1]{0:T(128)} %bitcast.1.refs_0_.refs_1_, f32[6,8,512]{2,1,0:T(8,128)} %bitcast.7, s32[1,64]{1,0:T(1,128)} %bitcast.14, s32[16,64]{1,0:T(8,128)} %refs_3_.4), custom_call_target="tpu_custom_call" | custom-call | tf_op jit(solution)/shard_map/pallas_call | solution.py:264
  2.4 10.6 %all-to-all-start = ((bf16[32,32,128]{2,1,0:T(8,128)(2,1)}), bf16[32,32,128]{2,1,0:T(8,128)(2,1)S(1)}, u32[]{:S(2)}, u32[]{:S(2)}) async-start(bf16[32,32,128]{2,1,0:T(8,128)(2,1)} %get-tuple-element.16), calls=%async_computation | async-start | bytes 524288 | tf_op jit(solution)/shard_map/all_to_all | solution.py:352
  13.0 4.7 %shard_map.114 = (bf16[256,128]{1,0:T(8,128)(2,1)S(1)}, bf16[256,128]{1,0:T(8,128)(2,1)S(1)}, bf16[256,256]{1,0:T(8,128)(2,1)S(1)}, bf16[256,256]{1,0:T(8,128)(2,1)S(1)}, bf16[1536,512]{1,0:T(8,128)(2,1)}) custom-call(bf16[3,32,256]{2,1,0:T(8,128)(2,1)} %bitcast.11, f32[64,64]{1,0:T(8,128)} %refs_2_.3, f32[64,64]{1,0:T(8,128)} %refs_3_.5, s32[16,64]{1,0:T(8,128)} %refs_3_.4, ...), custom_call_target="tpu_custom_call" | custom-call | tf_op jit(solution)/shard_map/pallas_call | solution.py:264
  17.7 6.7 %all-to-all-done.refs_1_.refs_4_ = bf16[32,32,128]{2,1,0:T(8,128)(2,1)S(1)} async-done(((bf16[32,32,128]{2,1,0:T(8,128)(2,1)}), bf16[32,32,128]{2,1,0:T(8,128)(2,1)S(1)}, u32[]{:S(2)}, u32[]{:S(2)}) %all-to-all-start) | async-done | bytes 262176 | tf_op jit(solution)/shard_map/all_to_all | solution.py:352
  24.4 0.6 shard_map.115
  25.1 11.7 %all-to-all-start.1 = ((bf16[16,16,128]{2,1,0:T(8,128)(2,1)}), bf16[16,16,128]{2,1,0:T(8,128)(2,1)S(1)}, u32[]{:S(2)}, u32[]{:S(2)}) async-start(bf16[16,16,128]{2,1,0:T(8,128)(2,1)} %shard_map.115), calls=%async_computation.1 | async-start | bytes 131072 | tf_op jit(solution)/shard_map/all_to_all | solution.py:327
  36.8 3.2 %shard_map.116.refs_5_.refs_6_ = bf16[1536,256]{1,0:T(8,128)(2,1)} custom-call(s32[1]{0:T(128)} %bitcast.1.refs_0_.refs_1_, bf16[32,32,128]{2,1,0:T(8,128)(2,1)S(1)} %all-to-all-done.refs_1_.refs_4_, f32[64,64]{1,0:T(8,128)} %refs_2_.3, f32[64,64]{1,0:T(8,128)} %refs_3_.5), custom_call_target="tpu_custom_call" | custom-call | tf_op jit(solution)/shard_map/pallas_call | solution.py:264
  40.0 5.9 %all-to-all-done.1.refs_0_ = bf16[16,16,128]{2,1,0:T(8,128)(2,1)S(1)} async-done(((bf16[16,16,128]{2,1,0:T(8,128)(2,1)}), bf16[16,16,128]{2,1,0:T(8,128)(2,1)S(1)}, u32[]{:S(2)}, u32[]{:S(2)}) %all-to-all-start.1) | async-done | bytes 65568 | tf_op jit(solution)/shard_map/all_to_all | solution.py:327
  45.9 0.5 shard_map.117
  46.4 12.3 %all_to_all.30.refs_2_ = bf16[16,32,128]{2,1,0:T(8,128)(2,1)S(1)} all-to-all(bf16[16,32,128]{2,1,0:T(8,128)(2,1)S(1)} %shard_map.117), channel_id=1, replica_groups=mesh['mode'=16,'mer'=32] {'mode'}, dimensions={0} | all-to-all | bytes 262144 | tf_op jit(solution)/shard_map/all_to_all | solution.py:331
  58.6 6.2 %collective-permute-start.1 = (bf16[16,32,128]{2,1,0:T(8,128)(2,1)S(1)}, bf16[16,32,128]{2,1,0:T(8,128)(2,1)S(1)}, u32[]{:S(2)}, u32[]{:S(2)}) collective-permute-start(bf16[16,32,128]{2,1,0:T(8,128)(2,1)S(1)} %all_to_all.30.refs_2_), channel_id=1, source_target_pairs={{1,2},{2,1},{3,4},{4,3},{5,6},{6,5},{7,8},{8,7},{9,10},{10,9},{11,... | collective-permute-start | bytes 393224 | tf_op jit(solution)/shard_map/ppermute | solution.py:333
  64.9 1.9 %collective-permute-start = (bf16[16,32,128]{2,1,0:T(8,128)(2,1)S(1)}, bf16[16,32,128]{2,1,0:T(8,128)(2,1)S(1)}, u32[]{:S(2)}, u32[]{:S(2)}) collective-permute-start(bf16[16,32,128]{2,1,0:T(8,128)(2,1)S(1)} %all_to_all.30.refs_2_), channel_id=1, source_target_pairs={{0,1},{1,0},{2,3},{3,2},{4,5},{5,4},{6,7},{7,6},{8,9},{9,8},{10,11... | collective-permute-start | bytes 393224 | tf_op jit(solution)/shard_map/ppermute | solution.py:332
  66.8 0.9 collective-permute-done.1.refs_4_
  67.7 0.4 collective-permute-done.refs_3_
  68.1 2.4 %shard_map.118.refs_3_ = f32[48,512]{1,0:T(8,128)S(1)} custom-call(s32[1]{0:T(128)} %bitcast.1.refs_0_.refs_1_, f32[6,8,512]{2,1,0:T(8,128)} %bitcast.8, bf16[16,32,128]{2,1,0:T(8,128)(2,1)S(1)} %all_to_all.30.refs_2_, bf16[16,32,128]{2,1,0:T(8,128)(2,1)S(1)} %collective-permute-done.refs_3_, bf16[16,32,128]{2,1,0:T(8,128)(2,1)S(1)} %collective-permute-done.1.refs_4_, ...), custom_call_target="tpu_custom_call" | custom-call | tf_op jit(solution)/shard_map/pallas_call | solution.py:264
  70.5 3.4 %shard_map.119 = (f32[6,8,512]{2,1,0:T(8,128)S(1)}, bf16[16,16,128]{2,1,0:T(8,128)(2,1)S(1)}, bf16[32,16,128]{2,1,0:T(8,128)(2,1)}, f32[16,128]{1,0:T(8,128)S(1)}) custom-call(s32[1]{0:T(128)} %bitcast.refs_0_, s32[1]{0:T(128)} %bitcast.1.refs_0_.refs_1_, f32[6,8,512]{2,1,0:T(8,128)} %bitcast.9, f32[48,512]{1,0:T(8,128)S(1)} %shard_map.118.refs_3_, ...), custom_call_target="tpu_custom_call" | custom-call | tf_op jit(solution)/shard_map/pallas_call | solution.py:264
  73.9 11.9 %all_to_all.31.refs_0_ = bf16[16,16,128]{2,1,0:T(8,128)(2,1)S(1)} all-to-all(bf16[16,16,128]{2,1,0:T(8,128)(2,1)S(1)} %get-tuple-element.23), channel_id=1, replica_groups=mesh['mode'=16,'mer'=32] {'mode'}, dimensions={0} | all-to-all | bytes 131072 | tf_op jit(solution)/shard_map/all_to_all | solution.py:327
  85.8 0.5 shard_map.120
  86.3 12.0 %all_to_all.32.refs_2_ = bf16[16,32,128]{2,1,0:T(8,128)(2,1)S(1)} all-to-all(bf16[16,32,128]{2,1,0:T(8,128)(2,1)S(1)} %shard_map.120), channel_id=1, replica_groups=mesh['mode'=16,'mer'=32] {'mode'}, dimensions={0} | all-to-all | bytes 262144 | tf_op jit(solution)/shard_map/all_to_all | solution.py:331
  98.3 7.1 %all-to-all-start.5 = ((bf16[32,16,128]{2,1,0:T(8,128)(2,1)}), bf16[32,16,128]{2,1,0:T(8,128)(2,1)S(1)}, u32[]{:S(2)}, u32[]{:S(2)}) async-start(bf16[32,16,128]{2,1,0:T(8,128)(2,1)} %get-tuple-element.24), calls=%async_computation.5 | async-start | bytes 262144 | tf_op jit(solution)/shard_map/all_to_all | solution.py:336
  105.4 3.5 %collective-permute-start.3 = (bf16[16,32,128]{2,1,0:T(8,128)(2,1)S(1)}, bf16[16,32,128]{2,1,0:T(8,128)(2,1)S(1)}, u32[]{:S(2)}, u32[]{:S(2)}) collective-permute-start(bf16[16,32,128]{2,1,0:T(8,128)(2,1)S(1)} %all_to_all.32.refs_2_), channel_id=1, source_target_pairs={{1,2},{2,1},{3,4},{4,3},{5,6},{6,5},{7,8},{8,7},{9,10},{10,9},{11,... | collective-permute-start | bytes 393224 | tf_op jit(solution)/shard_map/ppermute | solution.py:333
  109.0 1.9 %collective-permute-start.2 = (bf16[16,32,128]{2,1,0:T(8,128)(2,1)S(1)}, bf16[16,32,128]{2,1,0:T(8,128)(2,1)S(1)}, u32[]{:S(2)}, u32[]{:S(2)}) collective-permute-start(bf16[16,32,128]{2,1,0:T(8,128)(2,1)S(1)} %all_to_all.32.refs_2_), channel_id=1, source_target_pairs={{0,1},{1,0},{2,3},{3,2},{4,5},{5,4},{6,7},{7,6},{8,9},{9,8},{10,11... | collective-permute-start | bytes 393224 | tf_op jit(solution)/shard_map/ppermute | solution.py:332
  110.9 2.0 %collective-permute-done.3.refs_4_ = bf16[16,32,128]{2,1,0:T(8,128)(2,1)S(1)} collective-permute-done((bf16[16,32,128]{2,1,0:T(8,128)(2,1)S(1)}, bf16[16,32,128]{2,1,0:T(8,128)(2,1)S(1)}, u32[]{:S(2)}, u32[]{:S(2)}) %collective-permute-start.3) | collective-permute-done | bytes 131104 | tf_op jit(solution)/shard_map/ppermute | solution.py:333
  112.9 0.0 collective-permute-done.2.refs_3_
  112.9 2.3 %shard_map.121.refs_3_ = f32[48,512]{1,0:T(8,128)S(1)} custom-call(s32[1]{0:T(128)} %bitcast.1.refs_0_.refs_1_, f32[6,8,512]{2,1,0:T(8,128)S(1)} %get-tuple-element.22.refs_1_.refs_2_, bf16[16,32,128]{2,1,0:T(8,128)(2,1)S(1)} %all_to_all.32.refs_2_, bf16[16,32,128]{2,1,0:T(8,128)(2,1)S(1)} %collective-permute-done.2.refs_3_, ...), custom_call_target="tpu_custom_call" | custom-call | tf_op jit(solution)/shard_map/pallas_call | solution.py:264
  115.2 0.0 all-to-all-done.5.refs_4_
  115.3 3.2 %shard_map.122 = (f32[6,8,512]{2,1,0:T(8,128)}, f32[2,8,2,64]{3,2,1,0:T(2,128)}) custom-call(s32[1]{0:T(128)} %bitcast.refs_0_, s32[1]{0:T(128)} %bitcast.1.refs_0_.refs_1_, f32[6,8,512]{2,1,0:T(8,128)S(1)} %get-tuple-element.22.refs_1_.refs_2_, f32[48,512]{1,0:T(8,128)S(1)} %shard_map.121.refs_3_, bf16[32,16,128]{2,1,0:T(8,128)(2,1)S(1)} %all-to-all-done.5.refs_4_, ...), custom_call_target="tpu_custom_call" | custom-call | tf_op jit(solution)/shard_map/pallas_call | solution.py:264
Async XLA Ops:
  2.4 22.0 %all-to-all-start = ((bf16[32,32,128]{2,1,0:T(8,128)(2,1)}), bf16[32,32,128]{2,1,0:T(8,128)(2,1)S(1)}, u32[]{:S(2)}, u32[]{:S(2)}) async-start(bf16[32,32,128]{2,1,0:T(8,128)(2,1)} %get-tuple-element.16), calls=%async_computation | async-start | bytes 524288 | tf_op jit(solution)/shard_map/all_to_all | solution.py:352
  25.1 20.8 %all-to-all-start.1 = ((bf16[16,16,128]{2,1,0:T(8,128)(2,1)}), bf16[16,16,128]{2,1,0:T(8,128)(2,1)S(1)}, u32[]{:S(2)}, u32[]{:S(2)}) async-start(bf16[16,16,128]{2,1,0:T(8,128)(2,1)} %shard_map.115), calls=%async_computation.1 | async-start | bytes 131072 | tf_op jit(solution)/shard_map/all_to_all | solution.py:327
  58.6 9.1 %collective-permute-start.1 = (bf16[16,32,128]{2,1,0:T(8,128)(2,1)S(1)}, bf16[16,32,128]{2,1,0:T(8,128)(2,1)S(1)}, u32[]{:S(2)}, u32[]{:S(2)}) collective-permute-start(bf16[16,32,128]{2,1,0:T(8,128)(2,1)S(1)} %all_to_all.30.refs_2_), channel_id=1, source_target_pairs={{1,2},{2,1},{3,4},{4,3},{5,6},{6,5},{7,8},{8,7},{9,10},{10,9},{11,... | collective-permute-start | bytes 393224 | tf_op jit(solution)/shard_map/ppermute | solution.py:333
  64.9 3.2 %collective-permute-start = (bf16[16,32,128]{2,1,0:T(8,128)(2,1)S(1)}, bf16[16,32,128]{2,1,0:T(8,128)(2,1)S(1)}, u32[]{:S(2)}, u32[]{:S(2)}) collective-permute-start(bf16[16,32,128]{2,1,0:T(8,128)(2,1)S(1)} %all_to_all.30.refs_2_), channel_id=1, source_target_pairs={{0,1},{1,0},{2,3},{3,2},{4,5},{5,4},{6,7},{7,6},{8,9},{9,8},{10,11... | collective-permute-start | bytes 393224 | tf_op jit(solution)/shard_map/ppermute | solution.py:332
  98.3 17.0 %all-to-all-start.5 = ((bf16[32,16,128]{2,1,0:T(8,128)(2,1)}), bf16[32,16,128]{2,1,0:T(8,128)(2,1)S(1)}, u32[]{:S(2)}, u32[]{:S(2)}) async-start(bf16[32,16,128]{2,1,0:T(8,128)(2,1)} %get-tuple-element.24), calls=%async_computation.5 | async-start | bytes 262144 | tf_op jit(solution)/shard_map/all_to_all | solution.py:336
  105.4 7.5 %collective-permute-start.3 = (bf16[16,32,128]{2,1,0:T(8,128)(2,1)S(1)}, bf16[16,32,128]{2,1,0:T(8,128)(2,1)S(1)}, u32[]{:S(2)}, u32[]{:S(2)}) collective-permute-start(bf16[16,32,128]{2,1,0:T(8,128)(2,1)S(1)} %all_to_all.32.refs_2_), channel_id=1, source_target_pairs={{1,2},{2,1},{3,4},{4,3},{5,6},{6,5},{7,8},{8,7},{9,10},{10,9},{11,... | collective-permute-start | bytes 393224 | tf_op jit(solution)/shard_map/ppermute | solution.py:333
  109.0 3.9 %collective-permute-start.2 = (bf16[16,32,128]{2,1,0:T(8,128)(2,1)S(1)}, bf16[16,32,128]{2,1,0:T(8,128)(2,1)S(1)}, u32[]{:S(2)}, u32[]{:S(2)}) collective-permute-start(bf16[16,32,128]{2,1,0:T(8,128)(2,1)S(1)} %all_to_all.32.refs_2_), channel_id=1, source_target_pairs={{0,1},{1,0},{2,3},{3,2},{4,5},{5,4},{6,7},{7,6},{8,9},{9,8},{10,11... | collective-permute-start | bytes 393224 | tf_op jit(solution)/shard_map/ppermute | solution.py:332

commit v4 on v3

--- a/solution.py
+++ b/solution.py
@@ -77,21 +77,24 @@
     return jnp.concatenate([conn_ref[pl.ds(0, 8, 2), :], conn_ref[pl.ds(1, 8, 2), :]], 1)
 
 
-def open_kernel(mer_ref, field, wall, conn, pack_ref, out_ref):
+def open_kernel(mer_ref, field, wall, conn, vel, fwd, inv, pack_ref, out_ref, va_ref, vb_ref, fwd_ref, inv_ref):
     onehot = wall_onehot(wall(), mer_ref[0])
     conn = two_by_two(conn())
     field_ref = field()
     pack({(c, p): field_ref[3 * p + c] for c in range(3) for p in range(2)}, pack_ref)
+    vel_ref = vel()
+    vel = [vel_ref[c].astype(F32) for c in range(3)]
+    zero = jnp.zeros_like(vel[0])
+    va_ref[...] = jnp.concatenate([vel[0], vel[1], vel[2], zero], 0).T.astype(BF)
+    vb_ref[...] = jnp.concatenate([vel[1], vel[2], vel[0], zero], 0).T.astype(BF)
+    fwd_ref[...] = fwd()[...]
+    inv_ref[...] = inv()[...]
     last = jnp.concatenate([field_ref[2], field_ref[5]], 0).astype(BF)
     tr = nn(last, onehot)
     parts = [tr, (conn // 32).astype(F32), (conn % 32).astype(F32)]
     parts = jnp.concatenate(parts, 0).astype(BF)
     for j in range(out_ref.shape[0]):
         out_ref[j] = parts
-
-
-def gate_kernel(packed_ref, whole_ref, near_ref, out_ref):
-    out_ref[...] = packed_ref[...]
 
 
 def element_blocks(ref, sign):
@@ -121,37 +124,17 @@
     return nn(tall_ref[...], work_ref[0]), nn(tall_ref[...], work_ref[1])
 
 
-def own_kernel(vel, stiff, curl, conn, fwd, inv, *refs):
-    va_ref, vb_ref, fwd_ref, inv_ref, near_out, near_ref, tall_ref, work_ref, sem = refs
+def own_kernel(stiff, curl, conn, emf_ref, near_out, near_ref, tall_ref, work_ref, sem):
     conn = two_by_two(conn()).astype(F32)
     s, c = operators(conn, 0.0, 512, stiff(), curl(), tall_ref, work_ref)
     near_ref[:768] = c.astype(BF)
     near_ref[768:] = s.astype(BF)
     copy = pltpu.make_async_copy(near_ref, near_out, sem)
     copy.start()
-    vel_ref = vel()
-    vel = [vel_ref[c].astype(F32) for c in range(3)]
-    zero = jnp.zeros_like(vel[0])
-    va_ref[...] = jnp.concatenate([vel[0], vel[1], vel[2], zero], 0).T.astype(BF)
-    vb_ref[...] = jnp.concatenate([vel[1], vel[2], vel[0], zero], 0).T.astype(BF)
-    fwd_ref[...] = fwd()[...]
-    inv_ref[...] = inv()[...]
     copy.wait()
 
 
-def far_kernel(mer_ref, whole_ref, stiff, curl, far_out, far_ref, tall_ref, work_ref, sem):
-    code = whole_ref[jnp.maximum(mer_ref[0] - 1, 0)].astype(F32)
-    conn = 32.0 * code[16:24] + code[24:32]
-    s, c = operators(conn, 512.0, 256, stiff(), curl(), tall_ref, work_ref)
-    there = jnp.where(mer_ref[0] > 0, 1.0, 0.0)
-    far_ref[:768] = (c * there).astype(BF)
-    far_ref[768:] = (s * there).astype(BF)
-    copy = pltpu.make_async_copy(far_ref, far_out, sem)
-    copy.start()
-    copy.wait()
-
-
-def induce_kernel(moved_ref, va_ref, vb_ref, fwd_ref, inv_ref, far_ref, out_ref):
+def induce_kernel(moved_ref, va_ref, vb_ref, fwd_ref, inv_ref, out_ref):
     moved = moved_ref[...]
     rows = moved.reshape(256, 128)
     turned = pltpu.roll(rows.astype(F32), 96, 1).astype(BF)
@@ -171,7 +154,7 @@
     return jnp.concatenate([field_ref[s] for s in ORDER], 0)
 
 
-def operator_kernel(mer_ref, now, emf_ref, pa_ref, pb_ref, near, far, out_ref):
+def operator_rows(mer_ref, now, emf_ref, pa_ref, pb_ref, near, far):
     odd = (jnp.zeros((16, 128), jnp.int32) + mer_ref[0] % 2) == 1
 
     def before(part):
@@ -188,7 +171,25 @@
     field = rows_of(now).astype(BF)
     total = nn(jnp.concatenate([own, e_next, field, f_next], 1), near()[...])
     low = nn(jnp.concatenate([e_prev, own[:, :256], f_prev, field[:, :256]], 1), far()[...])
-    out_ref[...] = jnp.concatenate([total[:, :256] + low, total[:, 256:]], 1)
+    return jnp.concatenate([total[:, :256] + low, total[:, 256:]], 1)
+
+
+def first_operator_kernel(mer_ref, now, emf_ref, pa_ref, pb_ref, near, whole_ref, stiff, curl, *refs):
+    out_ref, far_out, far_ref, tall_ref, work_ref, sem = refs
+    code = whole_ref[jnp.maximum(mer_ref[0] - 1, 0)].astype(F32)
+    conn = 32.0 * code[16:24] + code[24:32]
+    s, c = operators(conn, 512.0, 256, stiff(), curl(), tall_ref, work_ref)
+    there = jnp.where(mer_ref[0] > 0, 1.0, 0.0)
+    far_ref[:768] = (c * there).astype(BF)
+    far_ref[768:] = (s * there).astype(BF)
+    copy = pltpu.make_async_copy(far_ref, far_out, sem)
+    copy.start()
+    out_ref[...] = operator_rows(mer_ref, now, emf_ref, pa_ref, pb_ref, near, lambda: far_ref)
+    copy.wait()
+
+
+def operator_kernel(mer_ref, now, emf_ref, pa_ref, pb_ref, near, far, out_ref):
+    out_ref[...] = operator_rows(mer_ref, now, emf_ref, pa_ref, pb_ref, near, far)
 
 
 def finish(mode_ref, mer_ref, now, total_ref, whole_ref, wall, mass, dtn):
@@ -198,7 +199,8 @@
     coef = (number.astype(F32) / 128.0) ** 2
     whole = jnp.concatenate([whole_ref[2 * a, :16] + whole_ref[2 * a + 1, :16] for a in range(16)], 1)
     weight = 1.0 / mass()[...]
-    every = nt(whole, dtn()[...].reshape(512, 2048))
+    every = [nt(whole, dtn(k)[2 * k : 2 * k + 2].reshape(128, 2048)) for k in range(4)]
+    every = jnp.concatenate(every, 1)
     mine = lax.broadcasted_iota(jnp.int32, (16, 512), 0) % 8
     every = jnp.where(mine == lax.broadcasted_iota(jnp.int32, (16, 512), 1) // 64, every, 0.0)
     flux = every[:, :128] + every[:, 128:256] + every[:, 256:384] + every[:, 384:]
@@ -240,27 +242,32 @@
 
 def call(kernel, out, where, args, scratch=(), limit=16):
     count = len(where)
-    brought = [a for a, k in zip(args, where, strict=True) if k == "c"]
+    brought = [(a, k) for a, k in zip(args, where, strict=True) if k in "cd"]
 
     def run(*refs):
         inner, sems, bufs = refs, None, []
         if brought:
             inner, sems = refs[: -len(brought) - 1], refs[-len(brought) - 1]
-            bufs = refs[-len(brought) :]
-        near, copies = [], []
+            bufs = list(refs[-len(brought) :])
+        near, used = [], 0
         for ref, k in zip(inner[:count], where, strict=True):
-            if k == "c":
-                n = len(copies)
-                copies.append(pltpu.make_async_copy(ref, bufs[n], sems.at[n]))
-                copies[n].start()
-                near.append(later(copies[n], bufs[n]))
-            else:
+            if k not in "cd":
                 near.append(ref)
+                continue
+            buf, copies = bufs.pop(0), []
+            for part in range(4 if k == "d" else 1):
+                piece = pl.ds(2 * part, 2) if k == "d" else Ellipsis
+                src, dst = (ref.at[piece], buf.at[piece]) if k == "d" else (ref, buf)
+                copies.append(pltpu.make_async_copy(src, dst, sems.at[used]))
+                copies[-1].start()
+                used += 1
+            near.append(later(copies, buf))
         kernel(*near, *inner[count:])
 
-    spaces = {"s": pltpu.SMEM, "v": pltpu.VMEM, "c": pltpu.HBM, "h": pltpu.HBM}
-    extra = [pltpu.SemaphoreType.DMA((len(brought),))] if brought else []
-    extra += [pltpu.VMEM(a.shape, a.dtype) for a in brought]
+    spaces = {"s": pltpu.SMEM, "v": pltpu.VMEM, "c": pltpu.HBM, "d": pltpu.HBM}
+    waits = sum(4 if k == "d" else 1 for _, k in brought)
+    extra = [pltpu.SemaphoreType.DMA((waits,))] if brought else []
+    extra += [pltpu.VMEM(a.shape, a.dtype) for a, _ in brought]
     return pl.pallas_call(
         run,
         out_shape=[space(s, d) if space else jax.ShapeDtypeStruct(s, d) for s, d, space in out],
@@ -276,13 +283,13 @@
     )
 
 
-def later(copy, buf):
-    arrived = []
-
-    def get():
-        if not arrived:
-            copy.wait()
-            arrived.append(True)
+def later(copies, buf):
+    arrived = set()
+
+    def get(part=0):
+        if part not in arrived:
+            copies[part].wait()
+            arrived.add(part)
         return buf
 
     return get
@@ -307,60 +314,57 @@
             pltpu.SemaphoreType.DMA,
         ]
 
-    packed, trace = call(
-        open_kernel, [chunk, ((spots, 32, 128), BF, near_space)], "sccc", (mer, start, wall, connect)
-    )
     table = [((256, 128), BF, near_space)] * 2 + [((256, 256), BF, near_space)] * 2
-    *table, near = call(
-        own_kernel,
-        table + [((1536, 512), BF, far_space)],
-        "cccccc",
-        (jnp.transpose(velocity, (0, 2, 1)), stiffness, curl_matrix, connect, fwd, inv),
-        works(1536, 512),
-        32,
-    )
-
+    packed, trace, *table = call(
+        open_kernel,
+        [chunk, ((spots, 32, 128), BF, near_space), *table],
+        "scccccc",
+        (mer, start, wall, connect, jnp.transpose(velocity, (0, 2, 1)), fwd, inv),
+    )
     twins = [(i, i ^ 1) for i in range(spots)]
     others = [(i, ((i + 1) ^ 1) - 1) for i in range(1, spots - 1)]
 
-    def section(now, packed, whole, far, last):
+    def exchange(packed, trace):
         moved = lax.all_to_all(packed, "mode", 0, 0, tiled=True)
         (back,) = call(
-            induce_kernel, [((16, 32, 128), BF, near_space)], "vvvvvh", (moved, *table, far)
+            induce_kernel, [((16, 32, 128), BF, near_space)], "vvvvv", (moved, *table)
         )
         emf = lax.all_to_all(back, "mode", 0, 0, tiled=True)
         e_twin = lax.ppermute(emf, "mer", twins)
         e_other = lax.ppermute(emf, "mer", others)
-        held = "c" if last is None else "v"
-        if last is not None:
-            whole = lax.all_to_all(whole, "mer", 0, 0, tiled=True)
-        (total,) = call(
-            operator_kernel,
-            [((48, 512), F32, near_space)],
-            "s" + held + "vvvcc",
-            (mer, now, emf, e_twin, e_other, near, far),
-        )
-        args = (mode, mer, now, total, whole, wall, row, dtn)
-        kinds = "ss" + held + "vvccc"
-        if last is None:
-            out = [((6, 8, 512), F32, near_space), chunk]
-            out += [((spots, 16, 128), BF, near_space), ((16, 128), F32, near_space)]
-            return call(first_kernel, out, kinds, args)
-        out = [((6, 8, 512), F32, None), ((2, 8, 2, 64), F32, None)]
-        return call(second_kernel, out, kinds + "cv", (*args, *last))
-
-    whole = lax.all_to_all(trace, "mer", 0, 0, tiled=True)
-    (far,) = call(
-        far_kernel,
-        [((1536, 256), BF, far_space)],
-        "svcc",
-        (mer, whole, stiffness, curl_matrix),
+        return emf, e_twin, e_other, lax.all_to_all(trace, "mer", 0, 0, tiled=True)
+
+    rows = ((48, 512), F32, near_space)
+    emf, e_twin, e_other, whole = exchange(packed, trace)
+    (near,) = call(
+        own_kernel,
+        [((1536, 512), BF, far_space)],
+        "cccv",
+        (stiffness, curl_matrix, connect, emf),
+        works(1536, 512),
+        32,
+    )
+    total, far = call(
+        first_operator_kernel,
+        [rows, ((1536, 256), BF, far_space)],
+        "scvvvcvcc",
+        (mer, start, emf, e_twin, e_other, near, whole, stiffness, curl_matrix),
         works(1536, 256),
         32,
     )
-    (packed,) = call(gate_kernel, [chunk], "vvh", (packed, whole, near))
-    sect, packed, trace, flux = section(start, packed, whole, far, None)
-    done, fluxes = section(sect, packed, trace, far, (start, flux))
+    out = [((6, 8, 512), F32, near_space), chunk]
+    out += [((spots, 16, 128), BF, near_space), ((16, 128), F32, near_space)]
+    sect, packed, trace, flux = call(
+        first_kernel, out, "sscvvccd", (mode, mer, start, total, whole, wall, row, dtn)
+    )
+    emf, e_twin, e_other, whole = exchange(packed, trace)
+    (total,) = call(
+        operator_kernel, [rows], "svvvvcc", (mer, sect, emf, e_twin, e_other, near, far)
+    )
+    out = [((6, 8, 512), F32, None), ((2, 8, 2, 64), F32, None)]
+    done, fluxes = call(
+        second_kernel, out, "ssvvvccdcv", (mode, mer, sect, total, whole, wall, row, dtn, start, flux)
+    )
     return (jnp.transpose(done, (1, 0, 2)), fluxes)
 
 

time: 120 us -> 116 us (0.967)
  blocking collectives: 36.2 us -> 58.6 us
  waiting for transfers between devices: 15.9 us -> 3.22 us
  starting transfers between devices: 43 us -> 30.8 us
  Pallas kernels: 22.6 us -> 21.1 us
    all_to_all x3 -> x4, blocking collectives: 36.2 us -> 58.6 us  [the longest x2 34.3 us: exchange(): moved = lax.all_to_all(packed, 'mode', 0, 0, tiled=True)]
    all_to_all x3 -> x2, waiting for transfers between devices: 12.6 us -> 1.23 us  [exchange(): lax.all_to_all(trace, 'mer', 0, 0, tiled=True)]
    all_to_all x3 -> x2, starting transfers between devices: 29.4 us -> 19.9 us  [exchange(): lax.all_to_all(trace, 'mer', 0, 0, tiled=True)]
    ppermute x4, starting transfers between devices: 13.6 us -> 10.9 us  [the longest x2 7.08 us: exchange(): e_other = lax.ppermute(emf, 'mer', others)]
    pallas_call x10 -> x8, Pallas kernels: 22.6 us -> 21.1 us  [call(): pl.pallas_call(run, out_shape=[space(s, d) if space else jax.ShapeDtypeSt...]
    ppermute x4, waiting for transfers between devices: 3.29 us -> 1.99 us  [the longest x2 1.98 us: exchange(): e_other = lax.ppermute(emf, 'mer', others)]
  transfers between devices with their start and end apart: 7 -> 6, of which waited for: 5 -> 2; matrix products, arithmetic and copies ran while one was open for 0% -> 0% of each run, Pallas kernels for 9% -> 6%
where the time goes in v4:
time: 116 us; the launch traced here: 115 us
  blocking collectives  58.6 us (51%)
  starting transfers between devices  30.8 us (27%)
  Pallas kernels  21.1 us (18%)
  waiting for transfers between devices  3.22 us (3%)
    all_to_all x2, blocking collectives, exchange(): moved = lax.all_to_all(packed, 'mode', 0, 0, tiled=True)  34.3 us
    all_to_all x2, blocking collectives, exchange(): emf = lax.all_to_all(back, 'mode', 0, 0, tiled=True)  24.4 us
    pallas_call x8, Pallas kernels, call(): pl.pallas_call(run, out_shape=[space(s, d) if space else jax.ShapeDtypeSt...  21.1 us
    all_to_all x2, starting transfers between devices, exchange(): lax.all_to_all(trace, 'mer', 0, 0, tiled=True)  19.9 us
    ppermute x2, starting transfers between devices, exchange(): e_other = lax.ppermute(emf, 'mer', others)  7.08 us
    ppermute x2, starting transfers between devices, exchange(): e_twin = lax.ppermute(emf, 'mer', twins)  3.84 us
  transfers between devices with their start and end apart: 6, of which 2 were waited for; matrix products, arithmetic and copies ran while one was open for 0% of the time, Pallas kernels for 6%

profile of v4, /device:TPU:1, one launch (start us, length us, event | category | flops | bytes accessed | tf_op | source)
XLA Modules:
  0.0 114.5 jit_solution(5299076513025946727)
XLA Ops:
  0.6 2.0 %shard_map.113 = (bf16[16,16,128]{2,1,0:T(8,128)(2,1)S(1)}, bf16[32,32,128]{2,1,0:T(8,128)(2,1)}, bf16[256,128]{1,0:T(8,128)(2,1)S(1)}, bf16[256,128]{1,0:T(8,12...) custom-call(s32[1]{0:T(128)} %bitcast.1.refs_0_.refs_1_, f32[6,8,512]{2,1,0:T(8,128)} %bitcast.7, ...), custom_call_target="tpu_custom_call" | custom-call | tf_op jit(solution)/shard_map/pallas_call | solution.py:271
  2.7 22.2 %all_to_all.30.refs_0_ = bf16[16,16,128]{2,1,0:T(8,128)(2,1)S(1)} all-to-all(bf16[16,16,128]{2,1,0:T(8,128)(2,1)S(1)} %get-tuple-element.16), channel_id=1, replica_groups=mesh['mode'=16,'mer'=32] {'mode'}, dimensions={0} | all-to-all | bytes 131072 | tf_op jit(solution)/shard_map/all_to_all | solution.py:328
  24.8 0.5 shard_map.114
  25.3 12.3 %all_to_all.31.refs_3_.refs_2_ = bf16[16,32,128]{2,1,0:T(8,128)(2,1)S(1)} all-to-all(bf16[16,32,128]{2,1,0:T(8,128)(2,1)S(1)} %shard_map.114), channel_id=1, replica_groups=mesh['mode'=16,'mer'=32] {'mode'}, dimensions={0} | all-to-all | bytes 262144 | tf_op jit(solution)/shard_map/all_to_all | solution.py:332
  37.6 11.1 %all-to-all-start.2 = ((bf16[32,32,128]{2,1,0:T(8,128)(2,1)}), bf16[32,32,128]{2,1,0:T(8,128)(2,1)S(1)}, u32[]{:S(2)}, u32[]{:S(2)}) async-start(bf16[32,32,128]{2,1,0:T(8,128)(2,1)} %get-tuple-element.21), calls=%async_computation.2 | async-start | bytes 524288 | tf_op jit(solution)/shard_map/all_to_all | solution.py:335
  48.7 3.5 %collective-permute-start.1 = (bf16[16,32,128]{2,1,0:T(8,128)(2,1)S(1)}, bf16[16,32,128]{2,1,0:T(8,128)(2,1)S(1)}, u32[]{:S(2)}, u32[]{:S(2)}) collective-permute-start(bf16[16,32,128]{2,1,0:T(8,128)(2,1)S(1)} %all_to_all.31.refs_3_.refs_2_), channel_id=1, source_target_pairs={{1,2},{2,1},{3,4},{4,3},{5,6},{6,5},{7,8},{8,7},{9,10},{10,9},{11,... | collective-permute-start | bytes 393224 | tf_op jit(solution)/shard_map/ppermute | solution.py:334
  52.2 1.9 %collective-permute-start = (bf16[16,32,128]{2,1,0:T(8,128)(2,1)S(1)}, bf16[16,32,128]{2,1,0:T(8,128)(2,1)S(1)}, u32[]{:S(2)}, u32[]{:S(2)}) collective-permute-start(bf16[16,32,128]{2,1,0:T(8,128)(2,1)S(1)} %all_to_all.31.refs_3_.refs_2_), channel_id=1, source_target_pairs={{0,1},{1,0},{2,3},{3,2},{4,5},{5,4},{6,7},{7,6},{8,9},{9,8},{10,11... | collective-permute-start | bytes 393224 | tf_op jit(solution)/shard_map/ppermute | solution.py:333
  54.2 4.7 %shard_map.115.refs_5_ = bf16[1536,512]{1,0:T(8,128)(2,1)} custom-call(f32[64,64]{1,0:T(8,128)} %refs_7_.3, f32[64,64]{1,0:T(8,128)} %refs_8_.1, s32[16,64]{1,0:T(8,128)} %refs_2_.1, bf16[16,32,128]{2,1,0:T(8,128)(2,1)S(1)} %all_to_all.31.refs_3_.refs_2_), custom_call_target="tpu_custom_call" | custom-call | tf_op jit(solution)/shard_map/pallas_call | solution.py:271
  58.8 0.0 collective-permute-done.1.refs_4_
  58.8 0.0 collective-permute-done.refs_3_
  58.8 1.2 %all-to-all-done.2.refs_6_.refs_4_ = bf16[32,32,128]{2,1,0:T(8,128)(2,1)S(1)} async-done(((bf16[32,32,128]{2,1,0:T(8,128)(2,1)}), bf16[32,32,128]{2,1,0:T(8,128)(2,1)S(1)}, u32[]{:S(2)}, u32[]{:S(2)}) %all-to-all-start.2) | async-done | bytes 262176 | tf_op jit(solution)/shard_map/all_to_all | solution.py:335
  60.1 3.9 %shard_map.116 = (f32[48,512]{1,0:T(8,128)S(1)}, bf16[1536,256]{1,0:T(8,128)(2,1)}) custom-call(s32[1]{0:T(128)} %bitcast.1.refs_0_.refs_1_, f32[6,8,512]{2,1,0:T(8,128)} %bitcast.8, bf16[16,32,128]{2,1,0:T(8,128)(2,1)S(1)} %all_to_all.31.refs_3_.refs_2_, bf16[16,32,128]{2,1,0:T(8,128)(2,1)S(1)} %collective-permute-done.refs_3_, ...), custom_call_target="tpu_custom_call" | custom-call | tf_op jit(solution)/shard_map/pallas_call | solution.py:271
  63.9 3.7 %shard_map.117 = (f32[6,8,512]{2,1,0:T(8,128)S(1)}, bf16[16,16,128]{2,1,0:T(8,128)(2,1)S(1)}, bf16[32,16,128]{2,1,0:T(8,128)(2,1)}, f32[16,128]{1,0:T(8,128)S(1)}) custom-call(s32[1]{0:T(128)} %bitcast.refs_0_, s32[1]{0:T(128)} %bitcast.1.refs_0_.refs_1_, f32[6,8,512]{2,1,0:T(8,128)} %bitcast.9, f32[48,512]{1,0:T(8,128)S(1)} %get-tuple-element.22.refs_3_, ...), custom_call_target="tpu_custom_call" | custom-call | tf_op jit(solution)/shard_map/pallas_call | solution.py:271
  67.7 12.1 %all_to_all.32.refs_0_ = bf16[16,16,128]{2,1,0:T(8,128)(2,1)S(1)} all-to-all(bf16[16,16,128]{2,1,0:T(8,128)(2,1)S(1)} %get-tuple-element.24), channel_id=1, replica_groups=mesh['mode'=16,'mer'=32] {'mode'}, dimensions={0} | all-to-all | bytes 131072 | tf_op jit(solution)/shard_map/all_to_all | solution.py:328
  79.8 0.5 shard_map.118
  80.2 12.1 %all_to_all.33.refs_2_ = bf16[16,32,128]{2,1,0:T(8,128)(2,1)S(1)} all-to-all(bf16[16,32,128]{2,1,0:T(8,128)(2,1)S(1)} %shard_map.118), channel_id=1, replica_groups=mesh['mode'=16,'mer'=32] {'mode'}, dimensions={0} | all-to-all | bytes 262144 | tf_op jit(solution)/shard_map/all_to_all | solution.py:332
  92.3 8.8 %all-to-all-start.5 = ((bf16[32,16,128]{2,1,0:T(8,128)(2,1)}), bf16[32,16,128]{2,1,0:T(8,128)(2,1)S(1)}, u32[]{:S(2)}, u32[]{:S(2)}) async-start(bf16[32,16,128]{2,1,0:T(8,128)(2,1)} %get-tuple-element.26), calls=%async_computation.5 | async-start | bytes 262144 | tf_op jit(solution)/shard_map/all_to_all | solution.py:335
  101.1 3.5 %collective-permute-start.3 = (bf16[16,32,128]{2,1,0:T(8,128)(2,1)S(1)}, bf16[16,32,128]{2,1,0:T(8,128)(2,1)S(1)}, u32[]{:S(2)}, u32[]{:S(2)}) collective-permute-start(bf16[16,32,128]{2,1,0:T(8,128)(2,1)S(1)} %all_to_all.33.refs_2_), channel_id=1, source_target_pairs={{1,2},{2,1},{3,4},{4,3},{5,6},{6,5},{7,8},{8,7},{9,10},{10,9},{11,... | collective-permute-start | bytes 393224 | tf_op jit(solution)/shard_map/ppermute | solution.py:334
  104.7 1.9 %collective-permute-start.2 = (bf16[16,32,128]{2,1,0:T(8,128)(2,1)S(1)}, bf16[16,32,128]{2,1,0:T(8,128)(2,1)S(1)}, u32[]{:S(2)}, u32[]{:S(2)}) collective-permute-start(bf16[16,32,128]{2,1,0:T(8,128)(2,1)S(1)} %all_to_all.33.refs_2_), channel_id=1, source_target_pairs={{0,1},{1,0},{2,3},{3,2},{4,5},{5,4},{6,7},{7,6},{8,9},{9,8},{10,11... | collective-permute-start | bytes 393224 | tf_op jit(solution)/shard_map/ppermute | solution.py:333
  106.6 2.0 %collective-permute-done.3.refs_4_ = bf16[16,32,128]{2,1,0:T(8,128)(2,1)S(1)} collective-permute-done((bf16[16,32,128]{2,1,0:T(8,128)(2,1)S(1)}, bf16[16,32,128]{2,1,0:T(8,128)(2,1)S(1)}, u32[]{:S(2)}, u32[]{:S(2)}) %collective-permute-start.3) | collective-permute-done | bytes 131104 | tf_op jit(solution)/shard_map/ppermute | solution.py:334
  108.6 0.0 collective-permute-done.2.refs_3_
  108.6 2.3 %shard_map.119.refs_3_ = f32[48,512]{1,0:T(8,128)S(1)} custom-call(s32[1]{0:T(128)} %bitcast.1.refs_0_.refs_1_, f32[6,8,512]{2,1,0:T(8,128)S(1)} %get-tuple-element.23.refs_1_.refs_2_, bf16[16,32,128]{2,1,0:T(8,128)(2,1)S(1)} %all_to_all.33.refs_2_, bf16[16,32,128]{2,1,0:T(8,128)(2,1)S(1)} %collective-permute-done.2.refs_3_, ...), custom_call_target="tpu_custom_call" | custom-call | tf_op jit(solution)/shard_map/pallas_call | solution.py:271
  111.0 0.0 all-to-all-done.5.refs_4_
  111.0 3.6 %shard_map.120 = (f32[6,8,512]{2,1,0:T(8,128)}, f32[2,8,2,64]{3,2,1,0:T(2,128)}) custom-call(s32[1]{0:T(128)} %bitcast.refs_0_, s32[1]{0:T(128)} %bitcast.1.refs_0_.refs_1_, f32[6,8,512]{2,1,0:T(8,128)S(1)} %get-tuple-element.23.refs_1_.refs_2_, f32[48,512]{1,0:T(8,128)S(1)} %shard_map.119.refs_3_, bf16[32,16,128]{2,1,0:T(8,128)(2,1)S(1)} %all-to-all-done.5.refs_4_, ...), custom_call_target="tpu_custom_call" | custom-call | tf_op jit(solution)/shard_map/pallas_call | solution.py:271
Async XLA Ops:
  37.6 22.5 %all-to-all-start.2 = ((bf16[32,32,128]{2,1,0:T(8,128)(2,1)}), bf16[32,32,128]{2,1,0:T(8,128)(2,1)S(1)}, u32[]{:S(2)}, u32[]{:S(2)}) async-start(bf16[32,32,128]{2,1,0:T(8,128)(2,1)} %get-tuple-element.21), calls=%async_computation.2 | async-start | bytes 524288 | tf_op jit(solution)/shard_map/all_to_all | solution.py:335
  48.7 10.1 %collective-permute-start.1 = (bf16[16,32,128]{2,1,0:T(8,128)(2,1)S(1)}, bf16[16,32,128]{2,1,0:T(8,128)(2,1)S(1)}, u32[]{:S(2)}, u32[]{:S(2)}) collective-permute-start(bf16[16,32,128]{2,1,0:T(8,128)(2,1)S(1)} %all_to_all.31.refs_3_.refs_2_), channel_id=1, source_target_pairs={{1,2},{2,1},{3,4},{4,3},{5,6},{6,5},{7,8},{8,7},{9,10},{10,9},{11,... | collective-permute-start | bytes 393224 | tf_op jit(solution)/shard_map/ppermute | solution.py:334
  52.2 6.6 %collective-permute-start = (bf16[16,32,128]{2,1,0:T(8,128)(2,1)S(1)}, bf16[16,32,128]{2,1,0:T(8,128)(2,1)S(1)}, u32[]{:S(2)}, u32[]{:S(2)}) collective-permute-start(bf16[16,32,128]{2,1,0:T(8,128)(2,1)S(1)} %all_to_all.31.refs_3_.refs_2_), channel_id=1, source_target_pairs={{0,1},{1,0},{2,3},{3,2},{4,5},{5,4},{6,7},{7,6},{8,9},{9,8},{10,11... | collective-permute-start | bytes 393224 | tf_op jit(solution)/shard_map/ppermute | solution.py:333
  92.3 18.7 %all-to-all-start.5 = ((bf16[32,16,128]{2,1,0:T(8,128)(2,1)}), bf16[32,16,128]{2,1,0:T(8,128)(2,1)S(1)}, u32[]{:S(2)}, u32[]{:S(2)}) async-start(bf16[32,16,128]{2,1,0:T(8,128)(2,1)} %get-tuple-element.26), calls=%async_computation.5 | async-start | bytes 262144 | tf_op jit(solution)/shard_map/all_to_all | solution.py:335
  101.1 7.5 %collective-permute-start.3 = (bf16[16,32,128]{2,1,0:T(8,128)(2,1)S(1)}, bf16[16,32,128]{2,1,0:T(8,128)(2,1)S(1)}, u32[]{:S(2)}, u32[]{:S(2)}) collective-permute-start(bf16[16,32,128]{2,1,0:T(8,128)(2,1)S(1)} %all_to_all.33.refs_2_), channel_id=1, source_target_pairs={{1,2},{2,1},{3,4},{4,3},{5,6},{6,5},{7,8},{8,7},{9,10},{10,9},{11,... | collective-permute-start | bytes 393224 | tf_op jit(solution)/shard_map/ppermute | solution.py:334
  104.7 3.9 %collective-permute-start.2 = (bf16[16,32,128]{2,1,0:T(8,128)(2,1)S(1)}, bf16[16,32,128]{2,1,0:T(8,128)(2,1)S(1)}, u32[]{:S(2)}, u32[]{:S(2)}) collective-permute-start(bf16[16,32,128]{2,1,0:T(8,128)(2,1)S(1)} %all_to_all.33.refs_2_), channel_id=1, source_target_pairs={{0,1},{1,0},{2,3},{3,2},{4,5},{5,4},{6,7},{7,6},{8,9},{9,8},{10,11... | collective-permute-start | bytes 393224 | tf_op jit(solution)/shard_map/ppermute | solution.py:333

commit v5 on v4

--- a/solution.py
+++ b/solution.py
@@ -66,22 +66,39 @@
     return jnp.concatenate(cols, 1)
 
 
-def wall_onehot(wall_ref, mer):
+def wall_onehot(wall_ref):
     twice = jnp.concatenate([wall_ref[...], wall_ref[...]], 1)
     nodes = lax.broadcasted_iota(jnp.int32, (512, 128), 0)
-    half = lax.broadcasted_iota(jnp.int32, (512, 128), 1) // 64
-    return jnp.where(half == mer % 2, (nodes == twice).astype(F32), 0.0).astype(BF)
+    return (nodes == twice).astype(F32).astype(BF)
+
+
+def trace_rows(rows, onehot):
+    both = nn(rows, onehot)
+    return jnp.where(low_lanes((8, 128)), both[:8], both[8:]).astype(BF)
+
+
+def low_lanes(shape):
+    return lax.broadcasted_iota(jnp.int32, shape, len(shape) - 1) < 64
 
 
 def two_by_two(conn_ref):
     return jnp.concatenate([conn_ref[pl.ds(0, 8, 2), :], conn_ref[pl.ds(1, 8, 2), :]], 1)
 
 
-def open_kernel(mer_ref, field, wall, conn, vel, fwd, inv, pack_ref, out_ref, va_ref, vb_ref, fwd_ref, inv_ref):
-    onehot = wall_onehot(wall(), mer_ref[0])
-    conn = two_by_two(conn())
+def open_kernel(mode_ref, field, wall, conn, vel, fwd, inv, pack_ref, out_ref, mark_ref, va_ref, vb_ref, fwd_ref, inv_ref):
+    onehot = wall_onehot(wall())
+    conn = conn()[...]
     field_ref = field()
     pack({(c, p): field_ref[3 * p + c] for c in range(3) for p in range(2)}, pack_ref)
+    tr = trace_rows(jnp.concatenate([field_ref[2], field_ref[5]], 0).astype(BF), onehot)
+    for j in range(out_ref.shape[0]):
+        out_ref[j] = tr
+    part = jnp.zeros((16, 64), jnp.int32) + mode_ref[0] % 4
+    code = jnp.where(part < 2, conn // 32, conn % 32).astype(F32)
+    code = jnp.concatenate([code, code], 1)
+    even = (jnp.zeros((16, 128), jnp.int32) + mode_ref[0] % 2) == 0
+    code = jnp.where(even, pltpu.roll(code, 32, 1), code)
+    mark_ref[...] = jnp.where(lane_group((16, 128)) == 3, code, 0.0)
     vel_ref = vel()
     vel = [vel_ref[c].astype(F32) for c in range(3)]
     zero = jnp.zeros_like(vel[0])
@@ -89,12 +106,6 @@
     vb_ref[...] = jnp.concatenate([vel[1], vel[2], vel[0], zero], 0).T.astype(BF)
     fwd_ref[...] = fwd()[...]
     inv_ref[...] = inv()[...]
-    last = jnp.concatenate([field_ref[2], field_ref[5]], 0).astype(BF)
-    tr = nn(last, onehot)
-    parts = [tr, (conn // 32).astype(F32), (conn % 32).astype(F32)]
-    parts = jnp.concatenate(parts, 0).astype(BF)
-    for j in range(out_ref.shape[0]):
-        out_ref[j] = parts
 
 
 def element_blocks(ref, sign):
@@ -134,7 +145,7 @@
     copy.wait()
 
 
-def induce_kernel(moved_ref, va_ref, vb_ref, fwd_ref, inv_ref, out_ref):
+def induce_kernel(moved_ref, mark_ref, va_ref, vb_ref, fwd_ref, inv_ref, out_ref):
     moved = moved_ref[...]
     rows = moved.reshape(256, 128)
     turned = pltpu.roll(rows.astype(F32), 96, 1).astype(BF)
@@ -142,7 +153,7 @@
     after = nn(fwd_ref[...], turned)
     cross = va_ref[...].astype(F32) * after - vb_ref[...].astype(F32) * here
     back = nn(inv_ref[...], cross.astype(BF))
-    out_ref[:, :16] = back.astype(BF).reshape(16, 16, 128)
+    out_ref[:, :16] = (back.reshape(16, 16, 128) + mark_ref[...][None]).astype(BF)
     out_ref[:, 16:] = moved
 
 
@@ -154,30 +165,31 @@
     return jnp.concatenate([field_ref[s] for s in ORDER], 0)
 
 
+def side(mer_ref, a_ref, b_ref, odd_takes, part):
+    rows = slice(16 * part, 16 * part + 16)
+    odd = (jnp.zeros((16, 128), jnp.int32) + mer_ref[0] % 2) == 1
+    first, second = (a_ref, b_ref) if odd_takes == 0 else (b_ref, a_ref)
+    return lambda s: jnp.where(odd, first[s, rows], second[s, rows])
+
+
 def operator_rows(mer_ref, now, emf_ref, pa_ref, pb_ref, near, far):
-    odd = (jnp.zeros((16, 128), jnp.int32) + mer_ref[0] % 2) == 1
-
-    def before(part):
-        rows = slice(16 * part, 16 * part + 16)
-        return lambda s: jnp.where(odd, pa_ref[s, rows].astype(F32), pb_ref[s, rows].astype(F32))
-
-    def behind(part):
-        rows = slice(16 * part, 16 * part + 16)
-        return lambda s: jnp.where(odd, pb_ref[s, rows].astype(F32), pa_ref[s, rows].astype(F32))
-
     own = unpack(lambda s: emf_ref[s, :16], 16)
-    e_next, f_next = unpack(behind(0), 8), unpack(behind(1), 8)
-    e_prev, f_prev = unpack(before(0), 16), unpack(before(1), 16)
+    e_next, f_next = [unpack(side(mer_ref, pa_ref, pb_ref, 1, part), 8) for part in range(2)]
+    e_prev, f_prev = [unpack(side(mer_ref, pa_ref, pb_ref, 0, part), 16) for part in range(2)]
     field = rows_of(now).astype(BF)
     total = nn(jnp.concatenate([own, e_next, field, f_next], 1), near()[...])
     low = nn(jnp.concatenate([e_prev, own[:, :256], f_prev, field[:, :256]], 1), far()[...])
     return jnp.concatenate([total[:, :256] + low, total[:, 256:]], 1)
 
 
-def first_operator_kernel(mer_ref, now, emf_ref, pa_ref, pb_ref, near, whole_ref, stiff, curl, *refs):
-    out_ref, far_out, far_ref, tall_ref, work_ref, sem = refs
-    code = whole_ref[jnp.maximum(mer_ref[0] - 1, 0)].astype(F32)
-    conn = 32.0 * code[16:24] + code[24:32]
+def first_operator_kernel(mer_ref, now, emf_ref, pa_ref, pb_ref, near, stiff, curl, *refs):
+    out_ref, far_out, far_ref, tall_ref, work_ref, conn_ref, sem = refs
+    tile = side(mer_ref, pa_ref, pb_ref, 0, 0)
+    code = [pltpu.roll(tile(s).astype(F32), 32 + 32 * (s % 2), 1) for s in range(4)]
+    first = lane_group((16, 128)) == 0
+    conn_ref[...] = 32.0 * jnp.where(first, code[0], code[1]) + jnp.where(first, code[2], code[3])
+    conn = [conn_ref[pl.ds(k, 8, 2), :] for k in range(2)]
+    conn = jnp.where(low_lanes((8, 128)), conn[0], pltpu.roll(conn[1], 64, 1))
     s, c = operators(conn, 512.0, 256, stiff(), curl(), tall_ref, work_ref)
     there = jnp.where(mer_ref[0] > 0, 1.0, 0.0)
     far_ref[:768] = (c * there).astype(BF)
@@ -192,19 +204,25 @@
     out_ref[...] = operator_rows(mer_ref, now, emf_ref, pa_ref, pb_ref, near, far)
 
 
-def finish(mode_ref, mer_ref, now, total_ref, whole_ref, wall, mass, dtn):
-    onehot = wall_onehot(wall(), mer_ref[0])
+def finish(mode_ref, now, total_ref, whole_ref, wall, mass, dtn):
+    onehot = wall_onehot(wall())
     field = rows_of(now)
     number = lax.broadcasted_iota(jnp.int32, (48, 512), 0) % 8 + 8 * mode_ref[0]
     coef = (number.astype(F32) / 128.0) ** 2
-    whole = jnp.concatenate([whole_ref[2 * a, :16] + whole_ref[2 * a + 1, :16] for a in range(16)], 1)
+    low = low_lanes((8, 128))
+    parts = [], []
+    for a in range(whole_ref.shape[0] // 2):
+        x, y = whole_ref[2 * a].astype(F32), whole_ref[2 * a + 1].astype(F32)
+        parts[0].append(jnp.where(low, x, pltpu.roll(y, 64, 1)))
+        parts[1].append(jnp.where(low, pltpu.roll(x, 64, 1), y))
+    whole = jnp.concatenate([jnp.concatenate(p, 1) for p in parts], 0).astype(BF)
     weight = 1.0 / mass()[...]
     every = [nt(whole, dtn(k)[2 * k : 2 * k + 2].reshape(128, 2048)) for k in range(4)]
     every = jnp.concatenate(every, 1)
     mine = lax.broadcasted_iota(jnp.int32, (16, 512), 0) % 8
     every = jnp.where(mine == lax.broadcasted_iota(jnp.int32, (16, 512), 1) // 64, every, 0.0)
     flux = every[:, :128] + every[:, 128:256] + every[:, 256:384] + every[:, 384:]
-    flux = flux + pltpu.roll(flux, 64, 1)
+    flux = jnp.where(low_lanes((16, 128)), flux + pltpu.roll(flux, 64, 1), 0.0)
     upper = flux.astype(BF)
     added = nt(upper, onehot) + nt((flux - upper.astype(F32)).astype(BF), onehot)
     total = total_ref[...]
@@ -214,22 +232,22 @@
 
 
 def first_kernel(*refs):
-    sect_ref, pack_ref, trace_ref, flux_ref = refs[8:]
-    rate, field, flux, onehot = finish(*refs[:8])
+    sect_ref, pack_ref, trace_ref, flux_ref = refs[7:]
+    rate, field, flux, onehot = finish(*refs[:7])
     sect = field + 0.2 * rate
     flux_ref[...] = flux
     rows = {(c, p): sect[16 * c + 8 * p : 16 * c + 8 * p + 8] for c in range(3) for p in range(2)}
     for (c, p), r in rows.items():
         sect_ref[3 * p + c] = r
     pack(rows, pack_ref)
-    tr = nn(sect[32:].astype(BF), onehot).astype(BF)
+    tr = trace_rows(sect[32:].astype(BF), onehot)
     for j in range(trace_ref.shape[0]):
         trace_ref[j] = tr
 
 
 def second_kernel(*refs):
-    start, first_flux_ref, out_ref, flux_ref = refs[8:]
-    rate, sect, flux, onehot = finish(*refs[:8])
+    start, first_flux_ref, out_ref, flux_ref = refs[7:]
+    rate, sect, flux, onehot = finish(*refs[:7])
     start_ref = start()
     for c in range(3):
         for p in range(2):
@@ -317,9 +335,9 @@
     table = [((256, 128), BF, near_space)] * 2 + [((256, 256), BF, near_space)] * 2
     packed, trace, *table = call(
         open_kernel,
-        [chunk, ((spots, 32, 128), BF, near_space), *table],
+        [chunk, ((spots, 8, 128), BF, near_space), ((16, 128), F32, near_space), *table],
         "scccccc",
-        (mer, start, wall, connect, jnp.transpose(velocity, (0, 2, 1)), fwd, inv),
+        (mode, start, wall, connect, jnp.transpose(velocity, (0, 2, 1)), fwd, inv),
     )
     twins = [(i, i ^ 1) for i in range(spots)]
     others = [(i, ((i + 1) ^ 1) - 1) for i in range(1, spots - 1)]
@@ -327,7 +345,7 @@
     def exchange(packed, trace):
         moved = lax.all_to_all(packed, "mode", 0, 0, tiled=True)
         (back,) = call(
-            induce_kernel, [((16, 32, 128), BF, near_space)], "vvvvv", (moved, *table)
+            induce_kernel, [((16, 32, 128), BF, near_space)], "vvvvvv", (moved, *table)
         )
         emf = lax.all_to_all(back, "mode", 0, 0, tiled=True)
         e_twin = lax.ppermute(emf, "mer", twins)
@@ -347,15 +365,15 @@
     total, far = call(
         first_operator_kernel,
         [rows, ((1536, 256), BF, far_space)],
-        "scvvvcvcc",
-        (mer, start, emf, e_twin, e_other, near, whole, stiffness, curl_matrix),
-        works(1536, 256),
+        "scvvvccc",
+        (mer, start, emf, e_twin, e_other, near, stiffness, curl_matrix),
+        [*works(1536, 256)[:3], pltpu.VMEM((16, 128), F32), pltpu.SemaphoreType.DMA],
         32,
     )
     out = [((6, 8, 512), F32, near_space), chunk]
-    out += [((spots, 16, 128), BF, near_space), ((16, 128), F32, near_space)]
+    out += [((spots, 8, 128), BF, near_space), ((16, 128), F32, near_space)]
     sect, packed, trace, flux = call(
-        first_kernel, out, "sscvvccd", (mode, mer, start, total, whole, wall, row, dtn)
+        first_kernel, out, "scvvccd", (mode, start, total, whole, wall, row, dtn)
     )
     emf, e_twin, e_other, whole = exchange(packed, trace)
     (total,) = call(
@@ -363,7 +381,7 @@
     )
     out = [((6, 8, 512), F32, None), ((2, 8, 2, 64), F32, None)]
     done, fluxes = call(
-        second_kernel, out, "ssvvvccdcv", (mode, mer, sect, total, whole, wall, row, dtn, start, flux)
+        second_kernel, out, "svvvccdcv", (mode, sect, total, whole, wall, row, dtn, start, flux)
     )
     return (jnp.transpose(done, (1, 0, 2)), fluxes)
 

time: 116 us -> 118 us (1.017)
  waiting for transfers between devices: 3.22 us -> 5.97 us
    all_to_all x2, waiting for transfers between devices: 1.23 us -> 5.96 us  [exchange(): lax.all_to_all(trace, 'mer', 0, 0, tiled=True)]
    ppermute x2, starting transfers between devices: 7.08 us -> 11.6 us  [exchange(): e_other = lax.ppermute(emf, 'mer', others)]
    all_to_all x2, starting transfers between devices: 19.9 us -> 15.8 us  [exchange(): lax.all_to_all(trace, 'mer', 0, 0, tiled=True)]
    ppermute x2, waiting for transfers between devices: 1.98 us -> 0.01 us  [exchange(): e_other = lax.ppermute(emf, 'mer', others)]
  transfers between devices with their start and end apart: 6 -> 6, of which waited for: 2 -> 1; matrix products, arithmetic and copies ran while one was open for 0% -> 0% of each run, Pallas kernels for 6% -> 9%
where the time goes in v5:
time: 118 us; the launch traced here: 117 us
  blocking collectives  58.4 us (49%)
  starting transfers between devices  31.2 us (26%)
  Pallas kernels  20.9 us (18%)
  waiting for transfers between devices  5.97 us (5%)
    all_to_all x2, blocking collectives, exchange(): moved = lax.all_to_all(packed, 'mode', 0, 0, tiled=True)  33.8 us
    all_to_all x2, blocking collectives, exchange(): emf = lax.all_to_all(back, 'mode', 0, 0, tiled=True)  24.6 us
    pallas_call x8, Pallas kernels, call(): pl.pallas_call(run, out_shape=[space(s, d) if space else jax.ShapeDtypeSt...  20.9 us
    all_to_all x2, starting transfers between devices, exchange(): lax.all_to_all(trace, 'mer', 0, 0, tiled=True)  15.8 us
    ppermute x2, starting transfers between devices, exchange(): e_other = lax.ppermute(emf, 'mer', others)  11.6 us
    all_to_all x2, waiting for transfers between devices, exchange(): lax.all_to_all(trace, 'mer', 0, 0, tiled=True)  5.96 us
    ppermute x2, starting transfers between devices, exchange(): e_twin = lax.ppermute(emf, 'mer', twins)  3.84 us
  transfers between devices with their start and end apart: 6, of which 1 were waited for; matrix products, arithmetic and copies ran while one was open for 0% of the time, Pallas kernels for 9%

profile of v5, /device:TPU:1, one launch (start us, length us, event | category | flops | bytes accessed | tf_op | source)
XLA Modules:
  0.0 117.3 jit_solution(13297823971331867188)
XLA Ops:
  0.6 1.8 %shard_map.113 = (bf16[16,16,128]{2,1,0:T(8,128)(2,1)S(1)}, bf16[32,8,128]{2,1,0:T(8,128)(2,1)}, f32[16,128]{1,0:T(8,128)S(1)}, bf16[256,128]{1,0:T(8,128)(2,1)S...) custom-call(s32[1]{0:T(128)} %bitcast.refs_0_, ...), custom_call_target="tpu_custom_call" | custom-call | tf_op jit(solution)/shard_map/pallas_call | solution.py:289
  2.5 22.2 %all_to_all.30.refs_0_ = bf16[16,16,128]{2,1,0:T(8,128)(2,1)S(1)} all-to-all(bf16[16,16,128]{2,1,0:T(8,128)(2,1)S(1)} %get-tuple-element.17), channel_id=1, replica_groups=mesh['mode'=16,'mer'=32] {'mode'}, dimensions={0} | all-to-all | bytes 131072 | tf_op jit(solution)/shard_map/all_to_all | solution.py:346
  24.7 0.5 shard_map.114
  25.1 12.3 %all_to_all.31.refs_3_.refs_2_ = bf16[16,32,128]{2,1,0:T(8,128)(2,1)S(1)} all-to-all(bf16[16,32,128]{2,1,0:T(8,128)(2,1)S(1)} %shard_map.114), channel_id=1, replica_groups=mesh['mode'=16,'mer'=32] {'mode'}, dimensions={0} | all-to-all | bytes 262144 | tf_op jit(solution)/shard_map/all_to_all | solution.py:350
  37.4 5.9 %collective-permute-start.1 = (bf16[16,32,128]{2,1,0:T(8,128)(2,1)S(1)}, bf16[16,32,128]{2,1,0:T(8,128)(2,1)S(1)}, u32[]{:S(2)}, u32[]{:S(2)}) collective-permute-start(bf16[16,32,128]{2,1,0:T(8,128)(2,1)S(1)} %all_to_all.31.refs_3_.refs_2_), channel_id=1, source_target_pairs={{1,2},{2,1},{3,4},{4,3},{5,6},{6,5},{7,8},{8,7},{9,10},{10,9},{11,... | collective-permute-start | bytes 393224 | tf_op jit(solution)/shard_map/ppermute | solution.py:352
  43.3 1.9 %collective-permute-start = (bf16[16,32,128]{2,1,0:T(8,128)(2,1)S(1)}, bf16[16,32,128]{2,1,0:T(8,128)(2,1)S(1)}, u32[]{:S(2)}, u32[]{:S(2)}) collective-permute-start(bf16[16,32,128]{2,1,0:T(8,128)(2,1)S(1)} %all_to_all.31.refs_3_.refs_2_), channel_id=1, source_target_pairs={{0,1},{1,0},{2,3},{3,2},{4,5},{5,4},{6,7},{7,6},{8,9},{9,8},{10,11... | collective-permute-start | bytes 393224 | tf_op jit(solution)/shard_map/ppermute | solution.py:351
  45.2 8.1 %all-to-all-start.2 = ((bf16[32,8,128]{2,1,0:T(8,128)(2,1)}), bf16[32,8,128]{2,1,0:T(8,128)(2,1)S(1)}, u32[]{:S(2)}, u32[]{:S(2)}) async-start(bf16[32,8,128]{2,1,0:T(8,128)(2,1)} %get-tuple-element.24), calls=%async_computation.2 | async-start | bytes 131072 | tf_op jit(solution)/shard_map/all_to_all | solution.py:353
  53.4 4.6 %shard_map.115.refs_5_ = bf16[1536,512]{1,0:T(8,128)(2,1)} custom-call(f32[64,64]{1,0:T(8,128)} %refs_6_.4, f32[64,64]{1,0:T(8,128)} %refs_7_.1, s32[16,64]{1,0:T(8,128)} %refs_2_.1, bf16[16,32,128]{2,1,0:T(8,128)(2,1)S(1)} %all_to_all.31.refs_3_.refs_2_), custom_call_target="tpu_custom_call" | custom-call | tf_op jit(solution)/shard_map/pallas_call | solution.py:289
  58.1 0.0 collective-permute-done.1.refs_4_
  58.1 0.0 collective-permute-done.refs_3_
  58.1 3.8 %shard_map.116 = (f32[48,512]{1,0:T(8,128)S(1)}, bf16[1536,256]{1,0:T(8,128)(2,1)}) custom-call(s32[1]{0:T(128)} %bitcast.2.refs_0_, f32[6,8,512]{2,1,0:T(8,128)} %bitcast.8, bf16[16,32,128]{2,1,0:T(8,128)(2,1)S(1)} %all_to_all.31.refs_3_.refs_2_, bf16[16,32,128]{2,1,0:T(8,128)(2,1)S(1)} %collective-permute-done.refs_3_, ...), custom_call_target="tpu_custom_call" | custom-call | tf_op jit(solution)/shard_map/pallas_call | solution.py:289
  61.9 0.0 all-to-all-done.2.refs_3_
  61.9 3.7 %shard_map.117 = (f32[6,8,512]{2,1,0:T(8,128)S(1)}, bf16[16,16,128]{2,1,0:T(8,128)(2,1)S(1)}, bf16[32,8,128]{2,1,0:T(8,128)(2,1)}, f32[16,128]{1,0:T(8,128)S(1)}) custom-call(s32[1]{0:T(128)} %bitcast.refs_0_, f32[6,8,512]{2,1,0:T(8,128)} %bitcast.9, f32[48,512]{1,0:T(8,128)S(1)} %get-tuple-element.23.refs_2_, ...), custom_call_target="tpu_custom_call" | custom-call | tf_op jit(solution)/shard_map/pallas_call | solution.py:289
  65.7 11.6 %all_to_all.32.refs_0_ = bf16[16,16,128]{2,1,0:T(8,128)(2,1)S(1)} all-to-all(bf16[16,16,128]{2,1,0:T(8,128)(2,1)S(1)} %get-tuple-element.26), channel_id=1, replica_groups=mesh['mode'=16,'mer'=32] {'mode'}, dimensions={0} | all-to-all | bytes 131072 | tf_op jit(solution)/shard_map/all_to_all | solution.py:346
  77.3 0.5 shard_map.118
  77.8 12.3 %all_to_all.33.refs_2_ = bf16[16,32,128]{2,1,0:T(8,128)(2,1)S(1)} all-to-all(bf16[16,32,128]{2,1,0:T(8,128)(2,1)S(1)} %shard_map.118), channel_id=1, replica_groups=mesh['mode'=16,'mer'=32] {'mode'}, dimensions={0} | all-to-all | bytes 262144 | tf_op jit(solution)/shard_map/all_to_all | solution.py:350
  90.1 5.7 %collective-permute-start.3 = (bf16[16,32,128]{2,1,0:T(8,128)(2,1)S(1)}, bf16[16,32,128]{2,1,0:T(8,128)(2,1)S(1)}, u32[]{:S(2)}, u32[]{:S(2)}) collective-permute-start(bf16[16,32,128]{2,1,0:T(8,128)(2,1)S(1)} %all_to_all.33.refs_2_), channel_id=1, source_target_pairs={{1,2},{2,1},{3,4},{4,3},{5,6},{6,5},{7,8},{8,7},{9,10},{10,9},{11,... | collective-permute-start | bytes 393224 | tf_op jit(solution)/shard_map/ppermute | solution.py:352
  95.8 1.9 %collective-permute-start.2 = (bf16[16,32,128]{2,1,0:T(8,128)(2,1)S(1)}, bf16[16,32,128]{2,1,0:T(8,128)(2,1)S(1)}, u32[]{:S(2)}, u32[]{:S(2)}) collective-permute-start(bf16[16,32,128]{2,1,0:T(8,128)(2,1)S(1)} %all_to_all.33.refs_2_), channel_id=1, source_target_pairs={{0,1},{1,0},{2,3},{3,2},{4,5},{5,4},{6,7},{7,6},{8,9},{9,8},{10,11... | collective-permute-start | bytes 393224 | tf_op jit(solution)/shard_map/ppermute | solution.py:351
  97.7 7.6 %all-to-all-start.5 = ((bf16[32,8,128]{2,1,0:T(8,128)(2,1)}), bf16[32,8,128]{2,1,0:T(8,128)(2,1)S(1)}, u32[]{:S(2)}, u32[]{:S(2)}) async-start(bf16[32,8,128]{2,1,0:T(8,128)(2,1)} %get-tuple-element.28), calls=%async_computation.5 | async-start | bytes 131072 | tf_op jit(solution)/shard_map/all_to_all | solution.py:353
  105.4 0.0 collective-permute-done.3.refs_4_
  105.4 0.0 collective-permute-done.2.refs_3_
  105.4 2.3 %shard_map.119.refs_2_ = f32[48,512]{1,0:T(8,128)S(1)} custom-call(s32[1]{0:T(128)} %bitcast.2.refs_0_, f32[6,8,512]{2,1,0:T(8,128)S(1)} %get-tuple-element.25.refs_1_, bf16[16,32,128]{2,1,0:T(8,128)(2,1)S(1)} %all_to_all.33.refs_2_, bf16[16,32,128]{2,1,0:T(8,128)(2,1)S(1)} %collective-permute-done.2.refs_3_, ...), custom_call_target="tpu_custom_call" | custom-call | tf_op jit(solution)/shard_map/pallas_call | solution.py:289
  107.8 6.0 %all-to-all-done.5.refs_3_ = bf16[32,8,128]{2,1,0:T(8,128)(2,1)S(1)} async-done(((bf16[32,8,128]{2,1,0:T(8,128)(2,1)}), bf16[32,8,128]{2,1,0:T(8,128)(2,1)S(1)}, u32[]{:S(2)}, u32[]{:S(2)}) %all-to-all-start.5) | async-done | bytes 65568 | tf_op jit(solution)/shard_map/all_to_all | solution.py:353
  113.7 3.6 %shard_map.120 = (f32[6,8,512]{2,1,0:T(8,128)}, f32[2,8,2,64]{3,2,1,0:T(2,128)}) custom-call(s32[1]{0:T(128)} %bitcast.refs_0_, f32[6,8,512]{2,1,0:T(8,128)S(1)} %get-tuple-element.25.refs_1_, f32[48,512]{1,0:T(8,128)S(1)} %shard_map.119.refs_2_, bf16[32,8,128]{2,1,0:T(8,128)(2,1)S(1)} %all-to-all-done.5.refs_3_, s32[1,64]{1,0:T(1,128)} %bitcast.16, ...), custom_call_target="tpu_custom_call" | custom-call | tf_op jit(solution)/shard_map/pallas_call | solution.py:289
Async XLA Ops:
  37.4 20.6 %collective-permute-start.1 = (bf16[16,32,128]{2,1,0:T(8,128)(2,1)S(1)}, bf16[16,32,128]{2,1,0:T(8,128)(2,1)S(1)}, u32[]{:S(2)}, u32[]{:S(2)}) collective-permute-start(bf16[16,32,128]{2,1,0:T(8,128)(2,1)S(1)} %all_to_all.31.refs_3_.refs_2_), channel_id=1, source_target_pairs={{1,2},{2,1},{3,4},{4,3},{5,6},{6,5},{7,8},{8,7},{9,10},{10,9},{11,... | collective-permute-start | bytes 393224 | tf_op jit(solution)/shard_map/ppermute | solution.py:352
  43.3 14.8 %collective-permute-start = (bf16[16,32,128]{2,1,0:T(8,128)(2,1)S(1)}, bf16[16,32,128]{2,1,0:T(8,128)(2,1)S(1)}, u32[]{:S(2)}, u32[]{:S(2)}) collective-permute-start(bf16[16,32,128]{2,1,0:T(8,128)(2,1)S(1)} %all_to_all.31.refs_3_.refs_2_), channel_id=1, source_target_pairs={{0,1},{1,0},{2,3},{3,2},{4,5},{5,4},{6,7},{7,6},{8,9},{9,8},{10,11... | collective-permute-start | bytes 393224 | tf_op jit(solution)/shard_map/ppermute | solution.py:351
  45.2 16.7 %all-to-all-start.2 = ((bf16[32,8,128]{2,1,0:T(8,128)(2,1)}), bf16[32,8,128]{2,1,0:T(8,128)(2,1)S(1)}, u32[]{:S(2)}, u32[]{:S(2)}) async-start(bf16[32,8,128]{2,1,0:T(8,128)(2,1)} %get-tuple-element.24), calls=%async_computation.2 | async-start | bytes 131072 | tf_op jit(solution)/shard_map/all_to_all | solution.py:353
  90.1 15.3 %collective-permute-start.3 = (bf16[16,32,128]{2,1,0:T(8,128)(2,1)S(1)}, bf16[16,32,128]{2,1,0:T(8,128)(2,1)S(1)}, u32[]{:S(2)}, u32[]{:S(2)}) collective-permute-start(bf16[16,32,128]{2,1,0:T(8,128)(2,1)S(1)} %all_to_all.33.refs_2_), channel_id=1, source_target_pairs={{1,2},{2,1},{3,4},{4,3},{5,6},{6,5},{7,8},{8,7},{9,10},{10,9},{11,... | collective-permute-start | bytes 393224 | tf_op jit(solution)/shard_map/ppermute | solution.py:352
  95.8 9.6 %collective-permute-start.2 = (bf16[16,32,128]{2,1,0:T(8,128)(2,1)S(1)}, bf16[16,32,128]{2,1,0:T(8,128)(2,1)S(1)}, u32[]{:S(2)}, u32[]{:S(2)}) collective-permute-start(bf16[16,32,128]{2,1,0:T(8,128)(2,1)S(1)} %all_to_all.33.refs_2_), channel_id=1, source_target_pairs={{0,1},{1,0},{2,3},{3,2},{4,5},{5,4},{6,7},{7,6},{8,9},{9,8},{10,11... | collective-permute-start | bytes 393224 | tf_op jit(solution)/shard_map/ppermute | solution.py:351
  97.7 16.0 %all-to-all-start.5 = ((bf16[32,8,128]{2,1,0:T(8,128)(2,1)}), bf16[32,8,128]{2,1,0:T(8,128)(2,1)S(1)}, u32[]{:S(2)}, u32[]{:S(2)}) async-start(bf16[32,8,128]{2,1,0:T(8,128)(2,1)} %get-tuple-element.28), calls=%async_computation.5 | async-start | bytes 131072 | tf_op jit(solution)/shard_map/all_to_all | solution.py:353

commit v6 on v5

--- a/solution.py
+++ b/solution.py
@@ -74,7 +74,7 @@
 
 def trace_rows(rows, onehot):
     both = nn(rows, onehot)
-    return jnp.where(low_lanes((8, 128)), both[:8], both[8:]).astype(BF)
+    return jnp.where(low_lanes((8, 128)), both[:8], both[8:])
 
 
 def low_lanes(shape):
@@ -131,18 +131,8 @@
         ]
         picks = jnp.concatenate(picks, 0)
         for k, mat in enumerate(mats):
-            work_ref[k, 256 * u : 256 * u + 256] = nn(mat, picks).astype(BF)
-    return nn(tall_ref[...], work_ref[0]), nn(tall_ref[...], work_ref[1])
-
-
-def own_kernel(stiff, curl, conn, emf_ref, near_out, near_ref, tall_ref, work_ref, sem):
-    conn = two_by_two(conn()).astype(F32)
-    s, c = operators(conn, 0.0, 512, stiff(), curl(), tall_ref, work_ref)
-    near_ref[:768] = c.astype(BF)
-    near_ref[768:] = s.astype(BF)
-    copy = pltpu.make_async_copy(near_ref, near_out, sem)
-    copy.start()
-    copy.wait()
+            work_ref[k, 256 * u : 256 * u + 256, :width] = nn(mat, picks).astype(BF)
+    return [nn(tall_ref[...], work_ref[k, :, :width]) for k in range(2)]
 
 
 def induce_kernel(moved_ref, mark_ref, va_ref, vb_ref, fwd_ref, inv_ref, out_ref):
@@ -182,22 +172,27 @@
     return jnp.concatenate([total[:, :256] + low, total[:, 256:]], 1)
 
 
-def first_operator_kernel(mer_ref, now, emf_ref, pa_ref, pb_ref, near, stiff, curl, *refs):
-    out_ref, far_out, far_ref, tall_ref, work_ref, conn_ref, sem = refs
+def first_operator_kernel(mer_ref, now, emf_ref, pa_ref, pb_ref, conn, stiff, curl, *refs):
+    out_ref, near_out, far_out, near_ref, far_ref, tall_ref, work_ref, conn_ref, sems = refs
     tile = side(mer_ref, pa_ref, pb_ref, 0, 0)
     code = [pltpu.roll(tile(s).astype(F32), 32 + 32 * (s % 2), 1) for s in range(4)]
     first = lane_group((16, 128)) == 0
     conn_ref[...] = 32.0 * jnp.where(first, code[0], code[1]) + jnp.where(first, code[2], code[3])
-    conn = [conn_ref[pl.ds(k, 8, 2), :] for k in range(2)]
-    conn = jnp.where(low_lanes((8, 128)), conn[0], pltpu.roll(conn[1], 64, 1))
-    s, c = operators(conn, 512.0, 256, stiff(), curl(), tall_ref, work_ref)
-    there = jnp.where(mer_ref[0] > 0, 1.0, 0.0)
-    far_ref[:768] = (c * there).astype(BF)
-    far_ref[768:] = (s * there).astype(BF)
-    copy = pltpu.make_async_copy(far_ref, far_out, sem)
-    copy.start()
-    out_ref[...] = operator_rows(mer_ref, now, emf_ref, pa_ref, pb_ref, near, lambda: far_ref)
-    copy.wait()
+    there = [conn_ref[pl.ds(k, 8, 2), :] for k in range(2)]
+    there = jnp.where(low_lanes((8, 128)), there[0], pltpu.roll(there[1], 64, 1))
+    here = two_by_two(conn()).astype(F32)
+    has = jnp.where(mer_ref[0] > 0, 1.0, 0.0)
+    jobs = ((here, 0.0, 512, near_ref, near_out, 1.0), (there, 512.0, 256, far_ref, far_out, has))
+    copies = []
+    for conn, start, width, ref, out, gain in jobs:
+        s, c = operators(conn, start, width, stiff(), curl(), tall_ref, work_ref)
+        ref[:768] = (c * gain).astype(BF)
+        ref[768:] = (s * gain).astype(BF)
+        copies.append(pltpu.make_async_copy(ref, out, sems.at[len(copies)]))
+        copies[-1].start()
+    out_ref[...] = operator_rows(mer_ref, now, emf_ref, pa_ref, pb_ref, lambda: near_ref, lambda: far_ref)
+    for copy in copies:
+        copy.wait()
 
 
 def operator_kernel(mer_ref, now, emf_ref, pa_ref, pb_ref, near, far, out_ref):
@@ -212,7 +207,7 @@
     low = low_lanes((8, 128))
     parts = [], []
     for a in range(whole_ref.shape[0] // 2):
-        x, y = whole_ref[2 * a].astype(F32), whole_ref[2 * a + 1].astype(F32)
+        x, y = whole_ref[2 * a], whole_ref[2 * a + 1]
         parts[0].append(jnp.where(low, x, pltpu.roll(y, 64, 1)))
         parts[1].append(jnp.where(low, pltpu.roll(x, 64, 1), y))
     whole = jnp.concatenate([jnp.concatenate(p, 1) for p in parts], 0).astype(BF)
@@ -324,18 +319,10 @@
     row = mass.reshape(1, 512)
     chunk = ((16, 16, 128), BF, near_space)
 
-    def works(rows, width):
-        return [
-            pltpu.VMEM((rows, width), BF),
-            pltpu.VMEM((768, 1024), BF),
-            pltpu.VMEM((2, 1024, width), BF),
-            pltpu.SemaphoreType.DMA,
-        ]
-
     table = [((256, 128), BF, near_space)] * 2 + [((256, 256), BF, near_space)] * 2
     packed, trace, *table = call(
         open_kernel,
-        [chunk, ((spots, 8, 128), BF, near_space), ((16, 128), F32, near_space), *table],
+        [chunk, ((spots, 8, 128), F32, near_space), ((16, 128), F32, near_space), *table],
         "scccccc",
         (mode, start, wall, connect, jnp.transpose(velocity, (0, 2, 1)), fwd, inv),
     )
@@ -354,24 +341,24 @@
 
     rows = ((48, 512), F32, near_space)
     emf, e_twin, e_other, whole = exchange(packed, trace)
-    (near,) = call(
-        own_kernel,
-        [((1536, 512), BF, far_space)],
-        "cccv",
-        (stiffness, curl_matrix, connect, emf),
-        works(1536, 512),
+    works = [
+        pltpu.VMEM((1536, 512), BF),
+        pltpu.VMEM((1536, 256), BF),
+        pltpu.VMEM((768, 1024), BF),
+        pltpu.VMEM((2, 1024, 512), BF),
+        pltpu.VMEM((16, 128), F32),
+        pltpu.SemaphoreType.DMA((2,)),
+    ]
+    total, near, far = call(
+        first_operator_kernel,
+        [rows, ((1536, 512), BF, far_space), ((1536, 256), BF, far_space)],
+        "scvvvccc",
+        (mer, start, emf, e_twin, e_other, connect, stiffness, curl_matrix),
+        works,
         32,
     )
-    total, far = call(
-        first_operator_kernel,
-        [rows, ((1536, 256), BF, far_space)],
-        "scvvvccc",
-        (mer, start, emf, e_twin, e_other, near, stiffness, curl_matrix),
-        [*works(1536, 256)[:3], pltpu.VMEM((16, 128), F32), pltpu.SemaphoreType.DMA],
-        32,
-    )
     out = [((6, 8, 512), F32, near_space), chunk]
-    out += [((spots, 8, 128), BF, near_space), ((16, 128), F32, near_space)]
+    out += [((spots, 8, 128), F32, near_space), ((16, 128), F32, near_space)]
     sect, packed, trace, flux = call(
         first_kernel, out, "scvvccd", (mode, start, total, whole, wall, row, dtn)
     )

time: 118 us -> 116 us (0.983)
  waiting for transfers between devices: 5.97 us -> 3.97 us
  Pallas kernels: 20.9 us -> 19.1 us
  starting transfers between devices: 31.2 us -> 32.8 us
    all_to_all x2, starting transfers between devices: 15.8 us -> 21.9 us  [exchange(): lax.all_to_all(trace, 'mer', 0, 0, tiled=True)]
    all_to_all x2, waiting for transfers between devices: 5.96 us -> 0.01 us  [exchange(): lax.all_to_all(trace, 'mer', 0, 0, tiled=True)]
    ppermute x2, starting transfers between devices: 11.6 us -> 7.08 us  [exchange(): e_other = lax.ppermute(emf, 'mer', others)]
    ppermute x2, waiting for transfers between devices: 0.01 us -> 3.96 us  [exchange(): e_other = lax.ppermute(emf, 'mer', others)]
    pallas_call x8 -> x7, Pallas kernels: 20.9 us -> 19.1 us  [call(): pl.pallas_call(run, out_shape=[space(s, d) if space else jax.ShapeDtypeSt...]
  transfers between devices with their start and end apart: 6 -> 6, of which waited for: 1 -> 2; matrix products, arithmetic and copies ran while one was open for 0% -> 0% of each run, Pallas kernels for 9% -> 8%
where the time goes in v6:
time: 116 us; the launch traced here: 115 us
  blocking collectives  58.8 us (51%)
  starting transfers between devices  32.8 us (28%)
  Pallas kernels  19.1 us (16%)
  waiting for transfers between devices  3.97 us (3%)
    all_to_all x2, blocking collectives, exchange(): moved = lax.all_to_all(packed, 'mode', 0, 0, tiled=True)  34.6 us
    all_to_all x2, blocking collectives, exchange(): emf = lax.all_to_all(back, 'mode', 0, 0, tiled=True)  24.2 us
    all_to_all x2, starting transfers between devices, exchange(): lax.all_to_all(trace, 'mer', 0, 0, tiled=True)  21.9 us
    pallas_call x7, Pallas kernels, call(): pl.pallas_call(run, out_shape=[space(s, d) if space else jax.ShapeDtypeSt...  19.1 us
    ppermute x2, starting transfers between devices, exchange(): e_other = lax.ppermute(emf, 'mer', others)  7.08 us
    ppermute x2, waiting for transfers between devices, exchange(): e_other = lax.ppermute(emf, 'mer', others)  3.96 us
    ppermute x2, starting transfers between devices, exchange(): e_twin = lax.ppermute(emf, 'mer', twins)  3.84 us
  transfers between devices with their start and end apart: 6, of which 2 were waited for; matrix products, arithmetic and copies ran while one was open for 0% of the time, Pallas kernels for 8%

profile of v6, /device:TPU:1, one launch (start us, length us, event | category | flops | bytes accessed | tf_op | source)
XLA Modules:
  0.0 115.4 jit_solution(2659753520721466721)
XLA Ops:
  0.6 1.9 %shard_map.113 = (bf16[16,16,128]{2,1,0:T(8,128)(2,1)S(1)}, f32[32,8,128]{2,1,0:T(8,128)}, f32[16,128]{1,0:T(8,128)S(1)}, bf16[256,128]{1,0:T(8,128)(2,1)S(1)}, ...) custom-call(s32[1]{0:T(128)} %bitcast.refs_0_, f32[6,8,512]{2,1,0:T(8,128)} %bitcast.7, ...), custom_call_target="tpu_custom_call" | custom-call | tf_op jit(solution)/shard_map/pallas_call | solution.py:284
  2.5 22.2 %all_to_all.30.refs_0_ = bf16[16,16,128]{2,1,0:T(8,128)(2,1)S(1)} all-to-all(bf16[16,16,128]{2,1,0:T(8,128)(2,1)S(1)} %get-tuple-element.18), channel_id=1, replica_groups=mesh['mode'=16,'mer'=32] {'mode'}, dimensions={0} | all-to-all | bytes 131072 | tf_op jit(solution)/shard_map/all_to_all | solution.py:333
  24.7 0.5 shard_map.114
  25.2 12.3 %all_to_all.31.refs_2_ = bf16[16,32,128]{2,1,0:T(8,128)(2,1)S(1)} all-to-all(bf16[16,32,128]{2,1,0:T(8,128)(2,1)S(1)} %shard_map.114), channel_id=1, replica_groups=mesh['mode'=16,'mer'=32] {'mode'}, dimensions={0} | all-to-all | bytes 262144 | tf_op jit(solution)/shard_map/all_to_all | solution.py:337
  37.4 11.1 %all-to-all-start.2 = ((f32[32,8,128]{2,1,0:T(8,128)}), f32[32,8,128]{2,1,0:T(8,128)S(1)}, u32[]{:S(2)}, u32[]{:S(2)}) async-start(f32[32,8,128]{2,1,0:T(8,128)} %get-tuple-element.25), calls=%async_computation.2 | async-start | bytes 262144 | tf_op jit(solution)/shard_map/all_to_all | solution.py:340
  48.5 3.5 %collective-permute-start.1 = (bf16[16,32,128]{2,1,0:T(8,128)(2,1)S(1)}, bf16[16,32,128]{2,1,0:T(8,128)(2,1)S(1)}, u32[]{:S(2)}, u32[]{:S(2)}) collective-permute-start(bf16[16,32,128]{2,1,0:T(8,128)(2,1)S(1)} %all_to_all.31.refs_2_), channel_id=1, source_target_pairs={{1,2},{2,1},{3,4},{4,3},{5,6},{6,5},{7,8},{8,7},{9,10},{10,9},{11,... | collective-permute-start | bytes 393224 | tf_op jit(solution)/shard_map/ppermute | solution.py:339
  52.1 1.9 %collective-permute-start = (bf16[16,32,128]{2,1,0:T(8,128)(2,1)S(1)}, bf16[16,32,128]{2,1,0:T(8,128)(2,1)S(1)}, u32[]{:S(2)}, u32[]{:S(2)}) collective-permute-start(bf16[16,32,128]{2,1,0:T(8,128)(2,1)S(1)} %all_to_all.31.refs_2_), channel_id=1, source_target_pairs={{0,1},{1,0},{2,3},{3,2},{4,5},{5,4},{6,7},{7,6},{8,9},{9,8},{10,11... | collective-permute-start | bytes 393224 | tf_op jit(solution)/shard_map/ppermute | solution.py:338
  54.0 2.0 %collective-permute-done.1.refs_4_ = bf16[16,32,128]{2,1,0:T(8,128)(2,1)S(1)} collective-permute-done((bf16[16,32,128]{2,1,0:T(8,128)(2,1)S(1)}, bf16[16,32,128]{2,1,0:T(8,128)(2,1)S(1)}, u32[]{:S(2)}, u32[]{:S(2)}) %collective-permute-start.1) | collective-permute-done | bytes 131104 | tf_op jit(solution)/shard_map/ppermute | solution.py:339
  56.0 0.0 collective-permute-done.refs_3_
  56.0 6.6 %shard_map.115 = (f32[48,512]{1,0:T(8,128)S(1)}, bf16[1536,512]{1,0:T(8,128)(2,1)}, bf16[1536,256]{1,0:T(8,128)(2,1)}) custom-call(s32[1]{0:T(128)} %bitcast.2.refs_0_, f32[6,8,512]{2,1,0:T(8,128)} %bitcast.8, bf16[16,32,128]{2,1,0:T(8,128)(2,1)S(1)} %all_to_all.31.refs_2_, bf16[16,32,128]{2,1,0:T(8,128)(2,1)S(1)} %collective-permute-done.refs_3_, ...), custom_call_target="tpu_custom_call" | custom-call | tf_op jit(solution)/shard_map/pallas_call | solution.py:284
  62.6 0.0 all-to-all-done.2.refs_3_
  62.6 3.7 %shard_map.116 = (f32[6,8,512]{2,1,0:T(8,128)S(1)}, bf16[16,16,128]{2,1,0:T(8,128)(2,1)S(1)}, f32[32,8,128]{2,1,0:T(8,128)}, f32[16,128]{1,0:T(8,128)S(1)}) custom-call(s32[1]{0:T(128)} %bitcast.refs_0_, f32[6,8,512]{2,1,0:T(8,128)} %bitcast.9, f32[48,512]{1,0:T(8,128)S(1)} %get-tuple-element.24.refs_2_, f32[32,8,128]{2,1,0:T(8,128)S(1)} %all-to-all-done.2.refs_3_, ...), custom_call_target="tpu_custom_call" | custom-call | tf_op jit(solution)/shard_map/pallas_call | solution.py:284
  66.4 12.4 %all_to_all.32.refs_0_ = bf16[16,16,128]{2,1,0:T(8,128)(2,1)S(1)} all-to-all(bf16[16,16,128]{2,1,0:T(8,128)(2,1)S(1)} %get-tuple-element.27), channel_id=1, replica_groups=mesh['mode'=16,'mer'=32] {'mode'}, dimensions={0} | all-to-all | bytes 131072 | tf_op jit(solution)/shard_map/all_to_all | solution.py:333
  78.7 0.5 shard_map.117
  79.2 11.9 %all_to_all.33.refs_2_ = bf16[16,32,128]{2,1,0:T(8,128)(2,1)S(1)} all-to-all(bf16[16,32,128]{2,1,0:T(8,128)(2,1)S(1)} %shard_map.117), channel_id=1, replica_groups=mesh['mode'=16,'mer'=32] {'mode'}, dimensions={0} | all-to-all | bytes 262144 | tf_op jit(solution)/shard_map/all_to_all | solution.py:337
  91.1 10.8 %all-to-all-start.5 = ((f32[32,8,128]{2,1,0:T(8,128)}), f32[32,8,128]{2,1,0:T(8,128)S(1)}, u32[]{:S(2)}, u32[]{:S(2)}) async-start(f32[32,8,128]{2,1,0:T(8,128)} %get-tuple-element.30), calls=%async_computation.5 | async-start | bytes 262144 | tf_op jit(solution)/shard_map/all_to_all | solution.py:340
  102.0 3.5 %collective-permute-start.3 = (bf16[16,32,128]{2,1,0:T(8,128)(2,1)S(1)}, bf16[16,32,128]{2,1,0:T(8,128)(2,1)S(1)}, u32[]{:S(2)}, u32[]{:S(2)}) collective-permute-start(bf16[16,32,128]{2,1,0:T(8,128)(2,1)S(1)} %all_to_all.33.refs_2_), channel_id=1, source_target_pairs={{1,2},{2,1},{3,4},{4,3},{5,6},{6,5},{7,8},{8,7},{9,10},{10,9},{11,... | collective-permute-start | bytes 393224 | tf_op jit(solution)/shard_map/ppermute | solution.py:339
  105.5 1.9 %collective-permute-start.2 = (bf16[16,32,128]{2,1,0:T(8,128)(2,1)S(1)}, bf16[16,32,128]{2,1,0:T(8,128)(2,1)S(1)}, u32[]{:S(2)}, u32[]{:S(2)}) collective-permute-start(bf16[16,32,128]{2,1,0:T(8,128)(2,1)S(1)} %all_to_all.33.refs_2_), channel_id=1, source_target_pairs={{0,1},{1,0},{2,3},{3,2},{4,5},{5,4},{6,7},{7,6},{8,9},{9,8},{10,11... | collective-permute-start | bytes 393224 | tf_op jit(solution)/shard_map/ppermute | solution.py:338
  107.5 2.0 %collective-permute-done.3.refs_4_ = bf16[16,32,128]{2,1,0:T(8,128)(2,1)S(1)} collective-permute-done((bf16[16,32,128]{2,1,0:T(8,128)(2,1)S(1)}, bf16[16,32,128]{2,1,0:T(8,128)(2,1)S(1)}, u32[]{:S(2)}, u32[]{:S(2)}) %collective-permute-start.3) | collective-permute-done | bytes 131104 | tf_op jit(solution)/shard_map/ppermute | solution.py:339
  109.4 0.0 collective-permute-done.2.refs_3_
  109.4 2.3 %shard_map.118.refs_2_ = f32[48,512]{1,0:T(8,128)S(1)} custom-call(s32[1]{0:T(128)} %bitcast.2.refs_0_, f32[6,8,512]{2,1,0:T(8,128)S(1)} %get-tuple-element.26.refs_1_, bf16[16,32,128]{2,1,0:T(8,128)(2,1)S(1)} %all_to_all.33.refs_2_, bf16[16,32,128]{2,1,0:T(8,128)(2,1)S(1)} %collective-permute-done.2.refs_3_, ...), custom_call_target="tpu_custom_call" | custom-call | tf_op jit(solution)/shard_map/pallas_call | solution.py:284
  111.8 0.0 all-to-all-done.5.refs_3_
  111.8 3.6 %shard_map.119 = (f32[6,8,512]{2,1,0:T(8,128)}, f32[2,8,2,64]{3,2,1,0:T(2,128)}) custom-call(s32[1]{0:T(128)} %bitcast.refs_0_, f32[6,8,512]{2,1,0:T(8,128)S(1)} %get-tuple-element.26.refs_1_, f32[48,512]{1,0:T(8,128)S(1)} %shard_map.118.refs_2_, f32[32,8,128]{2,1,0:T(8,128)S(1)} %all-to-all-done.5.refs_3_, s32[1,64]{1,0:T(1,128)} %bitcast.16, ...), custom_call_target="tpu_custom_call" | custom-call | tf_op jit(solution)/shard_map/pallas_call | solution.py:284
Async XLA Ops:
  37.4 25.2 %all-to-all-start.2 = ((f32[32,8,128]{2,1,0:T(8,128)}), f32[32,8,128]{2,1,0:T(8,128)S(1)}, u32[]{:S(2)}, u32[]{:S(2)}) async-start(f32[32,8,128]{2,1,0:T(8,128)} %get-tuple-element.25), calls=%async_computation.2 | async-start | bytes 262144 | tf_op jit(solution)/shard_map/all_to_all | solution.py:340
  48.5 7.5 %collective-permute-start.1 = (bf16[16,32,128]{2,1,0:T(8,128)(2,1)S(1)}, bf16[16,32,128]{2,1,0:T(8,128)(2,1)S(1)}, u32[]{:S(2)}, u32[]{:S(2)}) collective-permute-start(bf16[16,32,128]{2,1,0:T(8,128)(2,1)S(1)} %all_to_all.31.refs_2_), channel_id=1, source_target_pairs={{1,2},{2,1},{3,4},{4,3},{5,6},{6,5},{7,8},{8,7},{9,10},{10,9},{11,... | collective-permute-start | bytes 393224 | tf_op jit(solution)/shard_map/ppermute | solution.py:339
  52.1 3.9 %collective-permute-start = (bf16[16,32,128]{2,1,0:T(8,128)(2,1)S(1)}, bf16[16,32,128]{2,1,0:T(8,128)(2,1)S(1)}, u32[]{:S(2)}, u32[]{:S(2)}) collective-permute-start(bf16[16,32,128]{2,1,0:T(8,128)(2,1)S(1)} %all_to_all.31.refs_2_), channel_id=1, source_target_pairs={{0,1},{1,0},{2,3},{3,2},{4,5},{5,4},{6,7},{7,6},{8,9},{9,8},{10,11... | collective-permute-start | bytes 393224 | tf_op jit(solution)/shard_map/ppermute | solution.py:338
  91.1 20.7 %all-to-all-start.5 = ((f32[32,8,128]{2,1,0:T(8,128)}), f32[32,8,128]{2,1,0:T(8,128)S(1)}, u32[]{:S(2)}, u32[]{:S(2)}) async-start(f32[32,8,128]{2,1,0:T(8,128)} %get-tuple-element.30), calls=%async_computation.5 | async-start | bytes 262144 | tf_op jit(solution)/shard_map/all_to_all | solution.py:340
  102.0 7.5 %collective-permute-start.3 = (bf16[16,32,128]{2,1,0:T(8,128)(2,1)S(1)}, bf16[16,32,128]{2,1,0:T(8,128)(2,1)S(1)}, u32[]{:S(2)}, u32[]{:S(2)}) collective-permute-start(bf16[16,32,128]{2,1,0:T(8,128)(2,1)S(1)} %all_to_all.33.refs_2_), channel_id=1, source_target_pairs={{1,2},{2,1},{3,4},{4,3},{5,6},{6,5},{7,8},{8,7},{9,10},{10,9},{11,... | collective-permute-start | bytes 393224 | tf_op jit(solution)/shard_map/ppermute | solution.py:339
  105.5 3.9 %collective-permute-start.2 = (bf16[16,32,128]{2,1,0:T(8,128)(2,1)S(1)}, bf16[16,32,128]{2,1,0:T(8,128)(2,1)S(1)}, u32[]{:S(2)}, u32[]{:S(2)}) collective-permute-start(bf16[16,32,128]{2,1,0:T(8,128)(2,1)S(1)} %all_to_all.33.refs_2_), channel_id=1, source_target_pairs={{0,1},{1,0},{2,3},{3,2},{4,5},{5,4},{6,7},{7,6},{8,9},{9,8},{10,11... | collective-permute-start | bytes 393224 | tf_op jit(solution)/shard_map/ppermute | solution.py:338

commit v7 on v6

--- a/solution.py
+++ b/solution.py
@@ -66,15 +66,11 @@
     return jnp.concatenate(cols, 1)
 
 
-def wall_onehot(wall_ref):
+def wall_onehot(wall_ref, mer):
     twice = jnp.concatenate([wall_ref[...], wall_ref[...]], 1)
     nodes = lax.broadcasted_iota(jnp.int32, (512, 128), 0)
-    return (nodes == twice).astype(F32).astype(BF)
-
-
-def trace_rows(rows, onehot):
-    both = nn(rows, onehot)
-    return jnp.where(low_lanes((8, 128)), both[:8], both[8:])
+    half = lax.broadcasted_iota(jnp.int32, (512, 128), 1) // 64
+    return jnp.where(half == mer % 2, (nodes == twice).astype(F32), 0.0).astype(BF)
 
 
 def low_lanes(shape):
@@ -85,12 +81,12 @@
     return jnp.concatenate([conn_ref[pl.ds(0, 8, 2), :], conn_ref[pl.ds(1, 8, 2), :]], 1)
 
 
-def open_kernel(mode_ref, field, wall, conn, vel, fwd, inv, pack_ref, out_ref, mark_ref, va_ref, vb_ref, fwd_ref, inv_ref):
-    onehot = wall_onehot(wall())
+def open_kernel(mode_ref, mer_ref, field, wall, conn, vel, fwd, inv, pack_ref, out_ref, mark_ref, va_ref, vb_ref, fwd_ref, inv_ref):
+    onehot = wall_onehot(wall(), mer_ref[0])
     conn = conn()[...]
     field_ref = field()
     pack({(c, p): field_ref[3 * p + c] for c in range(3) for p in range(2)}, pack_ref)
-    tr = trace_rows(jnp.concatenate([field_ref[2], field_ref[5]], 0).astype(BF), onehot)
+    tr = nn(jnp.concatenate([field_ref[2], field_ref[5]], 0).astype(BF), onehot).astype(BF)
     for j in range(out_ref.shape[0]):
         out_ref[j] = tr
     part = jnp.zeros((16, 64), jnp.int32) + mode_ref[0] % 4
@@ -172,8 +168,10 @@
     return jnp.concatenate([total[:, :256] + low, total[:, 256:]], 1)
 
 
-def first_operator_kernel(mer_ref, now, emf_ref, pa_ref, pb_ref, conn, stiff, curl, *refs):
-    out_ref, near_out, far_out, near_ref, far_ref, tall_ref, work_ref, conn_ref, sems = refs
+def first_operator_kernel(mer_ref, now, emf_ref, pa_ref, pb_ref, conn, stiff, curl, dtn_ref, *refs):
+    out_ref, half_ref, near_out, far_out, near_ref, far_ref, tall_ref, work_ref, conn_ref, sems = refs
+    bring = pltpu.make_async_copy(dtn_ref.at[pl.ds(0, 4)], half_ref, sems.at[2])
+    bring.start()
     tile = side(mer_ref, pa_ref, pb_ref, 0, 0)
     code = [pltpu.roll(tile(s).astype(F32), 32 + 32 * (s % 2), 1) for s in range(4)]
     first = lane_group((16, 128)) == 0
@@ -191,33 +189,31 @@
         copies.append(pltpu.make_async_copy(ref, out, sems.at[len(copies)]))
         copies[-1].start()
     out_ref[...] = operator_rows(mer_ref, now, emf_ref, pa_ref, pb_ref, lambda: near_ref, lambda: far_ref)
-    for copy in copies:
+    for copy in [*copies, bring]:
         copy.wait()
 
 
-def operator_kernel(mer_ref, now, emf_ref, pa_ref, pb_ref, near, far, out_ref):
+def operator_kernel(mer_ref, now, emf_ref, pa_ref, pb_ref, near, far, dtn_ref, out_ref, half_ref, sem):
+    bring = pltpu.make_async_copy(dtn_ref.at[pl.ds(0, 4)], half_ref, sem)
+    bring.start()
     out_ref[...] = operator_rows(mer_ref, now, emf_ref, pa_ref, pb_ref, near, far)
-
-
-def finish(mode_ref, now, total_ref, whole_ref, wall, mass, dtn):
-    onehot = wall_onehot(wall())
+    bring.wait()
+
+
+def finish(mode_ref, mer_ref, now, total_ref, whole_ref, wall, mass, half_ref, dtn):
+    whole = jnp.concatenate([whole_ref[2 * a] + whole_ref[2 * a + 1] for a in range(16)], 1)
+    every = [nt(whole, half_ref[2 * k : 2 * k + 2].reshape(128, 2048)) for k in range(2)]
+    onehot = wall_onehot(wall(), mer_ref[0])
     field = rows_of(now)
     number = lax.broadcasted_iota(jnp.int32, (48, 512), 0) % 8 + 8 * mode_ref[0]
     coef = (number.astype(F32) / 128.0) ** 2
-    low = low_lanes((8, 128))
-    parts = [], []
-    for a in range(whole_ref.shape[0] // 2):
-        x, y = whole_ref[2 * a], whole_ref[2 * a + 1]
-        parts[0].append(jnp.where(low, x, pltpu.roll(y, 64, 1)))
-        parts[1].append(jnp.where(low, pltpu.roll(x, 64, 1), y))
-    whole = jnp.concatenate([jnp.concatenate(p, 1) for p in parts], 0).astype(BF)
     weight = 1.0 / mass()[...]
-    every = [nt(whole, dtn(k)[2 * k : 2 * k + 2].reshape(128, 2048)) for k in range(4)]
+    every += [nt(whole, dtn(k)[2 * k : 2 * k + 2].reshape(128, 2048)) for k in range(2)]
     every = jnp.concatenate(every, 1)
     mine = lax.broadcasted_iota(jnp.int32, (16, 512), 0) % 8
     every = jnp.where(mine == lax.broadcasted_iota(jnp.int32, (16, 512), 1) // 64, every, 0.0)
     flux = every[:, :128] + every[:, 128:256] + every[:, 256:384] + every[:, 384:]
-    flux = jnp.where(low_lanes((16, 128)), flux + pltpu.roll(flux, 64, 1), 0.0)
+    flux = flux + pltpu.roll(flux, 64, 1)
     upper = flux.astype(BF)
     added = nt(upper, onehot) + nt((flux - upper.astype(F32)).astype(BF), onehot)
     total = total_ref[...]
@@ -227,22 +223,22 @@
 
 
 def first_kernel(*refs):
-    sect_ref, pack_ref, trace_ref, flux_ref = refs[7:]
-    rate, field, flux, onehot = finish(*refs[:7])
+    sect_ref, pack_ref, trace_ref, flux_ref = refs[9:]
+    rate, field, flux, onehot = finish(*refs[:9])
     sect = field + 0.2 * rate
     flux_ref[...] = flux
     rows = {(c, p): sect[16 * c + 8 * p : 16 * c + 8 * p + 8] for c in range(3) for p in range(2)}
     for (c, p), r in rows.items():
         sect_ref[3 * p + c] = r
     pack(rows, pack_ref)
-    tr = trace_rows(sect[32:].astype(BF), onehot)
+    tr = nn(sect[32:].astype(BF), onehot).astype(BF)
     for j in range(trace_ref.shape[0]):
         trace_ref[j] = tr
 
 
 def second_kernel(*refs):
-    start, first_flux_ref, out_ref, flux_ref = refs[7:]
-    rate, sect, flux, onehot = finish(*refs[:7])
+    start, first_flux_ref, out_ref, flux_ref = refs[9:]
+    rate, sect, flux, onehot = finish(*refs[:9])
     start_ref = start()
     for c in range(3):
         for p in range(2):
@@ -268,19 +264,20 @@
                 near.append(ref)
                 continue
             buf, copies = bufs.pop(0), []
-            for part in range(4 if k == "d" else 1):
-                piece = pl.ds(2 * part, 2) if k == "d" else Ellipsis
-                src, dst = (ref.at[piece], buf.at[piece]) if k == "d" else (ref, buf)
+            for part in range(2 if k == "d" else 1):
+                src, dst = ref, buf
+                if k == "d":
+                    src, dst = ref.at[pl.ds(4 + 2 * part, 2)], buf.at[pl.ds(2 * part, 2)]
                 copies.append(pltpu.make_async_copy(src, dst, sems.at[used]))
                 copies[-1].start()
                 used += 1
             near.append(later(copies, buf))
         kernel(*near, *inner[count:])
 
-    spaces = {"s": pltpu.SMEM, "v": pltpu.VMEM, "c": pltpu.HBM, "d": pltpu.HBM}
-    waits = sum(4 if k == "d" else 1 for _, k in brought)
+    spaces = {"s": pltpu.SMEM, "v": pltpu.VMEM, "c": pltpu.HBM, "d": pltpu.HBM, "h": pltpu.HBM}
+    waits = sum(2 if k == "d" else 1 for _, k in brought)
     extra = [pltpu.SemaphoreType.DMA((waits,))] if brought else []
-    extra += [pltpu.VMEM(a.shape, a.dtype) for a, _ in brought]
+    extra += [pltpu.VMEM((4,) + a.shape[1:] if k == "d" else a.shape, a.dtype) for a, k in brought]
     return pl.pallas_call(
         run,
         out_shape=[space(s, d) if space else jax.ShapeDtypeStruct(s, d) for s, d, space in out],
@@ -322,9 +319,9 @@
     table = [((256, 128), BF, near_space)] * 2 + [((256, 256), BF, near_space)] * 2
     packed, trace, *table = call(
         open_kernel,
-        [chunk, ((spots, 8, 128), F32, near_space), ((16, 128), F32, near_space), *table],
-        "scccccc",
-        (mode, start, wall, connect, jnp.transpose(velocity, (0, 2, 1)), fwd, inv),
+        [chunk, ((spots, 16, 128), BF, near_space), ((16, 128), F32, near_space), *table],
+        "sscccccc",
+        (mode, mer, start, wall, connect, jnp.transpose(velocity, (0, 2, 1)), fwd, inv),
     )
     twins = [(i, i ^ 1) for i in range(spots)]
     others = [(i, ((i + 1) ^ 1) - 1) for i in range(1, spots - 1)]
@@ -347,28 +344,36 @@
         pltpu.VMEM((768, 1024), BF),
         pltpu.VMEM((2, 1024, 512), BF),
         pltpu.VMEM((16, 128), F32),
-        pltpu.SemaphoreType.DMA((2,)),
+        pltpu.SemaphoreType.DMA((3,)),
     ]
-    total, near, far = call(
+    some = ((4, 64, 2048), BF, near_space)
+    total, half, near, far = call(
         first_operator_kernel,
-        [rows, ((1536, 512), BF, far_space), ((1536, 256), BF, far_space)],
-        "scvvvccc",
-        (mer, start, emf, e_twin, e_other, connect, stiffness, curl_matrix),
+        [rows, some, ((1536, 512), BF, far_space), ((1536, 256), BF, far_space)],
+        "scvvvccch",
+        (mer, start, emf, e_twin, e_other, connect, stiffness, curl_matrix, dtn),
         works,
         32,
     )
     out = [((6, 8, 512), F32, near_space), chunk]
-    out += [((spots, 8, 128), F32, near_space), ((16, 128), F32, near_space)]
+    out += [((spots, 16, 128), BF, near_space), ((16, 128), F32, near_space)]
     sect, packed, trace, flux = call(
-        first_kernel, out, "scvvccd", (mode, start, total, whole, wall, row, dtn)
+        first_kernel, out, "sscvvccvd", (mode, mer, start, total, whole, wall, row, half, dtn)
     )
     emf, e_twin, e_other, whole = exchange(packed, trace)
-    (total,) = call(
-        operator_kernel, [rows], "svvvvcc", (mer, sect, emf, e_twin, e_other, near, far)
+    total, half = call(
+        operator_kernel,
+        [rows, some],
+        "svvvvcch",
+        (mer, sect, emf, e_twin, e_other, near, far, dtn),
+        [pltpu.SemaphoreType.DMA],
     )
     out = [((6, 8, 512), F32, None), ((2, 8, 2, 64), F32, None)]
     done, fluxes = call(
-        second_kernel, out, "svvvccdcv", (mode, sect, total, whole, wall, row, dtn, start, flux)
+        second_kernel,
+        out,
+        "ssvvvccvdcv",
+        (mode, mer, sect, total, whole, wall, row, half, dtn, start, flux),
     )
     return (jnp.transpose(done, (1, 0, 2)), fluxes)
 

time: 116 us -> 115 us (level)
  Pallas kernels: 19.1 us -> 17.8 us
    pallas_call x7, Pallas kernels: 19.1 us -> 17.8 us  [call(): pl.pallas_call(run, out_shape=[space(s, d) if space else jax.ShapeDtypeSt...]
where the time goes in v7:
time: 115 us; the launch traced here: 114 us
  blocking collectives  58.7 us (51%)
  starting transfers between devices  32.8 us (29%)
  Pallas kernels  17.8 us (15%)
  waiting for transfers between devices  3.97 us (3%)
    all_to_all x2, blocking collectives, exchange(): moved = lax.all_to_all(packed, 'mode', 0, 0, tiled=True)  34.6 us
    all_to_all x2, blocking collectives, exchange(): emf = lax.all_to_all(back, 'mode', 0, 0, tiled=True)  24.2 us
    all_to_all x2, starting transfers between devices, exchange(): lax.all_to_all(trace, 'mer', 0, 0, tiled=True)  21.9 us
    pallas_call x7, Pallas kernels, call(): pl.pallas_call(run, out_shape=[space(s, d) if space else jax.ShapeDtypeSt...  17.8 us
    ppermute x2, starting transfers between devices, exchange(): e_other = lax.ppermute(emf, 'mer', others)  7.08 us
    ppermute x2, waiting for transfers between devices, exchange(): e_other = lax.ppermute(emf, 'mer', others)  3.96 us
    ppermute x2, starting transfers between devices, exchange(): e_twin = lax.ppermute(emf, 'mer', twins)  3.84 us
  transfers between devices with their start and end apart: 6, of which 2 were waited for; matrix products, arithmetic and copies ran while one was open for 0% of the time, Pallas kernels for 8%

profile of v7, /device:TPU:1, one launch (start us, length us, event | category | flops | bytes accessed | tf_op | source)
XLA Modules:
  0.0 114.1 jit_solution(6987030948522179882)
XLA Ops:
  0.6 1.9 %shard_map.113 = (bf16[16,16,128]{2,1,0:T(8,128)(2,1)S(1)}, bf16[32,16,128]{2,1,0:T(8,128)(2,1)}, f32[16,128]{1,0:T(8,128)S(1)}, bf16[256,128]{1,0:T(8,128)(2,1)...) custom-call(s32[1]{0:T(128)} %bitcast.refs_0_, ...), custom_call_target="tpu_custom_call" | custom-call | tf_op jit(solution)/shard_map/pallas_call | solution.py:281
  2.5 22.2 %all_to_all.30.refs_0_ = bf16[16,16,128]{2,1,0:T(8,128)(2,1)S(1)} all-to-all(bf16[16,16,128]{2,1,0:T(8,128)(2,1)S(1)} %get-tuple-element.21), channel_id=1, replica_groups=mesh['mode'=16,'mer'=32] {'mode'}, dimensions={0} | all-to-all | bytes 131072 | tf_op jit(solution)/shard_map/all_to_all | solution.py:330
  24.7 0.5 shard_map.114
  25.2 12.3 %all_to_all.31.refs_2_ = bf16[16,32,128]{2,1,0:T(8,128)(2,1)S(1)} all-to-all(bf16[16,32,128]{2,1,0:T(8,128)(2,1)S(1)} %shard_map.114), channel_id=1, replica_groups=mesh['mode'=16,'mer'=32] {'mode'}, dimensions={0} | all-to-all | bytes 262144 | tf_op jit(solution)/shard_map/all_to_all | solution.py:334
  37.5 11.1 %all-to-all-start.2 = ((bf16[32,16,128]{2,1,0:T(8,128)(2,1)}), bf16[32,16,128]{2,1,0:T(8,128)(2,1)S(1)}, u32[]{:S(2)}, u32[]{:S(2)}) async-start(bf16[32,16,128]{2,1,0:T(8,128)(2,1)} %get-tuple-element.28), calls=%async_computation.2 | async-start | bytes 262144 | tf_op jit(solution)/shard_map/all_to_all | solution.py:337
  48.5 3.5 %collective-permute-start.1 = (bf16[16,32,128]{2,1,0:T(8,128)(2,1)S(1)}, bf16[16,32,128]{2,1,0:T(8,128)(2,1)S(1)}, u32[]{:S(2)}, u32[]{:S(2)}) collective-permute-start(bf16[16,32,128]{2,1,0:T(8,128)(2,1)S(1)} %all_to_all.31.refs_2_), channel_id=1, source_target_pairs={{1,2},{2,1},{3,4},{4,3},{5,6},{6,5},{7,8},{8,7},{9,10},{10,9},{11,... | collective-permute-start | bytes 393224 | tf_op jit(solution)/shard_map/ppermute | solution.py:336
  52.1 1.9 %collective-permute-start = (bf16[16,32,128]{2,1,0:T(8,128)(2,1)S(1)}, bf16[16,32,128]{2,1,0:T(8,128)(2,1)S(1)}, u32[]{:S(2)}, u32[]{:S(2)}) collective-permute-start(bf16[16,32,128]{2,1,0:T(8,128)(2,1)S(1)} %all_to_all.31.refs_2_), channel_id=1, source_target_pairs={{0,1},{1,0},{2,3},{3,2},{4,5},{5,4},{6,7},{7,6},{8,9},{9,8},{10,11... | collective-permute-start | bytes 393224 | tf_op jit(solution)/shard_map/ppermute | solution.py:335
  54.0 2.0 %collective-permute-done.1.refs_4_ = bf16[16,32,128]{2,1,0:T(8,128)(2,1)S(1)} collective-permute-done((bf16[16,32,128]{2,1,0:T(8,128)(2,1)S(1)}, bf16[16,32,128]{2,1,0:T(8,128)(2,1)S(1)}, u32[]{:S(2)}, u32[]{:S(2)}) %collective-permute-start.1) | collective-permute-done | bytes 131104 | tf_op jit(solution)/shard_map/ppermute | solution.py:336
  56.0 0.0 collective-permute-done.refs_3_
  56.0 6.7 %shard_map.115 = (f32[48,512]{1,0:T(8,128)S(1)}, bf16[4,64,2048]{2,1,0:T(8,128)(2,1)S(1)}, bf16[1536,512]{1,0:T(8,128)(2,1)}, bf16[1536,256]{1,0:T(8,128)(2,1)}) custom-call(s32[1]{0:T(128)} %bitcast.1.refs_1_.refs_0_, f32[6,8,512]{2,1,0:T(8,128)} %bitcast.8, bf16[16,32,128]{2,1,0:T(8,128)(2,1)S(1)} %all_to_all.31.refs_2_, ...), custom_call_target="tpu_custom_call" | custom-call | tf_op jit(solution)/shard_map/pallas_call | solution.py:281
  62.7 0.0 all-to-all-done.2.refs_4_
  62.7 3.0 %shard_map.116 = (f32[6,8,512]{2,1,0:T(8,128)S(1)}, bf16[16,16,128]{2,1,0:T(8,128)(2,1)S(1)}, bf16[32,16,128]{2,1,0:T(8,128)(2,1)}, f32[16,128]{1,0:T(8,128)S(1)}) custom-call(s32[1]{0:T(128)} %bitcast.refs_0_, s32[1]{0:T(128)} %bitcast.1.refs_1_.refs_0_, f32[6,8,512]{2,1,0:T(8,128)} %bitcast.9, f32[48,512]{1,0:T(8,128)S(1)} %get-tuple-element.27.refs_3_, ...), custom_call_target="tpu_custom_call" | custom-call | tf_op jit(solution)/shard_map/pallas_call | solution.py:281
  65.7 12.4 %all_to_all.32.refs_0_ = bf16[16,16,128]{2,1,0:T(8,128)(2,1)S(1)} all-to-all(bf16[16,16,128]{2,1,0:T(8,128)(2,1)S(1)} %get-tuple-element.31), channel_id=1, replica_groups=mesh['mode'=16,'mer'=32] {'mode'}, dimensions={0} | all-to-all | bytes 131072 | tf_op jit(solution)/shard_map/all_to_all | solution.py:330
  78.0 0.5 shard_map.117
  78.5 11.9 %all_to_all.33.refs_2_ = bf16[16,32,128]{2,1,0:T(8,128)(2,1)S(1)} all-to-all(bf16[16,32,128]{2,1,0:T(8,128)(2,1)S(1)} %shard_map.117), channel_id=1, replica_groups=mesh['mode'=16,'mer'=32] {'mode'}, dimensions={0} | all-to-all | bytes 262144 | tf_op jit(solution)/shard_map/all_to_all | solution.py:334
  90.4 10.8 %all-to-all-start.5 = ((bf16[32,16,128]{2,1,0:T(8,128)(2,1)}), bf16[32,16,128]{2,1,0:T(8,128)(2,1)S(1)}, u32[]{:S(2)}, u32[]{:S(2)}) async-start(bf16[32,16,128]{2,1,0:T(8,128)(2,1)} %get-tuple-element.35), calls=%async_computation.5 | async-start | bytes 262144 | tf_op jit(solution)/shard_map/all_to_all | solution.py:337
  101.2 3.5 %collective-permute-start.3 = (bf16[16,32,128]{2,1,0:T(8,128)(2,1)S(1)}, bf16[16,32,128]{2,1,0:T(8,128)(2,1)S(1)}, u32[]{:S(2)}, u32[]{:S(2)}) collective-permute-start(bf16[16,32,128]{2,1,0:T(8,128)(2,1)S(1)} %all_to_all.33.refs_2_), channel_id=1, source_target_pairs={{1,2},{2,1},{3,4},{4,3},{5,6},{6,5},{7,8},{8,7},{9,10},{10,9},{11,... | collective-permute-start | bytes 393224 | tf_op jit(solution)/shard_map/ppermute | solution.py:336
  104.8 1.9 %collective-permute-start.2 = (bf16[16,32,128]{2,1,0:T(8,128)(2,1)S(1)}, bf16[16,32,128]{2,1,0:T(8,128)(2,1)S(1)}, u32[]{:S(2)}, u32[]{:S(2)}) collective-permute-start(bf16[16,32,128]{2,1,0:T(8,128)(2,1)S(1)} %all_to_all.33.refs_2_), channel_id=1, source_target_pairs={{0,1},{1,0},{2,3},{3,2},{4,5},{5,4},{6,7},{7,6},{8,9},{9,8},{10,11... | collective-permute-start | bytes 393224 | tf_op jit(solution)/shard_map/ppermute | solution.py:335
  106.7 2.0 %collective-permute-done.3.refs_4_ = bf16[16,32,128]{2,1,0:T(8,128)(2,1)S(1)} collective-permute-done((bf16[16,32,128]{2,1,0:T(8,128)(2,1)S(1)}, bf16[16,32,128]{2,1,0:T(8,128)(2,1)S(1)}, u32[]{:S(2)}, u32[]{:S(2)}) %collective-permute-start.3) | collective-permute-done | bytes 131104 | tf_op jit(solution)/shard_map/ppermute | solution.py:336
  108.7 0.0 collective-permute-done.2.refs_3_
  108.7 2.6 %shard_map.118 = (f32[48,512]{1,0:T(8,128)S(1)}, bf16[4,64,2048]{2,1,0:T(8,128)(2,1)S(1)}) custom-call(s32[1]{0:T(128)} %bitcast.1.refs_1_.refs_0_, f32[6,8,512]{2,1,0:T(8,128)S(1)} %get-tuple-element.30.refs_1_.refs_2_, bf16[16,32,128]{2,1,0:T(8,128)(2,1)S(1)} %all_to_all.33.refs_2_, bf16[16,32,128]{2,1,0:T(8,128)(2,1)S(1)} %collective-permute-done.2.refs_3_, ...), custom_call_target="tpu_custom_call" | custom-call | tf_op jit(solution)/shard_map/pallas_call | solution.py:281
  111.3 0.0 all-to-all-done.5.refs_4_
  111.3 2.8 %shard_map.119 = (f32[6,8,512]{2,1,0:T(8,128)}, f32[2,8,2,64]{3,2,1,0:T(2,128)}) custom-call(s32[1]{0:T(128)} %bitcast.refs_0_, s32[1]{0:T(128)} %bitcast.1.refs_1_.refs_0_, f32[6,8,512]{2,1,0:T(8,128)S(1)} %get-tuple-element.30.refs_1_.refs_2_, f32[48,512]{1,0:T(8,128)S(1)} %get-tuple-element.34.refs_3_, bf16[32,16,128]{2,1,0:T(8,128)(2,1)S(1)} %all-to-all-done.5.refs_4_, ...), custom_call_target="tpu_custom_call" | custom-call | tf_op jit(solution)/shard_map/pallas_call | solution.py:281
Async XLA Ops:
  37.5 25.2 %all-to-all-start.2 = ((bf16[32,16,128]{2,1,0:T(8,128)(2,1)}), bf16[32,16,128]{2,1,0:T(8,128)(2,1)S(1)}, u32[]{:S(2)}, u32[]{:S(2)}) async-start(bf16[32,16,128]{2,1,0:T(8,128)(2,1)} %get-tuple-element.28), calls=%async_computation.2 | async-start | bytes 262144 | tf_op jit(solution)/shard_map/all_to_all | solution.py:337
  48.5 7.5 %collective-permute-start.1 = (bf16[16,32,128]{2,1,0:T(8,128)(2,1)S(1)}, bf16[16,32,128]{2,1,0:T(8,128)(2,1)S(1)}, u32[]{:S(2)}, u32[]{:S(2)}) collective-permute-start(bf16[16,32,128]{2,1,0:T(8,128)(2,1)S(1)} %all_to_all.31.refs_2_), channel_id=1, source_target_pairs={{1,2},{2,1},{3,4},{4,3},{5,6},{6,5},{7,8},{8,7},{9,10},{10,9},{11,... | collective-permute-start | bytes 393224 | tf_op jit(solution)/shard_map/ppermute | solution.py:336
  52.1 3.9 %collective-permute-start = (bf16[16,32,128]{2,1,0:T(8,128)(2,1)S(1)}, bf16[16,32,128]{2,1,0:T(8,128)(2,1)S(1)}, u32[]{:S(2)}, u32[]{:S(2)}) collective-permute-start(bf16[16,32,128]{2,1,0:T(8,128)(2,1)S(1)} %all_to_all.31.refs_2_), channel_id=1, source_target_pairs={{0,1},{1,0},{2,3},{3,2},{4,5},{5,4},{6,7},{7,6},{8,9},{9,8},{10,11... | collective-permute-start | bytes 393224 | tf_op jit(solution)/shard_map/ppermute | solution.py:335
  90.4 20.9 %all-to-all-start.5 = ((bf16[32,16,128]{2,1,0:T(8,128)(2,1)}), bf16[32,16,128]{2,1,0:T(8,128)(2,1)S(1)}, u32[]{:S(2)}, u32[]{:S(2)}) async-start(bf16[32,16,128]{2,1,0:T(8,128)(2,1)} %get-tuple-element.35), calls=%async_computation.5 | async-start | bytes 262144 | tf_op jit(solution)/shard_map/all_to_all | solution.py:337
  101.2 7.5 %collective-permute-start.3 = (bf16[16,32,128]{2,1,0:T(8,128)(2,1)S(1)}, bf16[16,32,128]{2,1,0:T(8,128)(2,1)S(1)}, u32[]{:S(2)}, u32[]{:S(2)}) collective-permute-start(bf16[16,32,128]{2,1,0:T(8,128)(2,1)S(1)} %all_to_all.33.refs_2_), channel_id=1, source_target_pairs={{1,2},{2,1},{3,4},{4,3},{5,6},{6,5},{7,8},{8,7},{9,10},{10,9},{11,... | collective-permute-start | bytes 393224 | tf_op jit(solution)/shard_map/ppermute | solution.py:336
  104.8 3.9 %collective-permute-start.2 = (bf16[16,32,128]{2,1,0:T(8,128)(2,1)S(1)}, bf16[16,32,128]{2,1,0:T(8,128)(2,1)S(1)}, u32[]{:S(2)}, u32[]{:S(2)}) collective-permute-start(bf16[16,32,128]{2,1,0:T(8,128)(2,1)S(1)} %all_to_all.33.refs_2_), channel_id=1, source_target_pairs={{0,1},{1,0},{2,3},{3,2},{4,5},{5,4},{6,7},{7,6},{8,9},{9,8},{10,11... | collective-permute-start | bytes 393224 | tf_op jit(solution)/shard_map/ppermute | solution.py:335

commit v8 on v7

--- a/solution.py
+++ b/solution.py
@@ -158,13 +158,18 @@
     return lambda s: jnp.where(odd, first[s, rows], second[s, rows])
 
 
-def operator_rows(mer_ref, now, emf_ref, pa_ref, pb_ref, near, far):
+def operands(mer_ref, now, emf_ref, pa_ref, pb_ref):
     own = unpack(lambda s: emf_ref[s, :16], 16)
     e_next, f_next = [unpack(side(mer_ref, pa_ref, pb_ref, 1, part), 8) for part in range(2)]
     e_prev, f_prev = [unpack(side(mer_ref, pa_ref, pb_ref, 0, part), 16) for part in range(2)]
     field = rows_of(now).astype(BF)
-    total = nn(jnp.concatenate([own, e_next, field, f_next], 1), near()[...])
-    low = nn(jnp.concatenate([e_prev, own[:, :256], f_prev, field[:, :256]], 1), far()[...])
+    near = jnp.concatenate([own, e_next, field, f_next], 1)
+    return near, jnp.concatenate([e_prev, own[:, :256], f_prev, field[:, :256]], 1)
+
+
+def operator_rows(rows, near, far):
+    total = sum(nn(rows[0][:, 512 * k : 512 * k + 512], near(k)) for k in range(3))
+    low = nn(rows[1], far())
     return jnp.concatenate([total[:, :256] + low, total[:, 256:]], 1)
 
 
@@ -188,16 +193,33 @@
         ref[768:] = (s * gain).astype(BF)
         copies.append(pltpu.make_async_copy(ref, out, sems.at[len(copies)]))
         copies[-1].start()
-    out_ref[...] = operator_rows(mer_ref, now, emf_ref, pa_ref, pb_ref, lambda: near_ref, lambda: far_ref)
+    rows = operands(mer_ref, now, emf_ref, pa_ref, pb_ref)
+    out_ref[...] = operator_rows(
+        rows, lambda k: near_ref[512 * k : 512 * k + 512], lambda: far_ref[...]
+    )
     for copy in [*copies, bring]:
         copy.wait()
 
 
-def operator_kernel(mer_ref, now, emf_ref, pa_ref, pb_ref, near, far, dtn_ref, out_ref, half_ref, sem):
-    bring = pltpu.make_async_copy(dtn_ref.at[pl.ds(0, 4)], half_ref, sem)
-    bring.start()
-    out_ref[...] = operator_rows(mer_ref, now, emf_ref, pa_ref, pb_ref, near, far)
-    bring.wait()
+def operator_kernel(mer_ref, now, emf_ref, pa_ref, pb_ref, near_ref, far_ref, dtn_ref, *refs):
+    out_ref, half_ref, near_buf, far_buf, sems = refs
+    pairs = [(near_ref.at[pl.ds(512 * k, 512)], near_buf.at[pl.ds(512 * k, 512)]) for k in range(3)]
+    pairs += [(far_ref, far_buf), (dtn_ref.at[pl.ds(0, 4)], half_ref)]
+    copies = [pltpu.make_async_copy(a, b, sems.at[k]) for k, (a, b) in enumerate(pairs)]
+    for copy in copies:
+        copy.start()
+    rows = operands(mer_ref, now, emf_ref, pa_ref, pb_ref)
+
+    def near(k):
+        copies[k].wait()
+        return near_buf[512 * k : 512 * k + 512]
+
+    def far():
+        copies[3].wait()
+        return far_buf[...]
+
+    out_ref[...] = operator_rows(rows, near, far)
+    copies[4].wait()
 
 
 def finish(mode_ref, mer_ref, now, total_ref, whole_ref, wall, mass, half_ref, dtn):
@@ -364,9 +386,9 @@
     total, half = call(
         operator_kernel,
         [rows, some],
-        "svvvvcch",
+        "svvvvhhh",
         (mer, sect, emf, e_twin, e_other, near, far, dtn),
-        [pltpu.SemaphoreType.DMA],
+        [*works[:2], pltpu.SemaphoreType.DMA((5,))],
     )
     out = [((6, 8, 512), F32, None), ((2, 8, 2, 64), F32, None)]
     done, fluxes = call(

time: 115 us -> 115 us (level)
  no operation moved by 1% of the time
where the time goes in v8:
time: 115 us; the launch traced here: 114 us
  blocking collectives  58.7 us (51%)
  starting transfers between devices  32.8 us (29%)
  Pallas kernels  17.5 us (15%)
  waiting for transfers between devices  3.97 us (3%)
    all_to_all x2, blocking collectives, exchange(): moved = lax.all_to_all(packed, 'mode', 0, 0, tiled=True)  34.6 us
    all_to_all x2, blocking collectives, exchange(): emf = lax.all_to_all(back, 'mode', 0, 0, tiled=True)  24.2 us
    all_to_all x2, starting transfers between devices, exchange(): lax.all_to_all(trace, 'mer', 0, 0, tiled=True)  21.9 us
    pallas_call x7, Pallas kernels, call(): pl.pallas_call(run, out_shape=[space(s, d) if space else jax.ShapeDtypeSt...  17.5 us
    ppermute x2, starting transfers between devices, exchange(): e_other = lax.ppermute(emf, 'mer', others)  7.08 us
    ppermute x2, waiting for transfers between devices, exchange(): e_other = lax.ppermute(emf, 'mer', others)  3.96 us
    ppermute x2, starting transfers between devices, exchange(): e_twin = lax.ppermute(emf, 'mer', twins)  3.84 us
  transfers between devices with their start and end apart: 6, of which 2 were waited for; matrix products, arithmetic and copies ran while one was open for 0% of the time, Pallas kernels for 8%

profile of v8, /device:TPU:1, one launch (start us, length us, event | category | flops | bytes accessed | tf_op | source)
XLA Modules:
  0.0 113.7 jit_solution(4814900904043626651)
XLA Ops:
  0.6 1.9 %shard_map.113 = (bf16[16,16,128]{2,1,0:T(8,128)(2,1)S(1)}, bf16[32,16,128]{2,1,0:T(8,128)(2,1)}, f32[16,128]{1,0:T(8,128)S(1)}, bf16[256,128]{1,0:T(8,128)(2,1)...) custom-call(s32[1]{0:T(128)} %bitcast.refs_0_, ...), custom_call_target="tpu_custom_call" | custom-call | tf_op jit(solution)/shard_map/pallas_call | solution.py:303
  2.5 22.2 %all_to_all.30.refs_0_ = bf16[16,16,128]{2,1,0:T(8,128)(2,1)S(1)} all-to-all(bf16[16,16,128]{2,1,0:T(8,128)(2,1)S(1)} %get-tuple-element.21), channel_id=1, replica_groups=mesh['mode'=16,'mer'=32] {'mode'}, dimensions={0} | all-to-all | bytes 131072 | tf_op jit(solution)/shard_map/all_to_all | solution.py:352
  24.7 0.5 shard_map.114
  25.2 12.3 %all_to_all.31.refs_2_ = bf16[16,32,128]{2,1,0:T(8,128)(2,1)S(1)} all-to-all(bf16[16,32,128]{2,1,0:T(8,128)(2,1)S(1)} %shard_map.114), channel_id=1, replica_groups=mesh['mode'=16,'mer'=32] {'mode'}, dimensions={0} | all-to-all | bytes 262144 | tf_op jit(solution)/shard_map/all_to_all | solution.py:356
  37.5 11.1 %all-to-all-start.2 = ((bf16[32,16,128]{2,1,0:T(8,128)(2,1)}), bf16[32,16,128]{2,1,0:T(8,128)(2,1)S(1)}, u32[]{:S(2)}, u32[]{:S(2)}) async-start(bf16[32,16,128]{2,1,0:T(8,128)(2,1)} %get-tuple-element.28), calls=%async_computation.2 | async-start | bytes 262144 | tf_op jit(solution)/shard_map/all_to_all | solution.py:359
  48.5 3.5 %collective-permute-start.1 = (bf16[16,32,128]{2,1,0:T(8,128)(2,1)S(1)}, bf16[16,32,128]{2,1,0:T(8,128)(2,1)S(1)}, u32[]{:S(2)}, u32[]{:S(2)}) collective-permute-start(bf16[16,32,128]{2,1,0:T(8,128)(2,1)S(1)} %all_to_all.31.refs_2_), channel_id=1, source_target_pairs={{1,2},{2,1},{3,4},{4,3},{5,6},{6,5},{7,8},{8,7},{9,10},{10,9},{11,... | collective-permute-start | bytes 393224 | tf_op jit(solution)/shard_map/ppermute | solution.py:358
  52.1 1.9 %collective-permute-start = (bf16[16,32,128]{2,1,0:T(8,128)(2,1)S(1)}, bf16[16,32,128]{2,1,0:T(8,128)(2,1)S(1)}, u32[]{:S(2)}, u32[]{:S(2)}) collective-permute-start(bf16[16,32,128]{2,1,0:T(8,128)(2,1)S(1)} %all_to_all.31.refs_2_), channel_id=1, source_target_pairs={{0,1},{1,0},{2,3},{3,2},{4,5},{5,4},{6,7},{7,6},{8,9},{9,8},{10,11... | collective-permute-start | bytes 393224 | tf_op jit(solution)/shard_map/ppermute | solution.py:357
  54.0 2.0 %collective-permute-done.1.refs_4_ = bf16[16,32,128]{2,1,0:T(8,128)(2,1)S(1)} collective-permute-done((bf16[16,32,128]{2,1,0:T(8,128)(2,1)S(1)}, bf16[16,32,128]{2,1,0:T(8,128)(2,1)S(1)}, u32[]{:S(2)}, u32[]{:S(2)}) %collective-permute-start.1) | collective-permute-done | bytes 131104 | tf_op jit(solution)/shard_map/ppermute | solution.py:358
  56.0 0.0 collective-permute-done.refs_3_
  56.0 6.7 %shard_map.115 = (f32[48,512]{1,0:T(8,128)S(1)}, bf16[4,64,2048]{2,1,0:T(8,128)(2,1)S(1)}, bf16[1536,512]{1,0:T(8,128)(2,1)}, bf16[1536,256]{1,0:T(8,128)(2,1)}) custom-call(s32[1]{0:T(128)} %bitcast.1.refs_1_.refs_0_, f32[6,8,512]{2,1,0:T(8,128)} %bitcast.8, bf16[16,32,128]{2,1,0:T(8,128)(2,1)S(1)} %all_to_all.31.refs_2_, ...), custom_call_target="tpu_custom_call" | custom-call | tf_op jit(solution)/shard_map/pallas_call | solution.py:303
  62.7 0.0 all-to-all-done.2.refs_4_
  62.7 3.0 %shard_map.116 = (f32[6,8,512]{2,1,0:T(8,128)S(1)}, bf16[16,16,128]{2,1,0:T(8,128)(2,1)S(1)}, bf16[32,16,128]{2,1,0:T(8,128)(2,1)}, f32[16,128]{1,0:T(8,128)S(1)}) custom-call(s32[1]{0:T(128)} %bitcast.refs_0_, s32[1]{0:T(128)} %bitcast.1.refs_1_.refs_0_, f32[6,8,512]{2,1,0:T(8,128)} %bitcast.9, f32[48,512]{1,0:T(8,128)S(1)} %get-tuple-element.27.refs_3_, ...), custom_call_target="tpu_custom_call" | custom-call | tf_op jit(solution)/shard_map/pallas_call | solution.py:303
  65.7 12.4 %all_to_all.32.refs_0_ = bf16[16,16,128]{2,1,0:T(8,128)(2,1)S(1)} all-to-all(bf16[16,16,128]{2,1,0:T(8,128)(2,1)S(1)} %get-tuple-element.31), channel_id=1, replica_groups=mesh['mode'=16,'mer'=32] {'mode'}, dimensions={0} | all-to-all | bytes 131072 | tf_op jit(solution)/shard_map/all_to_all | solution.py:352
  78.0 0.5 shard_map.117
  78.5 11.9 %all_to_all.33.refs_2_ = bf16[16,32,128]{2,1,0:T(8,128)(2,1)S(1)} all-to-all(bf16[16,32,128]{2,1,0:T(8,128)(2,1)S(1)} %shard_map.117), channel_id=1, replica_groups=mesh['mode'=16,'mer'=32] {'mode'}, dimensions={0} | all-to-all | bytes 262144 | tf_op jit(solution)/shard_map/all_to_all | solution.py:356
  90.4 10.8 %all-to-all-start.5 = ((bf16[32,16,128]{2,1,0:T(8,128)(2,1)}), bf16[32,16,128]{2,1,0:T(8,128)(2,1)S(1)}, u32[]{:S(2)}, u32[]{:S(2)}) async-start(bf16[32,16,128]{2,1,0:T(8,128)(2,1)} %get-tuple-element.35), calls=%async_computation.5 | async-start | bytes 262144 | tf_op jit(solution)/shard_map/all_to_all | solution.py:359
  101.2 3.5 %collective-permute-start.3 = (bf16[16,32,128]{2,1,0:T(8,128)(2,1)S(1)}, bf16[16,32,128]{2,1,0:T(8,128)(2,1)S(1)}, u32[]{:S(2)}, u32[]{:S(2)}) collective-permute-start(bf16[16,32,128]{2,1,0:T(8,128)(2,1)S(1)} %all_to_all.33.refs_2_), channel_id=1, source_target_pairs={{1,2},{2,1},{3,4},{4,3},{5,6},{6,5},{7,8},{8,7},{9,10},{10,9},{11,... | collective-permute-start | bytes 393224 | tf_op jit(solution)/shard_map/ppermute | solution.py:358
  104.8 1.9 %collective-permute-start.2 = (bf16[16,32,128]{2,1,0:T(8,128)(2,1)S(1)}, bf16[16,32,128]{2,1,0:T(8,128)(2,1)S(1)}, u32[]{:S(2)}, u32[]{:S(2)}) collective-permute-start(bf16[16,32,128]{2,1,0:T(8,128)(2,1)S(1)} %all_to_all.33.refs_2_), channel_id=1, source_target_pairs={{0,1},{1,0},{2,3},{3,2},{4,5},{5,4},{6,7},{7,6},{8,9},{9,8},{10,11... | collective-permute-start | bytes 393224 | tf_op jit(solution)/shard_map/ppermute | solution.py:357
  106.7 2.0 %collective-permute-done.3.refs_4_ = bf16[16,32,128]{2,1,0:T(8,128)(2,1)S(1)} collective-permute-done((bf16[16,32,128]{2,1,0:T(8,128)(2,1)S(1)}, bf16[16,32,128]{2,1,0:T(8,128)(2,1)S(1)}, u32[]{:S(2)}, u32[]{:S(2)}) %collective-permute-start.3) | collective-permute-done | bytes 131104 | tf_op jit(solution)/shard_map/ppermute | solution.py:358
  108.7 0.0 collective-permute-done.2.refs_3_
  108.7 2.2 %shard_map.118 = (f32[48,512]{1,0:T(8,128)S(1)}, bf16[4,64,2048]{2,1,0:T(8,128)(2,1)S(1)}) custom-call(s32[1]{0:T(128)} %bitcast.1.refs_1_.refs_0_, f32[6,8,512]{2,1,0:T(8,128)S(1)} %get-tuple-element.30.refs_1_.refs_2_, bf16[16,32,128]{2,1,0:T(8,128)(2,1)S(1)} %all_to_all.33.refs_2_, bf16[16,32,128]{2,1,0:T(8,128)(2,1)S(1)} %collective-permute-done.2.refs_3_, ...), custom_call_target="tpu_custom_call" | custom-call | tf_op jit(solution)/shard_map/pallas_call | solution.py:303
  110.9 0.0 all-to-all-done.5.refs_4_
  110.9 2.8 %shard_map.119 = (f32[6,8,512]{2,1,0:T(8,128)}, f32[2,8,2,64]{3,2,1,0:T(2,128)}) custom-call(s32[1]{0:T(128)} %bitcast.refs_0_, s32[1]{0:T(128)} %bitcast.1.refs_1_.refs_0_, f32[6,8,512]{2,1,0:T(8,128)S(1)} %get-tuple-element.30.refs_1_.refs_2_, f32[48,512]{1,0:T(8,128)S(1)} %get-tuple-element.34.refs_3_, bf16[32,16,128]{2,1,0:T(8,128)(2,1)S(1)} %all-to-all-done.5.refs_4_, ...), custom_call_target="tpu_custom_call" | custom-call | tf_op jit(solution)/shard_map/pallas_call | solution.py:303
Async XLA Ops:
  37.5 25.2 %all-to-all-start.2 = ((bf16[32,16,128]{2,1,0:T(8,128)(2,1)}), bf16[32,16,128]{2,1,0:T(8,128)(2,1)S(1)}, u32[]{:S(2)}, u32[]{:S(2)}) async-start(bf16[32,16,128]{2,1,0:T(8,128)(2,1)} %get-tuple-element.28), calls=%async_computation.2 | async-start | bytes 262144 | tf_op jit(solution)/shard_map/all_to_all | solution.py:359
  48.5 7.5 %collective-permute-start.1 = (bf16[16,32,128]{2,1,0:T(8,128)(2,1)S(1)}, bf16[16,32,128]{2,1,0:T(8,128)(2,1)S(1)}, u32[]{:S(2)}, u32[]{:S(2)}) collective-permute-start(bf16[16,32,128]{2,1,0:T(8,128)(2,1)S(1)} %all_to_all.31.refs_2_), channel_id=1, source_target_pairs={{1,2},{2,1},{3,4},{4,3},{5,6},{6,5},{7,8},{8,7},{9,10},{10,9},{11,... | collective-permute-start | bytes 393224 | tf_op jit(solution)/shard_map/ppermute | solution.py:358
  52.1 3.9 %collective-permute-start = (bf16[16,32,128]{2,1,0:T(8,128)(2,1)S(1)}, bf16[16,32,128]{2,1,0:T(8,128)(2,1)S(1)}, u32[]{:S(2)}, u32[]{:S(2)}) collective-permute-start(bf16[16,32,128]{2,1,0:T(8,128)(2,1)S(1)} %all_to_all.31.refs_2_), channel_id=1, source_target_pairs={{0,1},{1,0},{2,3},{3,2},{4,5},{5,4},{6,7},{7,6},{8,9},{9,8},{10,11... | collective-permute-start | bytes 393224 | tf_op jit(solution)/shard_map/ppermute | solution.py:357
  90.4 20.5 %all-to-all-start.5 = ((bf16[32,16,128]{2,1,0:T(8,128)(2,1)}), bf16[32,16,128]{2,1,0:T(8,128)(2,1)S(1)}, u32[]{:S(2)}, u32[]{:S(2)}) async-start(bf16[32,16,128]{2,1,0:T(8,128)(2,1)} %get-tuple-element.35), calls=%async_computation.5 | async-start | bytes 262144 | tf_op jit(solution)/shard_map/all_to_all | solution.py:359
  101.2 7.5 %collective-permute-start.3 = (bf16[16,32,128]{2,1,0:T(8,128)(2,1)S(1)}, bf16[16,32,128]{2,1,0:T(8,128)(2,1)S(1)}, u32[]{:S(2)}, u32[]{:S(2)}) collective-permute-start(bf16[16,32,128]{2,1,0:T(8,128)(2,1)S(1)} %all_to_all.33.refs_2_), channel_id=1, source_target_pairs={{1,2},{2,1},{3,4},{4,3},{5,6},{6,5},{7,8},{8,7},{9,10},{10,9},{11,... | collective-permute-start | bytes 393224 | tf_op jit(solution)/shard_map/ppermute | solution.py:358
  104.8 3.9 %collective-permute-start.2 = (bf16[16,32,128]{2,1,0:T(8,128)(2,1)S(1)}, bf16[16,32,128]{2,1,0:T(8,128)(2,1)S(1)}, u32[]{:S(2)}, u32[]{:S(2)}) collective-permute-start(bf16[16,32,128]{2,1,0:T(8,128)(2,1)S(1)} %all_to_all.33.refs_2_), channel_id=1, source_target_pairs={{0,1},{1,0},{2,3},{3,2},{4,5},{5,4},{6,7},{7,6},{8,9},{9,8},{10,11... | collective-permute-start | bytes 393224 | tf_op jit(solution)/shard_map/ppermute | solution.py:357

commit v9 on v8

--- a/solution.py
+++ b/solution.py
@@ -66,11 +66,27 @@
     return jnp.concatenate(cols, 1)
 
 
-def wall_onehot(wall_ref, mer):
+def wall_onehot(wall_ref, mer=None):
     twice = jnp.concatenate([wall_ref[...], wall_ref[...]], 1)
     nodes = lax.broadcasted_iota(jnp.int32, (512, 128), 0)
-    half = lax.broadcasted_iota(jnp.int32, (512, 128), 1) // 64
-    return jnp.where(half == mer % 2, (nodes == twice).astype(F32), 0.0).astype(BF)
+    hit = (nodes == twice).astype(F32)
+    if mer is not None:
+        half = lax.broadcasted_iota(jnp.int32, (512, 128), 1) // 64
+        hit = jnp.where(half == mer % 2, hit, 0.0)
+    return hit.astype(BF)
+
+
+def all_traces(whole_ref):
+    pairs = [(whole_ref[2 * a], whole_ref[2 * a + 1]) for a in range(16)]
+    if whole_ref.shape[1] == 16:
+        return jnp.concatenate([x + y for x, y in pairs], 1)
+    low = low_lanes((8, 128))
+    parts = [], []
+    for x, y in pairs:
+        x, y = x.astype(F32), y.astype(F32)
+        parts[0].append(jnp.where(low, x, pltpu.roll(y, 64, 1)))
+        parts[1].append(jnp.where(low, pltpu.roll(x, 64, 1), y))
+    return jnp.concatenate([jnp.concatenate(p, 1) for p in parts], 0).astype(BF)
 
 
 def low_lanes(shape):
@@ -81,12 +97,13 @@
     return jnp.concatenate([conn_ref[pl.ds(0, 8, 2), :], conn_ref[pl.ds(1, 8, 2), :]], 1)
 
 
-def open_kernel(mode_ref, mer_ref, field, wall, conn, vel, fwd, inv, pack_ref, out_ref, mark_ref, va_ref, vb_ref, fwd_ref, inv_ref):
-    onehot = wall_onehot(wall(), mer_ref[0])
+def open_kernel(mode_ref, field, wall, conn, vel, fwd, inv, pack_ref, out_ref, mark_ref, va_ref, vb_ref, fwd_ref, inv_ref):
+    onehot = wall_onehot(wall())
     conn = conn()[...]
     field_ref = field()
     pack({(c, p): field_ref[3 * p + c] for c in range(3) for p in range(2)}, pack_ref)
-    tr = nn(jnp.concatenate([field_ref[2], field_ref[5]], 0).astype(BF), onehot).astype(BF)
+    tr = nn(jnp.concatenate([field_ref[2], field_ref[5]], 0).astype(BF), onehot)
+    tr = jnp.where(low_lanes((8, 128)), tr[:8], tr[8:]).astype(BF)
     for j in range(out_ref.shape[0]):
         out_ref[j] = tr
     part = jnp.zeros((16, 64), jnp.int32) + mode_ref[0] % 4
@@ -223,7 +240,7 @@
 
 
 def finish(mode_ref, mer_ref, now, total_ref, whole_ref, wall, mass, half_ref, dtn):
-    whole = jnp.concatenate([whole_ref[2 * a] + whole_ref[2 * a + 1] for a in range(16)], 1)
+    whole = all_traces(whole_ref)
     every = [nt(whole, half_ref[2 * k : 2 * k + 2].reshape(128, 2048)) for k in range(2)]
     onehot = wall_onehot(wall(), mer_ref[0])
     field = rows_of(now)
@@ -341,9 +358,9 @@
     table = [((256, 128), BF, near_space)] * 2 + [((256, 256), BF, near_space)] * 2
     packed, trace, *table = call(
         open_kernel,
-        [chunk, ((spots, 16, 128), BF, near_space), ((16, 128), F32, near_space), *table],
-        "sscccccc",
-        (mode, mer, start, wall, connect, jnp.transpose(velocity, (0, 2, 1)), fwd, inv),
+        [chunk, ((spots, 8, 128), BF, near_space), ((16, 128), F32, near_space), *table],
+        "scccccc",
+        (mode, start, wall, connect, jnp.transpose(velocity, (0, 2, 1)), fwd, inv),
     )
     twins = [(i, i ^ 1) for i in range(spots)]
     others = [(i, ((i + 1) ^ 1) - 1) for i in range(1, spots - 1)]

time: 115 us -> 112 us (0.974)
  starting transfers between devices: 32.8 us -> 30.5 us
    all_to_all x2, starting transfers between devices: 21.9 us -> 17.3 us  [exchange(): lax.all_to_all(trace, 'mer', 0, 0, tiled=True)]
    ppermute x2, starting transfers between devices: 7.08 us -> 9.41 us  [exchange(): e_other = lax.ppermute(emf, 'mer', others)]
    ppermute x2, waiting for transfers between devices: 3.96 us -> 1.98 us  [exchange(): e_other = lax.ppermute(emf, 'mer', others)]
    all_to_all x2, waiting for transfers between devices: 0.01 us -> 1.64 us  [exchange(): lax.all_to_all(trace, 'mer', 0, 0, tiled=True)]
where the time goes in v9:
time: 112 us; the launch traced here: 111 us
  blocking collectives  58.2 us (52%)
  starting transfers between devices  30.5 us (27%)
  Pallas kernels  17.6 us (16%)
  waiting for transfers between devices  3.63 us (3%)
    all_to_all x2, blocking collectives, exchange(): moved = lax.all_to_all(packed, 'mode', 0, 0, tiled=True)  33.8 us
    all_to_all x2, blocking collectives, exchange(): emf = lax.all_to_all(back, 'mode', 0, 0, tiled=True)  24.4 us
    pallas_call x7, Pallas kernels, call(): pl.pallas_call(run, out_shape=[space(s, d) if space else jax.ShapeDtypeSt...  17.6 us
    all_to_all x2, starting transfers between devices, exchange(): lax.all_to_all(trace, 'mer', 0, 0, tiled=True)  17.3 us
    ppermute x2, starting transfers between devices, exchange(): e_other = lax.ppermute(emf, 'mer', others)  9.41 us
    ppermute x2, starting transfers between devices, exchange(): e_twin = lax.ppermute(emf, 'mer', twins)  3.84 us
  transfers between devices with their start and end apart: 6, of which 2 were waited for; matrix products, arithmetic and copies ran while one was open for 0% of the time, Pallas kernels for 8%

profile of v9, /device:TPU:1, one launch (start us, length us, event | category | flops | bytes accessed | tf_op | source)
XLA Modules:
  0.0 110.7 jit_solution(417549863595952064)
XLA Ops:
  0.6 1.8 %shard_map.113 = (bf16[16,16,128]{2,1,0:T(8,128)(2,1)S(1)}, bf16[32,8,128]{2,1,0:T(8,128)(2,1)}, f32[16,128]{1,0:T(8,128)S(1)}, bf16[256,128]{1,0:T(8,128)(2,1)S...) custom-call(s32[1]{0:T(128)} %bitcast.refs_0_, ...), custom_call_target="tpu_custom_call" | custom-call | tf_op jit(solution)/shard_map/pallas_call | solution.py:320
  2.5 22.2 %all_to_all.30.refs_0_ = bf16[16,16,128]{2,1,0:T(8,128)(2,1)S(1)} all-to-all(bf16[16,16,128]{2,1,0:T(8,128)(2,1)S(1)} %get-tuple-element.21), channel_id=1, replica_groups=mesh['mode'=16,'mer'=32] {'mode'}, dimensions={0} | all-to-all | bytes 131072 | tf_op jit(solution)/shard_map/all_to_all | solution.py:369
  24.7 0.5 shard_map.114
  25.1 12.3 %all_to_all.31.refs_2_ = bf16[16,32,128]{2,1,0:T(8,128)(2,1)S(1)} all-to-all(bf16[16,32,128]{2,1,0:T(8,128)(2,1)S(1)} %shard_map.114), channel_id=1, replica_groups=mesh['mode'=16,'mer'=32] {'mode'}, dimensions={0} | all-to-all | bytes 262144 | tf_op jit(solution)/shard_map/all_to_all | solution.py:373
  37.4 5.9 %collective-permute-start.1 = (bf16[16,32,128]{2,1,0:T(8,128)(2,1)S(1)}, bf16[16,32,128]{2,1,0:T(8,128)(2,1)S(1)}, u32[]{:S(2)}, u32[]{:S(2)}) collective-permute-start(bf16[16,32,128]{2,1,0:T(8,128)(2,1)S(1)} %all_to_all.31.refs_2_), channel_id=1, source_target_pairs={{1,2},{2,1},{3,4},{4,3},{5,6},{6,5},{7,8},{8,7},{9,10},{10,9},{11,... | collective-permute-start | bytes 393224 | tf_op jit(solution)/shard_map/ppermute | solution.py:375
  43.3 1.9 %collective-permute-start = (bf16[16,32,128]{2,1,0:T(8,128)(2,1)S(1)}, bf16[16,32,128]{2,1,0:T(8,128)(2,1)S(1)}, u32[]{:S(2)}, u32[]{:S(2)}) collective-permute-start(bf16[16,32,128]{2,1,0:T(8,128)(2,1)S(1)} %all_to_all.31.refs_2_), channel_id=1, source_target_pairs={{0,1},{1,0},{2,3},{3,2},{4,5},{5,4},{6,7},{7,6},{8,9},{9,8},{10,11... | collective-permute-start | bytes 393224 | tf_op jit(solution)/shard_map/ppermute | solution.py:374
  45.2 8.1 %all-to-all-start.2 = ((bf16[32,8,128]{2,1,0:T(8,128)(2,1)}), bf16[32,8,128]{2,1,0:T(8,128)(2,1)S(1)}, u32[]{:S(2)}, u32[]{:S(2)}) async-start(bf16[32,8,128]{2,1,0:T(8,128)(2,1)} %get-tuple-element.28), calls=%async_computation.2 | async-start | bytes 131072 | tf_op jit(solution)/shard_map/all_to_all | solution.py:376
  53.4 0.0 collective-permute-done.1.refs_4_
  53.4 0.0 collective-permute-done.refs_3_
  53.4 6.7 %shard_map.115 = (f32[48,512]{1,0:T(8,128)S(1)}, bf16[4,64,2048]{2,1,0:T(8,128)(2,1)S(1)}, bf16[1536,512]{1,0:T(8,128)(2,1)}, bf16[1536,256]{1,0:T(8,128)(2,1)}) custom-call(s32[1]{0:T(128)} %bitcast.1.refs_0_.refs_1_, f32[6,8,512]{2,1,0:T(8,128)} %bitcast.8, bf16[16,32,128]{2,1,0:T(8,128)(2,1)S(1)} %all_to_all.31.refs_2_, ...), custom_call_target="tpu_custom_call" | custom-call | tf_op jit(solution)/shard_map/pallas_call | solution.py:320
  60.1 1.6 %all-to-all-done.2.refs_4_ = bf16[32,8,128]{2,1,0:T(8,128)(2,1)S(1)} async-done(((bf16[32,8,128]{2,1,0:T(8,128)(2,1)}), bf16[32,8,128]{2,1,0:T(8,128)(2,1)S(1)}, u32[]{:S(2)}, u32[]{:S(2)}) %all-to-all-start.2) | async-done | bytes 65568 | tf_op jit(solution)/shard_map/all_to_all | solution.py:376
  61.7 3.2 %shard_map.116 = (f32[6,8,512]{2,1,0:T(8,128)S(1)}, bf16[16,16,128]{2,1,0:T(8,128)(2,1)S(1)}, bf16[32,16,128]{2,1,0:T(8,128)(2,1)}, f32[16,128]{1,0:T(8,128)S(1)}) custom-call(s32[1]{0:T(128)} %bitcast.refs_0_, s32[1]{0:T(128)} %bitcast.1.refs_0_.refs_1_, f32[6,8,512]{2,1,0:T(8,128)} %bitcast.9, f32[48,512]{1,0:T(8,128)S(1)} %get-tuple-element.27.refs_3_, ...), custom_call_target="tpu_custom_call" | custom-call | tf_op jit(solution)/shard_map/pallas_call | solution.py:320
  64.9 11.6 %all_to_all.32.refs_0_ = bf16[16,16,128]{2,1,0:T(8,128)(2,1)S(1)} all-to-all(bf16[16,16,128]{2,1,0:T(8,128)(2,1)S(1)} %get-tuple-element.31), channel_id=1, replica_groups=mesh['mode'=16,'mer'=32] {'mode'}, dimensions={0} | all-to-all | bytes 131072 | tf_op jit(solution)/shard_map/all_to_all | solution.py:369
  76.5 0.5 shard_map.117
  77.0 12.1 %all_to_all.33.refs_2_ = bf16[16,32,128]{2,1,0:T(8,128)(2,1)S(1)} all-to-all(bf16[16,32,128]{2,1,0:T(8,128)(2,1)S(1)} %shard_map.117), channel_id=1, replica_groups=mesh['mode'=16,'mer'=32] {'mode'}, dimensions={0} | all-to-all | bytes 262144 | tf_op jit(solution)/shard_map/all_to_all | solution.py:373
  89.1 9.1 %all-to-all-start.5 = ((bf16[32,16,128]{2,1,0:T(8,128)(2,1)}), bf16[32,16,128]{2,1,0:T(8,128)(2,1)S(1)}, u32[]{:S(2)}, u32[]{:S(2)}) async-start(bf16[32,16,128]{2,1,0:T(8,128)(2,1)} %get-tuple-element.35), calls=%async_computation.5 | async-start | bytes 262144 | tf_op jit(solution)/shard_map/all_to_all | solution.py:376
  98.2 3.5 %collective-permute-start.3 = (bf16[16,32,128]{2,1,0:T(8,128)(2,1)S(1)}, bf16[16,32,128]{2,1,0:T(8,128)(2,1)S(1)}, u32[]{:S(2)}, u32[]{:S(2)}) collective-permute-start(bf16[16,32,128]{2,1,0:T(8,128)(2,1)S(1)} %all_to_all.33.refs_2_), channel_id=1, source_target_pairs={{1,2},{2,1},{3,4},{4,3},{5,6},{6,5},{7,8},{8,7},{9,10},{10,9},{11,... | collective-permute-start | bytes 393224 | tf_op jit(solution)/shard_map/ppermute | solution.py:375
  101.7 1.9 %collective-permute-start.2 = (bf16[16,32,128]{2,1,0:T(8,128)(2,1)S(1)}, bf16[16,32,128]{2,1,0:T(8,128)(2,1)S(1)}, u32[]{:S(2)}, u32[]{:S(2)}) collective-permute-start(bf16[16,32,128]{2,1,0:T(8,128)(2,1)S(1)} %all_to_all.33.refs_2_), channel_id=1, source_target_pairs={{0,1},{1,0},{2,3},{3,2},{4,5},{5,4},{6,7},{7,6},{8,9},{9,8},{10,11... | collective-permute-start | bytes 393224 | tf_op jit(solution)/shard_map/ppermute | solution.py:374
  103.7 2.0 %collective-permute-done.3.refs_4_ = bf16[16,32,128]{2,1,0:T(8,128)(2,1)S(1)} collective-permute-done((bf16[16,32,128]{2,1,0:T(8,128)(2,1)S(1)}, bf16[16,32,128]{2,1,0:T(8,128)(2,1)S(1)}, u32[]{:S(2)}, u32[]{:S(2)}) %collective-permute-start.3) | collective-permute-done | bytes 131104 | tf_op jit(solution)/shard_map/ppermute | solution.py:375
  105.7 0.0 collective-permute-done.2.refs_3_
  105.7 2.2 %shard_map.118 = (f32[48,512]{1,0:T(8,128)S(1)}, bf16[4,64,2048]{2,1,0:T(8,128)(2,1)S(1)}) custom-call(s32[1]{0:T(128)} %bitcast.1.refs_0_.refs_1_, f32[6,8,512]{2,1,0:T(8,128)S(1)} %get-tuple-element.30.refs_1_.refs_2_, bf16[16,32,128]{2,1,0:T(8,128)(2,1)S(1)} %all_to_all.33.refs_2_, bf16[16,32,128]{2,1,0:T(8,128)(2,1)S(1)} %collective-permute-done.2.refs_3_, ...), custom_call_target="tpu_custom_call" | custom-call | tf_op jit(solution)/shard_map/pallas_call | solution.py:320
  107.9 0.0 all-to-all-done.5.refs_4_
  107.9 2.8 %shard_map.119 = (f32[6,8,512]{2,1,0:T(8,128)}, f32[2,8,2,64]{3,2,1,0:T(2,128)}) custom-call(s32[1]{0:T(128)} %bitcast.refs_0_, s32[1]{0:T(128)} %bitcast.1.refs_0_.refs_1_, f32[6,8,512]{2,1,0:T(8,128)S(1)} %get-tuple-element.30.refs_1_.refs_2_, f32[48,512]{1,0:T(8,128)S(1)} %get-tuple-element.34.refs_3_, bf16[32,16,128]{2,1,0:T(8,128)(2,1)S(1)} %all-to-all-done.5.refs_4_, ...), custom_call_target="tpu_custom_call" | custom-call | tf_op jit(solution)/shard_map/pallas_call | solution.py:320
Async XLA Ops:
  37.4 16.0 %collective-permute-start.1 = (bf16[16,32,128]{2,1,0:T(8,128)(2,1)S(1)}, bf16[16,32,128]{2,1,0:T(8,128)(2,1)S(1)}, u32[]{:S(2)}, u32[]{:S(2)}) collective-permute-start(bf16[16,32,128]{2,1,0:T(8,128)(2,1)S(1)} %all_to_all.31.refs_2_), channel_id=1, source_target_pairs={{1,2},{2,1},{3,4},{4,3},{5,6},{6,5},{7,8},{8,7},{9,10},{10,9},{11,... | collective-permute-start | bytes 393224 | tf_op jit(solution)/shard_map/ppermute | solution.py:375
  43.3 10.1 %collective-permute-start = (bf16[16,32,128]{2,1,0:T(8,128)(2,1)S(1)}, bf16[16,32,128]{2,1,0:T(8,128)(2,1)S(1)}, u32[]{:S(2)}, u32[]{:S(2)}) collective-permute-start(bf16[16,32,128]{2,1,0:T(8,128)(2,1)S(1)} %all_to_all.31.refs_2_), channel_id=1, source_target_pairs={{0,1},{1,0},{2,3},{3,2},{4,5},{5,4},{6,7},{7,6},{8,9},{9,8},{10,11... | collective-permute-start | bytes 393224 | tf_op jit(solution)/shard_map/ppermute | solution.py:374
  45.2 16.5 %all-to-all-start.2 = ((bf16[32,8,128]{2,1,0:T(8,128)(2,1)}), bf16[32,8,128]{2,1,0:T(8,128)(2,1)S(1)}, u32[]{:S(2)}, u32[]{:S(2)}) async-start(bf16[32,8,128]{2,1,0:T(8,128)(2,1)} %get-tuple-element.28), calls=%async_computation.2 | async-start | bytes 131072 | tf_op jit(solution)/shard_map/all_to_all | solution.py:376
  89.1 18.8 %all-to-all-start.5 = ((bf16[32,16,128]{2,1,0:T(8,128)(2,1)}), bf16[32,16,128]{2,1,0:T(8,128)(2,1)S(1)}, u32[]{:S(2)}, u32[]{:S(2)}) async-start(bf16[32,16,128]{2,1,0:T(8,128)(2,1)} %get-tuple-element.35), calls=%async_computation.5 | async-start | bytes 262144 | tf_op jit(solution)/shard_map/all_to_all | solution.py:376
  98.2 7.5 %collective-permute-start.3 = (bf16[16,32,128]{2,1,0:T(8,128)(2,1)S(1)}, bf16[16,32,128]{2,1,0:T(8,128)(2,1)S(1)}, u32[]{:S(2)}, u32[]{:S(2)}) collective-permute-start(bf16[16,32,128]{2,1,0:T(8,128)(2,1)S(1)} %all_to_all.33.refs_2_), channel_id=1, source_target_pairs={{1,2},{2,1},{3,4},{4,3},{5,6},{6,5},{7,8},{8,7},{9,10},{10,9},{11,... | collective-permute-start | bytes 393224 | tf_op jit(solution)/shard_map/ppermute | solution.py:375
  101.7 3.9 %collective-permute-start.2 = (bf16[16,32,128]{2,1,0:T(8,128)(2,1)S(1)}, bf16[16,32,128]{2,1,0:T(8,128)(2,1)S(1)}, u32[]{:S(2)}, u32[]{:S(2)}) collective-permute-start(bf16[16,32,128]{2,1,0:T(8,128)(2,1)S(1)} %all_to_all.33.refs_2_), channel_id=1, source_target_pairs={{0,1},{1,0},{2,3},{3,2},{4,5},{5,4},{6,7},{7,6},{8,9},{9,8},{10,11... | collective-permute-start | bytes 393224 | tf_op jit(solution)/shard_map/ppermute | solution.py:374

commit v10 on v9

--- a/solution.py
+++ b/solution.py
@@ -192,7 +192,7 @@
 
 def first_operator_kernel(mer_ref, now, emf_ref, pa_ref, pb_ref, conn, stiff, curl, dtn_ref, *refs):
     out_ref, half_ref, near_out, far_out, near_ref, far_ref, tall_ref, work_ref, conn_ref, sems = refs
-    bring = pltpu.make_async_copy(dtn_ref.at[pl.ds(0, 4)], half_ref, sems.at[2])
+    bring = pltpu.make_async_copy(dtn_ref.at[pl.ds(0, 6)], half_ref, sems.at[2])
     bring.start()
     tile = side(mer_ref, pa_ref, pb_ref, 0, 0)
     code = [pltpu.roll(tile(s).astype(F32), 32 + 32 * (s % 2), 1) for s in range(4)]
@@ -221,7 +221,7 @@
 def operator_kernel(mer_ref, now, emf_ref, pa_ref, pb_ref, near_ref, far_ref, dtn_ref, *refs):
     out_ref, half_ref, near_buf, far_buf, sems = refs
     pairs = [(near_ref.at[pl.ds(512 * k, 512)], near_buf.at[pl.ds(512 * k, 512)]) for k in range(3)]
-    pairs += [(far_ref, far_buf), (dtn_ref.at[pl.ds(0, 4)], half_ref)]
+    pairs += [(far_ref, far_buf), (dtn_ref.at[pl.ds(0, 6)], half_ref)]
     copies = [pltpu.make_async_copy(a, b, sems.at[k]) for k, (a, b) in enumerate(pairs)]
     for copy in copies:
         copy.start()
@@ -241,13 +241,13 @@
 
 def finish(mode_ref, mer_ref, now, total_ref, whole_ref, wall, mass, half_ref, dtn):
     whole = all_traces(whole_ref)
-    every = [nt(whole, half_ref[2 * k : 2 * k + 2].reshape(128, 2048)) for k in range(2)]
+    every = [nt(whole, half_ref[2 * k : 2 * k + 2].reshape(128, 2048)) for k in range(3)]
     onehot = wall_onehot(wall(), mer_ref[0])
     field = rows_of(now)
     number = lax.broadcasted_iota(jnp.int32, (48, 512), 0) % 8 + 8 * mode_ref[0]
     coef = (number.astype(F32) / 128.0) ** 2
     weight = 1.0 / mass()[...]
-    every += [nt(whole, dtn(k)[2 * k : 2 * k + 2].reshape(128, 2048)) for k in range(2)]
+    every.append(nt(whole, dtn()[...].reshape(128, 2048)))
     every = jnp.concatenate(every, 1)
     mine = lax.broadcasted_iota(jnp.int32, (16, 512), 0) % 8
     every = jnp.where(mine == lax.broadcasted_iota(jnp.int32, (16, 512), 1) // 64, every, 0.0)
@@ -303,20 +303,16 @@
                 near.append(ref)
                 continue
             buf, copies = bufs.pop(0), []
-            for part in range(2 if k == "d" else 1):
-                src, dst = ref, buf
-                if k == "d":
-                    src, dst = ref.at[pl.ds(4 + 2 * part, 2)], buf.at[pl.ds(2 * part, 2)]
-                copies.append(pltpu.make_async_copy(src, dst, sems.at[used]))
-                copies[-1].start()
-                used += 1
+            src = ref.at[pl.ds(6, 2)] if k == "d" else ref
+            copies.append(pltpu.make_async_copy(src, buf, sems.at[used]))
+            copies[-1].start()
+            used += 1
             near.append(later(copies, buf))
         kernel(*near, *inner[count:])
 
     spaces = {"s": pltpu.SMEM, "v": pltpu.VMEM, "c": pltpu.HBM, "d": pltpu.HBM, "h": pltpu.HBM}
-    waits = sum(2 if k == "d" else 1 for _, k in brought)
-    extra = [pltpu.SemaphoreType.DMA((waits,))] if brought else []
-    extra += [pltpu.VMEM((4,) + a.shape[1:] if k == "d" else a.shape, a.dtype) for a, k in brought]
+    extra = [pltpu.SemaphoreType.DMA((len(brought),))] if brought else []
+    extra += [pltpu.VMEM((2,) + a.shape[1:] if k == "d" else a.shape, a.dtype) for a, k in brought]
     return pl.pallas_call(
         run,
         out_shape=[space(s, d) if space else jax.ShapeDtypeStruct(s, d) for s, d, space in out],
@@ -385,7 +381,7 @@
         pltpu.VMEM((16, 128), F32),
         pltpu.SemaphoreType.DMA((3,)),
     ]
-    some = ((4, 64, 2048), BF, near_space)
+    some = ((6, 64, 2048), BF, near_space)
     total, half, near, far = call(
         first_operator_kernel,
         [rows, some, ((1536, 512), BF, far_space), ((1536, 256), BF, far_space)],

time: 112 us -> 111 us (level)
  no operation moved by 1% of the time
where the time goes in v10:
time: 111 us; the launch traced here: 110 us
  blocking collectives  58.2 us (52%)
  starting transfers between devices  30.5 us (27%)
  Pallas kernels  17.1 us (15%)
  waiting for transfers between devices  3.63 us (3%)
    all_to_all x2, blocking collectives, exchange(): moved = lax.all_to_all(packed, 'mode', 0, 0, tiled=True)  33.8 us
    all_to_all x2, blocking collectives, exchange(): emf = lax.all_to_all(back, 'mode', 0, 0, tiled=True)  24.4 us
    all_to_all x2, starting transfers between devices, exchange(): lax.all_to_all(trace, 'mer', 0, 0, tiled=True)  17.3 us
    pallas_call x7, Pallas kernels, call(): pl.pallas_call(run, out_shape=[space(s, d) if space else jax.ShapeDtypeSt...  17.1 us
    ppermute x2, starting transfers between devices, exchange(): e_other = lax.ppermute(emf, 'mer', others)  9.41 us
    ppermute x2, starting transfers between devices, exchange(): e_twin = lax.ppermute(emf, 'mer', twins)  3.84 us
  transfers between devices with their start and end apart: 6, of which 2 were waited for; matrix products, arithmetic and copies ran while one was open for 0% of the time, Pallas kernels for 8%

profile of v10, /device:TPU:1, one launch (start us, length us, event | category | flops | bytes accessed | tf_op | source)
XLA Modules:
  0.0 110.2 jit_solution(12000249514173538812)
XLA Ops:
  0.6 1.8 %shard_map.113 = (bf16[16,16,128]{2,1,0:T(8,128)(2,1)S(1)}, bf16[32,8,128]{2,1,0:T(8,128)(2,1)}, f32[16,128]{1,0:T(8,128)S(1)}, bf16[256,128]{1,0:T(8,128)(2,1)S...) custom-call(s32[1]{0:T(128)} %bitcast.refs_0_, ...), custom_call_target="tpu_custom_call" | custom-call | tf_op jit(solution)/shard_map/pallas_call | solution.py:316
  2.5 22.2 %all_to_all.30.refs_0_ = bf16[16,16,128]{2,1,0:T(8,128)(2,1)S(1)} all-to-all(bf16[16,16,128]{2,1,0:T(8,128)(2,1)S(1)} %get-tuple-element.21), channel_id=1, replica_groups=mesh['mode'=16,'mer'=32] {'mode'}, dimensions={0} | all-to-all | bytes 131072 | tf_op jit(solution)/shard_map/all_to_all | solution.py:365
  24.7 0.5 shard_map.114
  25.1 12.3 %all_to_all.31.refs_2_ = bf16[16,32,128]{2,1,0:T(8,128)(2,1)S(1)} all-to-all(bf16[16,32,128]{2,1,0:T(8,128)(2,1)S(1)} %shard_map.114), channel_id=1, replica_groups=mesh['mode'=16,'mer'=32] {'mode'}, dimensions={0} | all-to-all | bytes 262144 | tf_op jit(solution)/shard_map/all_to_all | solution.py:369
  37.4 5.9 %collective-permute-start.1 = (bf16[16,32,128]{2,1,0:T(8,128)(2,1)S(1)}, bf16[16,32,128]{2,1,0:T(8,128)(2,1)S(1)}, u32[]{:S(2)}, u32[]{:S(2)}) collective-permute-start(bf16[16,32,128]{2,1,0:T(8,128)(2,1)S(1)} %all_to_all.31.refs_2_), channel_id=1, source_target_pairs={{1,2},{2,1},{3,4},{4,3},{5,6},{6,5},{7,8},{8,7},{9,10},{10,9},{11,... | collective-permute-start | bytes 393224 | tf_op jit(solution)/shard_map/ppermute | solution.py:371
  43.3 1.9 %collective-permute-start = (bf16[16,32,128]{2,1,0:T(8,128)(2,1)S(1)}, bf16[16,32,128]{2,1,0:T(8,128)(2,1)S(1)}, u32[]{:S(2)}, u32[]{:S(2)}) collective-permute-start(bf16[16,32,128]{2,1,0:T(8,128)(2,1)S(1)} %all_to_all.31.refs_2_), channel_id=1, source_target_pairs={{0,1},{1,0},{2,3},{3,2},{4,5},{5,4},{6,7},{7,6},{8,9},{9,8},{10,11... | collective-permute-start | bytes 393224 | tf_op jit(solution)/shard_map/ppermute | solution.py:370
  45.2 8.1 %all-to-all-start.2 = ((bf16[32,8,128]{2,1,0:T(8,128)(2,1)}), bf16[32,8,128]{2,1,0:T(8,128)(2,1)S(1)}, u32[]{:S(2)}, u32[]{:S(2)}) async-start(bf16[32,8,128]{2,1,0:T(8,128)(2,1)} %get-tuple-element.28), calls=%async_computation.2 | async-start | bytes 131072 | tf_op jit(solution)/shard_map/all_to_all | solution.py:372
  53.4 0.0 collective-permute-done.1.refs_4_
  53.4 0.0 collective-permute-done.refs_3_
  53.4 6.7 %shard_map.115 = (f32[48,512]{1,0:T(8,128)S(1)}, bf16[6,64,2048]{2,1,0:T(8,128)(2,1)S(1)}, bf16[1536,512]{1,0:T(8,128)(2,1)}, bf16[1536,256]{1,0:T(8,128)(2,1)}) custom-call(s32[1]{0:T(128)} %bitcast.1.refs_0_.refs_1_, f32[6,8,512]{2,1,0:T(8,128)} %bitcast.8, bf16[16,32,128]{2,1,0:T(8,128)(2,1)S(1)} %all_to_all.31.refs_2_, ...), custom_call_target="tpu_custom_call" | custom-call | tf_op jit(solution)/shard_map/pallas_call | solution.py:316
  60.1 1.6 %all-to-all-done.2.refs_4_ = bf16[32,8,128]{2,1,0:T(8,128)(2,1)S(1)} async-done(((bf16[32,8,128]{2,1,0:T(8,128)(2,1)}), bf16[32,8,128]{2,1,0:T(8,128)(2,1)S(1)}, u32[]{:S(2)}, u32[]{:S(2)}) %all-to-all-start.2) | async-done | bytes 65568 | tf_op jit(solution)/shard_map/all_to_all | solution.py:372
  61.7 2.6 %shard_map.116 = (f32[6,8,512]{2,1,0:T(8,128)S(1)}, bf16[16,16,128]{2,1,0:T(8,128)(2,1)S(1)}, bf16[32,16,128]{2,1,0:T(8,128)(2,1)}, f32[16,128]{1,0:T(8,128)S(1)}) custom-call(s32[1]{0:T(128)} %bitcast.refs_0_, s32[1]{0:T(128)} %bitcast.1.refs_0_.refs_1_, f32[6,8,512]{2,1,0:T(8,128)} %bitcast.9, f32[48,512]{1,0:T(8,128)S(1)} %get-tuple-element.27.refs_3_, ...), custom_call_target="tpu_custom_call" | custom-call | tf_op jit(solution)/shard_map/pallas_call | solution.py:316
  64.3 11.6 %all_to_all.32.refs_0_ = bf16[16,16,128]{2,1,0:T(8,128)(2,1)S(1)} all-to-all(bf16[16,16,128]{2,1,0:T(8,128)(2,1)S(1)} %get-tuple-element.31), channel_id=1, replica_groups=mesh['mode'=16,'mer'=32] {'mode'}, dimensions={0} | all-to-all | bytes 131072 | tf_op jit(solution)/shard_map/all_to_all | solution.py:365
  75.9 0.5 shard_map.117
  76.4 12.1 %all_to_all.33.refs_2_ = bf16[16,32,128]{2,1,0:T(8,128)(2,1)S(1)} all-to-all(bf16[16,32,128]{2,1,0:T(8,128)(2,1)S(1)} %shard_map.117), channel_id=1, replica_groups=mesh['mode'=16,'mer'=32] {'mode'}, dimensions={0} | all-to-all | bytes 262144 | tf_op jit(solution)/shard_map/all_to_all | solution.py:369
  88.5 9.1 %all-to-all-start.5 = ((bf16[32,16,128]{2,1,0:T(8,128)(2,1)}), bf16[32,16,128]{2,1,0:T(8,128)(2,1)S(1)}, u32[]{:S(2)}, u32[]{:S(2)}) async-start(bf16[32,16,128]{2,1,0:T(8,128)(2,1)} %get-tuple-element.35), calls=%async_computation.5 | async-start | bytes 262144 | tf_op jit(solution)/shard_map/all_to_all | solution.py:372
  97.6 3.5 %collective-permute-start.3 = (bf16[16,32,128]{2,1,0:T(8,128)(2,1)S(1)}, bf16[16,32,128]{2,1,0:T(8,128)(2,1)S(1)}, u32[]{:S(2)}, u32[]{:S(2)}) collective-permute-start(bf16[16,32,128]{2,1,0:T(8,128)(2,1)S(1)} %all_to_all.33.refs_2_), channel_id=1, source_target_pairs={{1,2},{2,1},{3,4},{4,3},{5,6},{6,5},{7,8},{8,7},{9,10},{10,9},{11,... | collective-permute-start | bytes 393224 | tf_op jit(solution)/shard_map/ppermute | solution.py:371
  101.1 1.9 %collective-permute-start.2 = (bf16[16,32,128]{2,1,0:T(8,128)(2,1)S(1)}, bf16[16,32,128]{2,1,0:T(8,128)(2,1)S(1)}, u32[]{:S(2)}, u32[]{:S(2)}) collective-permute-start(bf16[16,32,128]{2,1,0:T(8,128)(2,1)S(1)} %all_to_all.33.refs_2_), channel_id=1, source_target_pairs={{0,1},{1,0},{2,3},{3,2},{4,5},{5,4},{6,7},{7,6},{8,9},{9,8},{10,11... | collective-permute-start | bytes 393224 | tf_op jit(solution)/shard_map/ppermute | solution.py:370
  103.1 2.0 %collective-permute-done.3.refs_4_ = bf16[16,32,128]{2,1,0:T(8,128)(2,1)S(1)} collective-permute-done((bf16[16,32,128]{2,1,0:T(8,128)(2,1)S(1)}, bf16[16,32,128]{2,1,0:T(8,128)(2,1)S(1)}, u32[]{:S(2)}, u32[]{:S(2)}) %collective-permute-start.3) | collective-permute-done | bytes 131104 | tf_op jit(solution)/shard_map/ppermute | solution.py:371
  105.1 0.0 collective-permute-done.2.refs_3_
  105.1 2.3 %shard_map.118 = (f32[48,512]{1,0:T(8,128)S(1)}, bf16[6,64,2048]{2,1,0:T(8,128)(2,1)S(1)}) custom-call(s32[1]{0:T(128)} %bitcast.1.refs_0_.refs_1_, f32[6,8,512]{2,1,0:T(8,128)S(1)} %get-tuple-element.30.refs_1_.refs_2_, bf16[16,32,128]{2,1,0:T(8,128)(2,1)S(1)} %all_to_all.33.refs_2_, bf16[16,32,128]{2,1,0:T(8,128)(2,1)S(1)} %collective-permute-done.2.refs_3_, ...), custom_call_target="tpu_custom_call" | custom-call | tf_op jit(solution)/shard_map/pallas_call | solution.py:316
  107.4 0.0 all-to-all-done.5.refs_4_
  107.4 2.8 %shard_map.119 = (f32[6,8,512]{2,1,0:T(8,128)}, f32[2,8,2,64]{3,2,1,0:T(2,128)}) custom-call(s32[1]{0:T(128)} %bitcast.refs_0_, s32[1]{0:T(128)} %bitcast.1.refs_0_.refs_1_, f32[6,8,512]{2,1,0:T(8,128)S(1)} %get-tuple-element.30.refs_1_.refs_2_, f32[48,512]{1,0:T(8,128)S(1)} %get-tuple-element.34.refs_3_, bf16[32,16,128]{2,1,0:T(8,128)(2,1)S(1)} %all-to-all-done.5.refs_4_, ...), custom_call_target="tpu_custom_call" | custom-call | tf_op jit(solution)/shard_map/pallas_call | solution.py:316
Async XLA Ops:
  37.4 16.0 %collective-permute-start.1 = (bf16[16,32,128]{2,1,0:T(8,128)(2,1)S(1)}, bf16[16,32,128]{2,1,0:T(8,128)(2,1)S(1)}, u32[]{:S(2)}, u32[]{:S(2)}) collective-permute-start(bf16[16,32,128]{2,1,0:T(8,128)(2,1)S(1)} %all_to_all.31.refs_2_), channel_id=1, source_target_pairs={{1,2},{2,1},{3,4},{4,3},{5,6},{6,5},{7,8},{8,7},{9,10},{10,9},{11,... | collective-permute-start | bytes 393224 | tf_op jit(solution)/shard_map/ppermute | solution.py:371
  43.3 10.1 %collective-permute-start = (bf16[16,32,128]{2,1,0:T(8,128)(2,1)S(1)}, bf16[16,32,128]{2,1,0:T(8,128)(2,1)S(1)}, u32[]{:S(2)}, u32[]{:S(2)}) collective-permute-start(bf16[16,32,128]{2,1,0:T(8,128)(2,1)S(1)} %all_to_all.31.refs_2_), channel_id=1, source_target_pairs={{0,1},{1,0},{2,3},{3,2},{4,5},{5,4},{6,7},{7,6},{8,9},{9,8},{10,11... | collective-permute-start | bytes 393224 | tf_op jit(solution)/shard_map/ppermute | solution.py:370
  45.2 16.5 %all-to-all-start.2 = ((bf16[32,8,128]{2,1,0:T(8,128)(2,1)}), bf16[32,8,128]{2,1,0:T(8,128)(2,1)S(1)}, u32[]{:S(2)}, u32[]{:S(2)}) async-start(bf16[32,8,128]{2,1,0:T(8,128)(2,1)} %get-tuple-element.28), calls=%async_computation.2 | async-start | bytes 131072 | tf_op jit(solution)/shard_map/all_to_all | solution.py:372
  88.5 18.9 %all-to-all-start.5 = ((bf16[32,16,128]{2,1,0:T(8,128)(2,1)}), bf16[32,16,128]{2,1,0:T(8,128)(2,1)S(1)}, u32[]{:S(2)}, u32[]{:S(2)}) async-start(bf16[32,16,128]{2,1,0:T(8,128)(2,1)} %get-tuple-element.35), calls=%async_computation.5 | async-start | bytes 262144 | tf_op jit(solution)/shard_map/all_to_all | solution.py:372
  97.6 7.5 %collective-permute-start.3 = (bf16[16,32,128]{2,1,0:T(8,128)(2,1)S(1)}, bf16[16,32,128]{2,1,0:T(8,128)(2,1)S(1)}, u32[]{:S(2)}, u32[]{:S(2)}) collective-permute-start(bf16[16,32,128]{2,1,0:T(8,128)(2,1)S(1)} %all_to_all.33.refs_2_), channel_id=1, source_target_pairs={{1,2},{2,1},{3,4},{4,3},{5,6},{6,5},{7,8},{8,7},{9,10},{10,9},{11,... | collective-permute-start | bytes 393224 | tf_op jit(solution)/shard_map/ppermute | solution.py:371
  101.1 3.9 %collective-permute-start.2 = (bf16[16,32,128]{2,1,0:T(8,128)(2,1)S(1)}, bf16[16,32,128]{2,1,0:T(8,128)(2,1)S(1)}, u32[]{:S(2)}, u32[]{:S(2)}) collective-permute-start(bf16[16,32,128]{2,1,0:T(8,128)(2,1)S(1)} %all_to_all.33.refs_2_), channel_id=1, source_target_pairs={{0,1},{1,0},{2,3},{3,2},{4,5},{5,4},{6,7},{7,6},{8,9},{9,8},{10,11... | collective-permute-start | bytes 393224 | tf_op jit(solution)/shard_map/ppermute | solution.py:370

commit v11 on v10

--- a/solution.py
+++ b/solution.py
@@ -97,7 +97,10 @@
     return jnp.concatenate([conn_ref[pl.ds(0, 8, 2), :], conn_ref[pl.ds(1, 8, 2), :]], 1)
 
 
-def open_kernel(mode_ref, field, wall, conn, vel, fwd, inv, pack_ref, out_ref, mark_ref, va_ref, vb_ref, fwd_ref, inv_ref):
+def open_kernel(mode_ref, field, wall, conn, vel, fwd, inv, pack_ref, out_ref, mark_ref, va_ref, vb_ref, fwd_ref, inv_ref, sems):
+    tables = [pltpu.make_async_copy(a, b, sems.at[k]) for k, (a, b) in enumerate(((fwd, fwd_ref), (inv, inv_ref)))]
+    for copy in tables:
+        copy.start()
     onehot = wall_onehot(wall())
     conn = conn()[...]
     field_ref = field()
@@ -117,8 +120,8 @@
     zero = jnp.zeros_like(vel[0])
     va_ref[...] = jnp.concatenate([vel[0], vel[1], vel[2], zero], 0).T.astype(BF)
     vb_ref[...] = jnp.concatenate([vel[1], vel[2], vel[0], zero], 0).T.astype(BF)
-    fwd_ref[...] = fwd()[...]
-    inv_ref[...] = inv()[...]
+    for copy in tables:
+        copy.wait()
 
 
 def element_blocks(ref, sign):
@@ -355,8 +358,9 @@
     packed, trace, *table = call(
         open_kernel,
         [chunk, ((spots, 8, 128), BF, near_space), ((16, 128), F32, near_space), *table],
-        "scccccc",
+        "scccchh",
         (mode, start, wall, connect, jnp.transpose(velocity, (0, 2, 1)), fwd, inv),
+        [pltpu.SemaphoreType.DMA((2,))],
     )
     twins = [(i, i ^ 1) for i in range(spots)]
     others = [(i, ((i + 1) ^ 1) - 1) for i in range(1, spots - 1)]

time: 111 us -> 111 us (level)
  no operation moved by 1% of the time
where the time goes in v11:
time: 111 us; the launch traced here: 110 us
  blocking collectives  58.2 us (52%)
  starting transfers between devices  30.5 us (27%)
  Pallas kernels  17.1 us (15%)
  waiting for transfers between devices  3.63 us (3%)
    all_to_all x2, blocking collectives, exchange(): moved = lax.all_to_all(packed, 'mode', 0, 0, tiled=True)  33.8 us
    all_to_all x2, blocking collectives, exchange(): emf = lax.all_to_all(back, 'mode', 0, 0, tiled=True)  24.4 us
    all_to_all x2, starting transfers between devices, exchange(): lax.all_to_all(trace, 'mer', 0, 0, tiled=True)  17.3 us
    pallas_call x7, Pallas kernels, call(): pl.pallas_call(run, out_shape=[space(s, d) if space else jax.ShapeDtypeSt...  17.1 us
    ppermute x2, starting transfers between devices, exchange(): e_other = lax.ppermute(emf, 'mer', others)  9.41 us
    ppermute x2, starting transfers between devices, exchange(): e_twin = lax.ppermute(emf, 'mer', twins)  3.84 us
  transfers between devices with their start and end apart: 6, of which 2 were waited for; matrix products, arithmetic and copies ran while one was open for 0% of the time, Pallas kernels for 8%

profile of v11, /device:TPU:1, one launch (start us, length us, event | category | flops | bytes accessed | tf_op | source)
XLA Modules:
  0.0 110.2 jit_solution(568049369815412351)
XLA Ops:
  0.6 1.8 %shard_map.113 = (bf16[16,16,128]{2,1,0:T(8,128)(2,1)S(1)}, bf16[32,8,128]{2,1,0:T(8,128)(2,1)}, f32[16,128]{1,0:T(8,128)S(1)}, bf16[256,128]{1,0:T(8,128)(2,1)S...) custom-call(s32[1]{0:T(128)} %bitcast.refs_0_, ...), custom_call_target="tpu_custom_call" | custom-call | tf_op jit(solution)/shard_map/pallas_call | solution.py:319
  2.5 22.2 %all_to_all.30.refs_0_ = bf16[16,16,128]{2,1,0:T(8,128)(2,1)S(1)} all-to-all(bf16[16,16,128]{2,1,0:T(8,128)(2,1)S(1)} %get-tuple-element.21), channel_id=1, replica_groups=mesh['mode'=16,'mer'=32] {'mode'}, dimensions={0} | all-to-all | bytes 131072 | tf_op jit(solution)/shard_map/all_to_all | solution.py:369
  24.7 0.5 shard_map.114
  25.1 12.3 %all_to_all.31.refs_2_ = bf16[16,32,128]{2,1,0:T(8,128)(2,1)S(1)} all-to-all(bf16[16,32,128]{2,1,0:T(8,128)(2,1)S(1)} %shard_map.114), channel_id=1, replica_groups=mesh['mode'=16,'mer'=32] {'mode'}, dimensions={0} | all-to-all | bytes 262144 | tf_op jit(solution)/shard_map/all_to_all | solution.py:373
  37.4 5.9 %collective-permute-start.1 = (bf16[16,32,128]{2,1,0:T(8,128)(2,1)S(1)}, bf16[16,32,128]{2,1,0:T(8,128)(2,1)S(1)}, u32[]{:S(2)}, u32[]{:S(2)}) collective-permute-start(bf16[16,32,128]{2,1,0:T(8,128)(2,1)S(1)} %all_to_all.31.refs_2_), channel_id=1, source_target_pairs={{1,2},{2,1},{3,4},{4,3},{5,6},{6,5},{7,8},{8,7},{9,10},{10,9},{11,... | collective-permute-start | bytes 393224 | tf_op jit(solution)/shard_map/ppermute | solution.py:375
  43.3 1.9 %collective-permute-start = (bf16[16,32,128]{2,1,0:T(8,128)(2,1)S(1)}, bf16[16,32,128]{2,1,0:T(8,128)(2,1)S(1)}, u32[]{:S(2)}, u32[]{:S(2)}) collective-permute-start(bf16[16,32,128]{2,1,0:T(8,128)(2,1)S(1)} %all_to_all.31.refs_2_), channel_id=1, source_target_pairs={{0,1},{1,0},{2,3},{3,2},{4,5},{5,4},{6,7},{7,6},{8,9},{9,8},{10,11... | collective-permute-start | bytes 393224 | tf_op jit(solution)/shard_map/ppermute | solution.py:374
  45.2 8.1 %all-to-all-start.2 = ((bf16[32,8,128]{2,1,0:T(8,128)(2,1)}), bf16[32,8,128]{2,1,0:T(8,128)(2,1)S(1)}, u32[]{:S(2)}, u32[]{:S(2)}) async-start(bf16[32,8,128]{2,1,0:T(8,128)(2,1)} %get-tuple-element.28), calls=%async_computation.2 | async-start | bytes 131072 | tf_op jit(solution)/shard_map/all_to_all | solution.py:376
  53.4 0.0 collective-permute-done.1.refs_4_
  53.4 0.0 collective-permute-done.refs_3_
  53.4 6.7 %shard_map.115 = (f32[48,512]{1,0:T(8,128)S(1)}, bf16[6,64,2048]{2,1,0:T(8,128)(2,1)S(1)}, bf16[1536,512]{1,0:T(8,128)(2,1)}, bf16[1536,256]{1,0:T(8,128)(2,1)}) custom-call(s32[1]{0:T(128)} %bitcast.1.refs_0_.refs_1_, f32[6,8,512]{2,1,0:T(8,128)} %bitcast.8, bf16[16,32,128]{2,1,0:T(8,128)(2,1)S(1)} %all_to_all.31.refs_2_, ...), custom_call_target="tpu_custom_call" | custom-call | tf_op jit(solution)/shard_map/pallas_call | solution.py:319
  60.1 1.6 %all-to-all-done.2.refs_4_ = bf16[32,8,128]{2,1,0:T(8,128)(2,1)S(1)} async-done(((bf16[32,8,128]{2,1,0:T(8,128)(2,1)}), bf16[32,8,128]{2,1,0:T(8,128)(2,1)S(1)}, u32[]{:S(2)}, u32[]{:S(2)}) %all-to-all-start.2) | async-done | bytes 65568 | tf_op jit(solution)/shard_map/all_to_all | solution.py:376
  61.7 2.6 %shard_map.116 = (f32[6,8,512]{2,1,0:T(8,128)S(1)}, bf16[16,16,128]{2,1,0:T(8,128)(2,1)S(1)}, bf16[32,16,128]{2,1,0:T(8,128)(2,1)}, f32[16,128]{1,0:T(8,128)S(1)}) custom-call(s32[1]{0:T(128)} %bitcast.refs_0_, s32[1]{0:T(128)} %bitcast.1.refs_0_.refs_1_, f32[6,8,512]{2,1,0:T(8,128)} %bitcast.9, f32[48,512]{1,0:T(8,128)S(1)} %get-tuple-element.27.refs_3_, ...), custom_call_target="tpu_custom_call" | custom-call | tf_op jit(solution)/shard_map/pallas_call | solution.py:319
  64.3 11.6 %all_to_all.32.refs_0_ = bf16[16,16,128]{2,1,0:T(8,128)(2,1)S(1)} all-to-all(bf16[16,16,128]{2,1,0:T(8,128)(2,1)S(1)} %get-tuple-element.31), channel_id=1, replica_groups=mesh['mode'=16,'mer'=32] {'mode'}, dimensions={0} | all-to-all | bytes 131072 | tf_op jit(solution)/shard_map/all_to_all | solution.py:369
  75.9 0.5 shard_map.117
  76.4 12.1 %all_to_all.33.refs_2_ = bf16[16,32,128]{2,1,0:T(8,128)(2,1)S(1)} all-to-all(bf16[16,32,128]{2,1,0:T(8,128)(2,1)S(1)} %shard_map.117), channel_id=1, replica_groups=mesh['mode'=16,'mer'=32] {'mode'}, dimensions={0} | all-to-all | bytes 262144 | tf_op jit(solution)/shard_map/all_to_all | solution.py:373
  88.5 9.1 %all-to-all-start.5 = ((bf16[32,16,128]{2,1,0:T(8,128)(2,1)}), bf16[32,16,128]{2,1,0:T(8,128)(2,1)S(1)}, u32[]{:S(2)}, u32[]{:S(2)}) async-start(bf16[32,16,128]{2,1,0:T(8,128)(2,1)} %get-tuple-element.35), calls=%async_computation.5 | async-start | bytes 262144 | tf_op jit(solution)/shard_map/all_to_all | solution.py:376
  97.6 3.5 %collective-permute-start.3 = (bf16[16,32,128]{2,1,0:T(8,128)(2,1)S(1)}, bf16[16,32,128]{2,1,0:T(8,128)(2,1)S(1)}, u32[]{:S(2)}, u32[]{:S(2)}) collective-permute-start(bf16[16,32,128]{2,1,0:T(8,128)(2,1)S(1)} %all_to_all.33.refs_2_), channel_id=1, source_target_pairs={{1,2},{2,1},{3,4},{4,3},{5,6},{6,5},{7,8},{8,7},{9,10},{10,9},{11,... | collective-permute-start | bytes 393224 | tf_op jit(solution)/shard_map/ppermute | solution.py:375
  101.1 1.9 %collective-permute-start.2 = (bf16[16,32,128]{2,1,0:T(8,128)(2,1)S(1)}, bf16[16,32,128]{2,1,0:T(8,128)(2,1)S(1)}, u32[]{:S(2)}, u32[]{:S(2)}) collective-permute-start(bf16[16,32,128]{2,1,0:T(8,128)(2,1)S(1)} %all_to_all.33.refs_2_), channel_id=1, source_target_pairs={{0,1},{1,0},{2,3},{3,2},{4,5},{5,4},{6,7},{7,6},{8,9},{9,8},{10,11... | collective-permute-start | bytes 393224 | tf_op jit(solution)/shard_map/ppermute | solution.py:374
  103.1 2.0 %collective-permute-done.3.refs_4_ = bf16[16,32,128]{2,1,0:T(8,128)(2,1)S(1)} collective-permute-done((bf16[16,32,128]{2,1,0:T(8,128)(2,1)S(1)}, bf16[16,32,128]{2,1,0:T(8,128)(2,1)S(1)}, u32[]{:S(2)}, u32[]{:S(2)}) %collective-permute-start.3) | collective-permute-done | bytes 131104 | tf_op jit(solution)/shard_map/ppermute | solution.py:375
  105.0 0.0 collective-permute-done.2.refs_3_
  105.0 2.3 %shard_map.118 = (f32[48,512]{1,0:T(8,128)S(1)}, bf16[6,64,2048]{2,1,0:T(8,128)(2,1)S(1)}) custom-call(s32[1]{0:T(128)} %bitcast.1.refs_0_.refs_1_, f32[6,8,512]{2,1,0:T(8,128)S(1)} %get-tuple-element.30.refs_1_.refs_2_, bf16[16,32,128]{2,1,0:T(8,128)(2,1)S(1)} %all_to_all.33.refs_2_, bf16[16,32,128]{2,1,0:T(8,128)(2,1)S(1)} %collective-permute-done.2.refs_3_, ...), custom_call_target="tpu_custom_call" | custom-call | tf_op jit(solution)/shard_map/pallas_call | solution.py:319
  107.4 0.0 all-to-all-done.5.refs_4_
  107.4 2.8 %shard_map.119 = (f32[6,8,512]{2,1,0:T(8,128)}, f32[2,8,2,64]{3,2,1,0:T(2,128)}) custom-call(s32[1]{0:T(128)} %bitcast.refs_0_, s32[1]{0:T(128)} %bitcast.1.refs_0_.refs_1_, f32[6,8,512]{2,1,0:T(8,128)S(1)} %get-tuple-element.30.refs_1_.refs_2_, f32[48,512]{1,0:T(8,128)S(1)} %get-tuple-element.34.refs_3_, bf16[32,16,128]{2,1,0:T(8,128)(2,1)S(1)} %all-to-all-done.5.refs_4_, ...), custom_call_target="tpu_custom_call" | custom-call | tf_op jit(solution)/shard_map/pallas_call | solution.py:319
Async XLA Ops:
  37.4 16.0 %collective-permute-start.1 = (bf16[16,32,128]{2,1,0:T(8,128)(2,1)S(1)}, bf16[16,32,128]{2,1,0:T(8,128)(2,1)S(1)}, u32[]{:S(2)}, u32[]{:S(2)}) collective-permute-start(bf16[16,32,128]{2,1,0:T(8,128)(2,1)S(1)} %all_to_all.31.refs_2_), channel_id=1, source_target_pairs={{1,2},{2,1},{3,4},{4,3},{5,6},{6,5},{7,8},{8,7},{9,10},{10,9},{11,... | collective-permute-start | bytes 393224 | tf_op jit(solution)/shard_map/ppermute | solution.py:375
  43.3 10.1 %collective-permute-start = (bf16[16,32,128]{2,1,0:T(8,128)(2,1)S(1)}, bf16[16,32,128]{2,1,0:T(8,128)(2,1)S(1)}, u32[]{:S(2)}, u32[]{:S(2)}) collective-permute-start(bf16[16,32,128]{2,1,0:T(8,128)(2,1)S(1)} %all_to_all.31.refs_2_), channel_id=1, source_target_pairs={{0,1},{1,0},{2,3},{3,2},{4,5},{5,4},{6,7},{7,6},{8,9},{9,8},{10,11... | collective-permute-start | bytes 393224 | tf_op jit(solution)/shard_map/ppermute | solution.py:374
  45.2 16.5 %all-to-all-start.2 = ((bf16[32,8,128]{2,1,0:T(8,128)(2,1)}), bf16[32,8,128]{2,1,0:T(8,128)(2,1)S(1)}, u32[]{:S(2)}, u32[]{:S(2)}) async-start(bf16[32,8,128]{2,1,0:T(8,128)(2,1)} %get-tuple-element.28), calls=%async_computation.2 | async-start | bytes 131072 | tf_op jit(solution)/shard_map/all_to_all | solution.py:376
  88.5 18.9 %all-to-all-start.5 = ((bf16[32,16,128]{2,1,0:T(8,128)(2,1)}), bf16[32,16,128]{2,1,0:T(8,128)(2,1)S(1)}, u32[]{:S(2)}, u32[]{:S(2)}) async-start(bf16[32,16,128]{2,1,0:T(8,128)(2,1)} %get-tuple-element.35), calls=%async_computation.5 | async-start | bytes 262144 | tf_op jit(solution)/shard_map/all_to_all | solution.py:376
  97.6 7.5 %collective-permute-start.3 = (bf16[16,32,128]{2,1,0:T(8,128)(2,1)S(1)}, bf16[16,32,128]{2,1,0:T(8,128)(2,1)S(1)}, u32[]{:S(2)}, u32[]{:S(2)}) collective-permute-start(bf16[16,32,128]{2,1,0:T(8,128)(2,1)S(1)} %all_to_all.33.refs_2_), channel_id=1, source_target_pairs={{1,2},{2,1},{3,4},{4,3},{5,6},{6,5},{7,8},{8,7},{9,10},{10,9},{11,... | collective-permute-start | bytes 393224 | tf_op jit(solution)/shard_map/ppermute | solution.py:375
  101.1 3.9 %collective-permute-start.2 = (bf16[16,32,128]{2,1,0:T(8,128)(2,1)S(1)}, bf16[16,32,128]{2,1,0:T(8,128)(2,1)S(1)}, u32[]{:S(2)}, u32[]{:S(2)}) collective-permute-start(bf16[16,32,128]{2,1,0:T(8,128)(2,1)S(1)} %all_to_all.33.refs_2_), channel_id=1, source_target_pairs={{0,1},{1,0},{2,3},{3,2},{4,5},{5,4},{6,7},{7,6},{8,9},{9,8},{10,11... | collective-permute-start | bytes 393224 | tf_op jit(solution)/shard_map/ppermute | solution.py:374
